TPU v7x, 32 devices: a whole 2x2x4 slice. The times are simulated.
32 devices in a mesh: seq: 8 (over y, x, core), fsdp: 4 (over z).
Axes of the slice: x: 2, y: 2, z: 4, core: 2. Of those that a mesh axis runs over, the one named last changes fastest.
Arguments:
- tokens: bfloat16 [4, 2048, 1536], P('fsdp', 'seq'), may hold values from -6 to 6
- segment_ids: int32 [4, 2048], P('fsdp'), may hold values from 0 to 7, never falling along the last dimension, each value on 1 to 512 neighbouring positions
- cotangent: bfloat16 [4, 2048, 1536], P('fsdp', 'seq'), may hold values from -6 to 6
- w_in: bfloat16 [1536, 6448], P('fsdp'), may hold values from -0.15625 to 0.15625
- w_out: bfloat16 [3072, 1536], P('fsdp'), may hold values from -0.109375 to 0.109375
- conv_w: bfloat16 [4, 3328], P(None, 'fsdp'), may hold values from -3 to 3
- conv_b: bfloat16 [3328], P('fsdp'), may hold values from -1.5 to 1.5
- a_log: bfloat16 [48], P('fsdp'), may hold values from -3 to 1.5
- dt_bias: bfloat16 [48], P('fsdp'), may hold values from -5.5 to -3
- d_skip: bfloat16 [48], P('fsdp'), may hold values from 0.5 to 1.5
- norm_w: bfloat16 [1536], P('fsdp'), may hold values from 0.5 to 1.5
- gate_w: bfloat16 [3072], P('fsdp'), may hold values from 0.5 to 1.5
Outputs:
- layer_out: bfloat16 [4, 2048, 1536], P('fsdp', 'seq')
- token_grad: float32 [4, 2048, 1536], P('fsdp', 'seq')
- w_in_grad: float32 [1536, 6448], P('fsdp')
- w_out_grad: float32 [3072, 1536], P('fsdp')
- conv_w_grad: float32 [4, 3328], P(None, 'fsdp')
- conv_b_grad: float32 [3328], P('fsdp')
- a_log_grad: float32 [48], P('fsdp')
- dt_bias_grad: float32 [48], P('fsdp')
- d_skip_grad: float32 [48], P('fsdp')
- norm_w_grad: float32 [1536], P('fsdp')
- gate_w_grad: float32 [3072], P('fsdp')
Inputs may be any that keep to these rules, and one draw needn't show every extreme that they name: `segment_ids`: in each sequence the ids never fall from one token to the next, start at 0 and take every value; each document has 1 to 512 tokens and one has exactly 512.
All inputs are finite; a program needn't handle non-finite values.
Results may differ from a plain program's by a relative error of at most 0.011.
Values may be sent and summed in bfloat16 or wider, within the bound.
A program may use at most 320 MiB of HBM per device.

v0:
```python
import jax
import jax.numpy as jnp
from jax import lax
from jax.sharding import PartitionSpec as P

DI = 3072
HEADDIM = 64
STATE = 128
CONV = 4
SPAN = 256
HEADS = 48
CHAN = 3328


EPSILON = 1e-05
HIGHEST = lax.Precision.HIGHEST


def passed_along(value, axis, steps):
    count = lax.axis_size(axis)
    first, last = (max(0, -steps), min(count, count - steps))
    return lax.ppermute(value, axis, [(source, source + steps) for source in range(first, last)])


def shortened(array):

    def short(part):
        return part.astype(jnp.bfloat16) if part.dtype == jnp.float32 else part

    return jax.tree.map(short, array)


def block_masks(ids_blocks, before_ids):
    block_len = ids_blocks.shape[1]
    places = jnp.arange(block_len)
    causal_mask = (places[:, None] >= places[None, :])[None] & (
        ids_blocks[:, :, None] == ids_blocks[:, None, :]
    )
    keep_flag = (ids_blocks == before_ids[:, None]).astype(jnp.float32)
    same_last = (ids_blocks == ids_blocks[:, -1:]).astype(jnp.float32)
    return (causal_mask, keep_flag, same_last)


def local_states(x_heads, b_rows, step_size, log_decay, same_last, keep_flag):
    cum_decay = jnp.cumsum(log_decay, axis=1)
    last_cum = cum_decay[:, -1]
    weights = jnp.exp(last_cum[:, None, :] - cum_decay) * step_size * same_last[:, :, None]
    fresh_state = jnp.einsum("csh,cshp,csn->chpn", weights, x_heads, b_rows, precision=HIGHEST)
    passing = keep_flag[:, -1:] * jnp.exp(last_cum)
    total_state = jnp.zeros_like(fresh_state[0])
    total_decay = jnp.ones_like(passing[0])
    total_state = fresh_state[0] + passing[0][:, None, None] * total_state
    total_decay = total_decay * passing[0]
    return (fresh_state, passing, total_state, total_decay)


def local_output(x_heads, b_rows, c_rows, step_size, log_decay, incoming, causal_mask, keep_flag):
    cum_decay = jnp.cumsum(log_decay, axis=1)
    cum_heads = jnp.swapaxes(cum_decay, 1, 2)
    gap_decay = cum_heads[:, :, :, None] - cum_heads[:, :, None, :]
    head_mask = causal_mask[:, None]
    decay_map = jnp.exp(jnp.where(head_mask, gap_decay, 0.0)) * head_mask.astype(jnp.float32)
    scores = jnp.einsum("ctn,csn->cts", c_rows, b_rows, precision=HIGHEST)
    mixing = scores[:, None] * decay_map * jnp.swapaxes(step_size, 1, 2)[:, :, None, :]
    inner_out = jnp.einsum("chts,cshp->cthp", mixing, x_heads, precision=HIGHEST)
    starts = [incoming]
    start_states = jnp.stack(starts)
    carried = jnp.einsum("ctn,chpn->cthp", c_rows, start_states, precision=HIGHEST)
    carried = carried * (keep_flag[:, :, None] * jnp.exp(cum_decay))[..., None]
    return inner_out + carried


def on_device(
    tokens,
    segment_ids,
    cotangent,
    w_in,
    w_out,
    conv_w,
    conv_b,
    a_log,
    dt_bias,
    d_skip,
    norm_w,
    gate_w,
):
    gathered = (
        lax.all_gather(w_in, "fsdp", axis=0, tiled=True),
        lax.all_gather(w_out, "fsdp", axis=0, tiled=True),
        lax.all_gather(conv_w, "fsdp", axis=1, tiled=True),
        lax.all_gather(conv_b, "fsdp", axis=0, tiled=True),
        lax.all_gather(a_log, "fsdp", axis=0, tiled=True),
        lax.all_gather(dt_bias, "fsdp", axis=0, tiled=True),
        lax.all_gather(d_skip, "fsdp", axis=0, tiled=True),
        lax.all_gather(norm_w, "fsdp", axis=0, tiled=True),
        lax.all_gather(gate_w, "fsdp", axis=0, tiled=True),
    )
    (
        w_in_full,
        w_out_full,
        conv_full,
        bias_full,
        a_log_full,
        dt_bias_full,
        skip_full,
        norm_full,
        gate_full,
    ) = gathered
    inputs = tokens[0].astype(jnp.float32)
    length = inputs.shape[0]
    norm_gain = norm_full.astype(jnp.float32)
    scale_in = lax.rsqrt(jnp.mean(inputs * inputs, axis=-1, keepdims=True) + EPSILON)
    normed = (inputs * scale_in * norm_gain).astype(jnp.bfloat16)
    projected = jnp.dot(normed, w_in_full, preferred_element_type=jnp.float32).astype(jnp.bfloat16)
    gate_z = projected[:, :DI].astype(jnp.float32)
    conv_in = projected[:, DI : DI + CHAN]
    dt_raw = projected[:, DI + CHAN :].astype(jnp.float32)
    first_row = lax.axis_index("seq") * length
    id_row = jnp.concatenate([jnp.full((CONV - 1,), -1, jnp.int32), segment_ids[0]], axis=0)
    ids_pad = lax.dynamic_slice_in_dim(id_row, first_row, length + CONV - 1)
    ids_own = ids_pad[CONV - 1 :]
    left_edge = passed_along(conv_in[length - (CONV - 1) :], "seq", 1)
    padded = jnp.concatenate([left_edge, conv_in], axis=0).astype(jnp.float32)
    kernel = conv_full.astype(jnp.float32)
    conv_out = jnp.zeros((length, CHAN), jnp.float32) + bias_full.astype(jnp.float32)
    same_docs = []
    for offset in range(CONV):
        same_doc = (ids_pad[offset : offset + length] == ids_own).astype(jnp.float32)
        same_docs.append(same_doc)
        conv_out = conv_out + kernel[offset] * padded[offset : offset + length] * same_doc[:, None]
    activated = jax.nn.silu(conv_out)
    blocks = length // SPAN
    x_heads = activated[:, :DI].reshape(blocks, SPAN, HEADS, HEADDIM)
    b_rows = activated[:, DI : DI + STATE].reshape(blocks, SPAN, STATE)
    c_rows = activated[:, DI + STATE :].reshape(blocks, SPAN, STATE)
    dt_bias_f = dt_bias_full.astype(jnp.float32)
    decay_rate = jnp.exp(a_log_full.astype(jnp.float32))
    step_flat = jax.nn.softplus(dt_raw + dt_bias_f)
    step_size = step_flat.reshape(blocks, SPAN, HEADS)
    log_decay = (-step_flat * decay_rate).reshape(blocks, SPAN, HEADS)
    ids_blocks = ids_own.reshape(blocks, SPAN)
    before_ids = ids_pad[CONV - 2 : CONV - 2 + length : SPAN]
    causal_mask, keep_flag, same_last = block_masks(ids_blocks, before_ids)

    def state_part(heads_in, rows_b, steps_in, decay_in):
        return local_states(heads_in, rows_b, steps_in, decay_in, same_last, keep_flag)

    (fresh_state, passing, total_state, total_decay), state_pull = jax.vjp(
        state_part, x_heads, b_rows, step_size, log_decay
    )

    def pass_forward(turn_index, received):
        return passed_along(
            (total_state + total_decay[:, None, None] * received).astype(jnp.bfloat16), "seq", 1
        ).astype(jnp.float32)

    incoming = lax.fori_loop(0, lax.axis_size("seq") - 1, pass_forward, jnp.zeros_like(total_state))

    def output_part(
        heads_in, rows_b, rows_c, steps_in, decay_in, fresh_in, passing_in, incoming_in
    ):
        return local_output(
            heads_in, rows_b, rows_c, steps_in, decay_in, incoming_in, causal_mask, keep_flag
        )

    ssd_out, output_pull = jax.vjp(
        output_part, x_heads, b_rows, c_rows, step_size, log_decay, fresh_state, passing, incoming
    )
    skip_heads = skip_full.astype(jnp.float32)
    y_full = (ssd_out + skip_heads[:, None] * x_heads).reshape(length, DI)
    silu_z = jax.nn.silu(gate_z)
    gated = y_full * silu_z
    scale_out = lax.rsqrt(jnp.mean(gated * gated, axis=-1, keepdims=True) + EPSILON)
    gate_gain = gate_full.astype(jnp.float32)
    normed_out = (gated * scale_out * gate_gain).astype(jnp.bfloat16)
    branch = jnp.dot(normed_out, w_out_full, preferred_element_type=jnp.float32)
    layer_out = (inputs + branch).astype(jnp.bfloat16)[None]
    grad_out = cotangent[0]
    d_w_out = lax.dot_general(
        normed_out, grad_out, (((0,), (0,)), ((), ())), preferred_element_type=jnp.float32
    )
    d_normed_out = lax.dot_general(
        grad_out, w_out_full, (((1,), (1,)), ((), ())), preferred_element_type=jnp.float32
    )
    d_gate_w = jnp.sum(d_normed_out * gated * scale_out, axis=0)
    along_out = d_normed_out * gate_gain
    cube_out = scale_out * scale_out * scale_out
    d_gated = scale_out * along_out - gated * cube_out * jnp.mean(
        along_out * gated, axis=-1, keepdims=True
    )
    d_y = d_gated * silu_z
    sig_z = jax.nn.sigmoid(gate_z)
    d_gate_z = d_gated * y_full * sig_z * (1.0 + gate_z * (1.0 - sig_z))
    d_ssd = d_y.reshape(blocks, SPAN, HEADS, HEADDIM)
    d_skip_grad = jnp.sum(d_ssd * x_heads, axis=(0, 1, 3))
    dx_out, db_out, dc_out, dstep_out, ddecay_out, d_fresh, d_passing, d_incoming = output_pull(
        d_ssd
    )

    def pass_backward(turn_index, received):
        return passed_along(d_incoming + total_decay[:, None, None] * received, "seq", -1)

    d_total = lax.fori_loop(0, lax.axis_size("seq") - 1, pass_backward, jnp.zeros_like(d_incoming))
    d_total_decay = jnp.sum(d_total * incoming, axis=(1, 2))
    dx_state, db_state, dstep_state, ddecay_state = state_pull(
        (d_fresh, d_passing, d_total, d_total_decay)
    )
    d_x = dx_out + dx_state + skip_heads[:, None] * d_ssd
    d_b = db_out + db_state
    d_log = (ddecay_out + ddecay_state).reshape(length, HEADS)
    d_step = (dstep_out + dstep_state).reshape(length, HEADS) - d_log * decay_rate
    d_a_log = -jnp.sum(d_log * step_flat, axis=0) * decay_rate
    d_dt_raw = d_step * jax.nn.sigmoid(dt_raw + dt_bias_f)
    d_dt_bias = jnp.sum(d_dt_raw, axis=0)
    d_act = jnp.concatenate(
        [d_x.reshape(length, DI), d_b.reshape(length, STATE), dc_out.reshape(length, STATE)], axis=1
    )
    sig_conv = jax.nn.sigmoid(conv_out)
    d_conv = d_act * sig_conv * (1.0 + conv_out * (1.0 - sig_conv))
    d_conv_b = jnp.sum(d_conv, axis=0)
    kernel_rows = []
    d_padded = jnp.zeros((length + CONV - 1, CHAN), jnp.float32)
    for offset in range(CONV):
        masked = d_conv * same_docs[offset][:, None]
        kernel_rows.append(jnp.sum(masked * padded[offset : offset + length], axis=0))
        d_padded = d_padded + jnp.pad(
            kernel[offset] * masked, ((offset, CONV - 1 - offset), (0, 0))
        )
    d_kernel = jnp.stack(kernel_rows)
    d_edge = passed_along(shortened(d_padded[: CONV - 1]), "seq", -1)
    d_conv_in = d_padded[CONV - 1 :] + jnp.pad(d_edge, ((length - (CONV - 1), 0), (0, 0)))
    d_projected = jnp.concatenate([d_gate_z, d_conv_in, d_dt_raw], axis=1).astype(jnp.bfloat16)
    d_normed = lax.dot_general(
        d_projected, w_in_full, (((1,), (1,)), ((), ())), preferred_element_type=jnp.float32
    )
    d_norm_w = jnp.sum(d_normed * inputs * scale_in, axis=0)
    along_in = d_normed * norm_gain
    cube_in = scale_in * scale_in * scale_in
    d_inputs = (
        scale_in * along_in
        - inputs * cube_in * jnp.mean(along_in * inputs, axis=-1, keepdims=True)
        + grad_out.astype(jnp.float32)
    )
    d_w_in = lax.dot_general(
        normed, d_projected, (((0,), (0,)), ((), ())), preferred_element_type=jnp.float32
    )
    weight_grads = (
        d_w_in,
        d_w_out,
        d_kernel,
        d_conv_b,
        d_a_log,
        d_dt_bias,
        d_skip_grad,
        d_norm_w,
        d_gate_w,
    )
    shares = tuple(
        (
            lax.psum_scatter(weight_grads[0], "fsdp", scatter_dimension=0, tiled=True),
            lax.psum_scatter(weight_grads[1], "fsdp", scatter_dimension=0, tiled=True),
            lax.psum_scatter(weight_grads[2], "fsdp", scatter_dimension=1, tiled=True),
            lax.psum_scatter(weight_grads[3], "fsdp", scatter_dimension=0, tiled=True),
            lax.psum_scatter(weight_grads[4], "fsdp", scatter_dimension=0, tiled=True),
            lax.psum_scatter(weight_grads[5], "fsdp", scatter_dimension=0, tiled=True),
            lax.psum_scatter(weight_grads[6], "fsdp", scatter_dimension=0, tiled=True),
            lax.psum_scatter(weight_grads[7], "fsdp", scatter_dimension=0, tiled=True),
            lax.psum_scatter(weight_grads[8], "fsdp", scatter_dimension=0, tiled=True),
        )
    )
    totals = lax.psum(shares, "seq")
    return (layer_out, d_inputs[None]) + tuple(totals)


def solution(mesh):
    return jax.shard_map(
        on_device,
        mesh=mesh,
        in_specs=(
            P("fsdp", "seq", None),
            P("fsdp", None),
            P("fsdp", "seq", None),
            P("fsdp", None),
            P("fsdp", None),
            P(None, "fsdp"),
            P("fsdp"),
            P("fsdp"),
            P("fsdp"),
            P("fsdp"),
            P("fsdp"),
            P("fsdp"),
        ),
        out_specs=(
            P("fsdp", "seq", None),
            P("fsdp", "seq", None),
            P("fsdp", None),
            P("fsdp", None),
            P(None, "fsdp"),
            P("fsdp"),
            P("fsdp"),
            P("fsdp"),
            P("fsdp"),
            P("fsdp"),
            P("fsdp"),
        ),
        check_vma=False,
    )
```

profile of v0, /device:TPU:0, one launch (start us, length us, event | category | flops | bytes accessed | tf_op | source)
XLA Modules:
  0.0 1850.9 jit_solution(16285410717219535761)
XLA Ops:
  9.6 13.5 all-gather.1
  23.2 13.2 all-gather
  40.1 30.4 %all-reduce.20 = (bf16[3328]{0:T(1024)(128)(2,1)S(1)}, bf16[48]{0:T(256)(128)(2,1)S(1)}, bf16[48]{0:T(256)(128)(2,1)S(1)}, bf16[48]{0:T(256)(128)(2,1)S(1)}) all-reduce(bf16[3328]{0:T(1024)(128)(2,1)S(1)} %dynamic-update-slice, bf16[48]{0:T(256)(128)(2,1)S(1)} %dynamic-update-slice.2, ...), channel_id=1, replica_groups=mesh['seq'=8,'fsdp'=4] {'fsdp'}, use_global_device_ids=true, to_apply=%add.7 | all-reduce | flops 3472 | bytes 13888
  74.6 30.3 %all-gather.2 = bf16[4,1,768]{2,1,0:T(2,128)(2,1)S(1)} all-gather(bf16[1,1,768]{2,1,0:T(2,128)(2,1)S(1)} %reshape.689), channel_id=1, replica_groups=mesh['seq'=8,'fsdp'=4] {'fsdp'}, dimensions={0}, use_global_device_ids=true | all-gather | bytes 7680 | tf_op jit(solution)/shard_map/all_gather | solution.py:96
  107.8 243.6 %all-gather.6.cloned.1.call-done = bf16[1536,6448]{0,1:T(8,128)(2,1)} async-done(((bf16[384,6448]{0,1:T(8,128)(2,1)}), bf16[1536,6448]{0,1:T(8,128)(2,1)}) %all-gather.6.cloned.1.call-update) | async-done | bytes 19808272 | tf_op jit(solution)/shard_map/all_gather | solution.py:88
  351.4 9.9 convolution_convert_fusion
  385.6 4.7 fusion.27
  394.1 3.6 copy.162
  399.7 5.7 fusion.61
  405.4 122.5 %while.22 = (s32[]{:T(128)}, f32[48,64,128]{2,1,0:T(8,128)}, f32[1,48]{1,0:T(1,128)}, f32[48,64,128]{2,1,0:T(8,128)}, s32[]{:T(128)}, /*index=5*/s32[]{:T(128)}) while((s32[]{:T(128)}, f32[48,64,128]{2,1,0:T(8,128)}, f32[1,48]{1,0:T(1,128)}, f32[48,64,128]{2,1,0:T(8,128)}, s32[]{:T(128)}, /*index=5*/s32[]{:T(128)}) %tuple.82), condition=%wide.region_4.5_spmd.clone, body=%wide.region_3.4_spmd.clone.sunk | while | flops 1966083 | bytes 9437495 | solution.py:157
  408.0 3.9 collective-permute-start.1
  418.7 9.9 collective-permute-start.1
  432.4 3.0 fusion.137
  435.4 12.2 collective-permute-start.1
  454.5 12.3 collective-permute-start.1
  473.7 12.3 collective-permute-start.1
  492.7 12.3 collective-permute-start.1
  511.8 12.3 collective-permute-start.1
  527.9 4.2 fusion.94
  532.3 16.0 fusion.35
  548.2 3.5 copy.171
  551.8 3.6 multiply_reduce_fusion.10
  557.0 8.0 fusion.76
  567.8 4.0 copy.174
  571.8 8.4 multiply_reduce_fusion.6
  580.2 5.7 multiply_reduce_fusion.7
  585.9 3.8 copy.173
  589.7 5.0 mul.702
  594.7 3.6 copy.175
  598.3 5.6 fusion.92
  605.3 173.5 %while.21 = (s32[]{:T(128)}, f32[48,64,128]{2,1,0:T(8,128)}, f32[1,48]{1,0:T(1,128)}, f32[48,64,128]{2,1,0:T(8,128)}, s32[]{:T(128)}) while((s32[]{:T(128)}, f32[48,64,128]{2,1,0:T(8,128)}, f32[1,48]{1,0:T(1,128)}, f32[48,64,128]{2,1,0:T(8,128)}, s32[]{:T(128)}) %tuple.102), condition=%wide.region_8.9_spmd, body=%wide.region_7.8_spmd.sunk | while | flops 786434 | bytes 11010341 | solution.py:203
  605.4 3.3 multiply_add_fusion.4
  610.0 13.3 collective-permute-done
  623.3 3.4 multiply_add_fusion.4
  627.9 22.5 %collective-permute-done = f32[48,64,128]{2,1,0:T(8,128)} collective-permute-done((f32[48,64,128]{2,1,0:T(8,128)}, f32[48,64,128]{2,1,0:T(8,128)}, u32[]{:S(2)}, u32[]{:S(2)}) %collective-permute-start) | collective-permute-done | bytes 1572896 | tf_op jit(solution)/shard_map/while/body/eval_jaxpr/ppermute | solution.py:22
  650.4 3.3 multiply_add_fusion.4
  655.0 21.0 %collective-permute-done = f32[48,64,128]{2,1,0:T(8,128)} collective-permute-done((f32[48,64,128]{2,1,0:T(8,128)}, f32[48,64,128]{2,1,0:T(8,128)}, u32[]{:S(2)}, u32[]{:S(2)}) %collective-permute-start) | collective-permute-done | bytes 1572896 | tf_op jit(solution)/shard_map/while/body/eval_jaxpr/ppermute | solution.py:22
  676.0 3.3 multiply_add_fusion.4
  680.7 21.1 %collective-permute-done = f32[48,64,128]{2,1,0:T(8,128)} collective-permute-done((f32[48,64,128]{2,1,0:T(8,128)}, f32[48,64,128]{2,1,0:T(8,128)}, u32[]{:S(2)}, u32[]{:S(2)}) %collective-permute-start) | collective-permute-done | bytes 1572896 | tf_op jit(solution)/shard_map/while/body/eval_jaxpr/ppermute | solution.py:22
  701.8 3.3 multiply_add_fusion.4
  706.4 21.0 %collective-permute-done = f32[48,64,128]{2,1,0:T(8,128)} collective-permute-done((f32[48,64,128]{2,1,0:T(8,128)}, f32[48,64,128]{2,1,0:T(8,128)}, u32[]{:S(2)}, u32[]{:S(2)}) %collective-permute-start) | collective-permute-done | bytes 1572896 | tf_op jit(solution)/shard_map/while/body/eval_jaxpr/ppermute | solution.py:22
  727.4 3.6 multiply_add_fusion.4
  732.3 20.8 %collective-permute-done = f32[48,64,128]{2,1,0:T(8,128)} collective-permute-done((f32[48,64,128]{2,1,0:T(8,128)}, f32[48,64,128]{2,1,0:T(8,128)}, u32[]{:S(2)}, u32[]{:S(2)}) %collective-permute-start) | collective-permute-done | bytes 1572896 | tf_op jit(solution)/shard_map/while/body/eval_jaxpr/ppermute | solution.py:22
  753.1 3.4 multiply_add_fusion.4
  757.8 21.0 %collective-permute-done = f32[48,64,128]{2,1,0:T(8,128)} collective-permute-done((f32[48,64,128]{2,1,0:T(8,128)}, f32[48,64,128]{2,1,0:T(8,128)}, u32[]{:S(2)}, u32[]{:S(2)}) %collective-permute-start) | collective-permute-done | bytes 1572896 | tf_op jit(solution)/shard_map/while/body/eval_jaxpr/ppermute | solution.py:22
  778.8 7.4 fusion.37
  787.8 23.1 %fusion.10 = (f32[48,256]{1,0:T(8,128)}, f32[48,256]{1,0:T(8,128)}, f32[48,256]{1,0:T(8,128)}, f32[256,256]{1,0:T(8,128)}) fusion(f32[48,256]{1,0:T(8,128)} %copy.166, f32[256,256]{1,0:T(8,128)} %get-tuple-element.160, f32[48,256]{1,0:T(8,128)} %bitcast_add_fusion.7, f32[256,256]{1,0:T(8,128)} %fusion.101, pred[256,256]{1,0:T(8,128)(4,1)} %get-tuple-element.159, ...), kind=kOutput, calls=%fused_computation.15 | convolution fusion | flops 2463002624 | bytes 7389184 | tf_op jit(solution)/shard_map/transpose(jvp(chts,cshp->cthp))/dot_general | solution.py:65
  813.9 4.2 multiply_reduce_fusion.8
  826.8 3.8 reduce-window.26
  835.0 3.8 reduce-window.24
  841.4 15.3 fusion.34
  856.8 3.9 copy.180
  862.5 7.5 convolution_bitcast_fusion
  871.5 6.5 fusion.72
  878.1 4.7 multiply_reduce_fusion.5
  894.9 11.3 collective-permute-done.3
  908.4 17.6 fusion.64
  928.7 661.8 %reduce-scatter.6.cloned.1.call-done = f32[384,6448]{0,1:T(8,128)} async-done(((f32[1536,6448]{0,1:T(8,128)}), f32[384,6448]{0,1:T(8,128)}) %reduce-scatter.6.cloned.1.call-update) | async-done | bytes 9904144 | tf_op jit(solution)/shard_map/reduce_scatter | solution.py:260
  1593.8 7.5 fusion.43
  1601.4 9.9 fusion.57
  1611.3 22.4 %all-reduce.19 = (f32[3328]{0:T(1024)S(1)}, f32[48]{0:T(128)S(1)}, f32[48]{0:T(128)S(1)}, f32[48]{0:T(128)S(1)}, f32[1536]{0:T(1024)S(1)}, /*index=5*/f32[3072]{0:T(1024)S(1)}) all-reduce(f32[3328]{0:T(1024)S(1)} %copy-done.36, f32[48]{0:T(128)S(1)} %negate_multiply_fusion.1, ...), channel_id=5, replica_groups=mesh['seq'=8,'fsdp'=4] {'fsdp'}, use_global_device_ids=true, to_apply=%region_33.34.clone | all-reduce | flops 8080 | bytes 64640
  1637.0 23.9 %all-reduce.17 = (f32[4,832]{1,0:T(4,128)}, f32[832]{0:T(1024)}, f32[12]{0:T(128)}, f32[12]{0:T(128)}, f32[12]{0:T(128)}, /*index=5*/f32[384]{0:T(512)}, f32[768]{0:T(1024)}) all-reduce(f32[4,832]{1,0:T(4,128)S(1)} %copy.204, f32[832]{0:T(1024)S(1)} %dynamic-slice.5, ...), channel_id=1, replica_groups=mesh['seq'=8,'fsdp'=4] {'seq'}, use_global_device_ids=true, to_apply=%region_31.32 | all-reduce | flops 5348 | bytes 42784 | tf_op jit(solution)/shard_map/psum | solution.py:271
  1660.9 172.3 %all-reduce.23.cloned.1.call-done = (f32[384,6448]{0,1:T(8,128)}, f32[768,1536]{1,0:T(8,128)}) async-done(((f32[384,6448]{0,1:T(8,128)}, f32[768,1536]{1,0:T(8,128)}), (f32[384,6448]{0,1:T(8,128)}, f32[768,1536]{1,0:T(8,128)})) %all-reduce.23.cloned.1.call-update) | async-done | bytes 14622736 | tf_op jit(solution)/shard_map/psum | solution.py:271
  1833.2 8.5 copy.227
  (311 shorter events, 146.6 us)
Async XLA Ops:
  7.2 29.9 %copy-start.69 = (u32[32]{0:T(128)S(1)}, u32[32]{0:T(128)}, u32[]{:S(2)}) copy-start(u32[32]{0:T(128)} %constant.79) | copy-start | bytes 388
  7.2 15.9 copy-start.64
  7.2 31.8 %copy-start.76 = (bf16[12]{0:T(256)(128)(2,1)S(1)}, bf16[12]{0:T(256)(128)(2,1)}, u32[]{:S(2)}) copy-start(bf16[12]{0:T(256)(128)(2,1)} %param.23) | copy-start | bytes 76
  7.2 32.1 %copy-start.77 = (bf16[12]{0:T(256)(128)(2,1)S(1)}, bf16[12]{0:T(256)(128)(2,1)}, u32[]{:S(2)}) copy-start(bf16[12]{0:T(256)(128)(2,1)} %param.24) | copy-start | bytes 76
  7.2 32.3 %copy-start.78 = (bf16[12]{0:T(256)(128)(2,1)S(1)}, bf16[12]{0:T(256)(128)(2,1)}, u32[]{:S(2)}) copy-start(bf16[12]{0:T(256)(128)(2,1)} %param.25) | copy-start | bytes 76
  7.3 32.6 %copy-start.70 = (bf16[832]{0:T(1024)(128)(2,1)S(1)}, bf16[832]{0:T(1024)(128)(2,1)}, u32[]{:S(2)}) copy-start(bf16[832]{0:T(1024)(128)(2,1)} %param.22) | copy-start | bytes 4996
  7.3 67.3 %copy-start.71 = (bf16[768]{0:T(1024)(128)(2,1)S(1)}, bf16[768]{0:T(1024)(128)(2,1)}, u32[]{:S(2)}) copy-start(bf16[768]{0:T(1024)(128)(2,1)} %param.27) | copy-start | bytes 4612
  7.3 98.3 %copy-start.12 = (bf16[1,256,1536]{2,1,0:T(8,128)(2,1)S(1)}, bf16[1,256,1536]{2,1,0:T(8,128)(2,1)}, u32[]{:S(2)}) copy-start(bf16[1,256,1536]{2,1,0:T(8,128)(2,1)} %param.16) | copy-start | bytes 2359300
  7.3 344.1 %all-gather.6.cloned.1.call-start = ((), (), s32[]{:S(2)}) async-start(), calls=%async_computation.3 | async-start | bytes 24760320 | tf_op jit(solution)/shard_map/all_gather | solution.py:88
  8.0 563.8 %all-gather.8.cloned.1.call-start = ((), (), s32[]{:S(2)}) async-start(), calls=%async_computation.4 | async-start | bytes 11796480 | tf_op jit(solution)/shard_map/all_gather | solution.py:89
  8.8 920.0 %reduce-scatter.8.cloned.1.call-start = ((), (), s32[]{:S(2)}) async-start(), calls=%async_computation.6 | async-start | bytes 23592960 | tf_op jit(solution)/shard_map/reduce_scatter | solution.py:261
  70.4 281.0 %copy-start.79 = (bf16[48]{0:T(256)(128)(2,1)}, bf16[48]{0:T(256)(128)(2,1)S(1)}, u32[]{:S(2)}) copy-start(bf16[48]{0:T(256)(128)(2,1)S(1)} %get-tuple-element.123) | copy-start | bytes 292
  73.5 301.7 %copy-start.47 = (f32[256]{0:T(256)}, f32[256]{0:T(256)S(1)}, u32[]{:S(2)}) copy-start(f32[256]{0:T(256)S(1)} %get-tuple-element.150) | copy-start | bytes 3076
  351.4 10.0 copy-start.58
  351.4 10.0 copy-start.72
  351.4 17.1 copy-start.55
  361.3 22.4 %copy-start.11 = (bf16[256,6448]{1,0:T(8,128)(2,1)}, bf16[256,6448]{1,0:T(8,128)(2,1)S(1)}, u32[]{:S(2)}) copy-start(bf16[256,6448]{1,0:T(8,128)(2,1)S(1)} %convolution_convert_fusion) | copy-start | bytes 9904132
  365.8 18.0 collective-permute-start.2
  370.2 13.6 copy-start.20
  373.7 10.1 copy-start.61
  408.0 5.3 collective-permute-start.1
  418.7 11.2 collective-permute-start.1
  435.4 13.6 collective-permute-start.1
  454.5 13.7 collective-permute-start.1
  473.7 13.6 collective-permute-start.1
  492.7 13.6 collective-permute-start.1
  511.8 13.6 collective-permute-start.1
  532.2 16.1 copy-start.9
  565.1 1025.4 %reduce-scatter.6.cloned.1.call-start = ((), (), s32[]{:S(2)}) async-start(), calls=%async_computation.5 | async-start | bytes 49520640 | tf_op jit(solution)/shard_map/reduce_scatter | solution.py:260
  571.8 8.4 copy-start.3
  571.8 8.4 copy-start.5
  571.8 8.4 copy-start.7
  571.8 8.4 copy-start.51
  571.8 8.4 copy-start.68
  608.7 14.6 collective-permute-start
  626.6 23.7 %collective-permute-start = (f32[48,64,128]{2,1,0:T(8,128)}, f32[48,64,128]{2,1,0:T(8,128)}, u32[]{:S(2)}, u32[]{:S(2)}) collective-permute-start(f32[48,64,128]{2,1,0:T(8,128)} %multiply_add_fusion.4), channel_id=1, source_target_pairs={{4,0},{8,4},{12,8},{16,12},{20,16},{24,20},{28,24},{5,1},{9,5},{13... | collective-permute-start | bytes 4718600 | tf_op jit(solution)/shard_map/while/body/eval_jaxpr/ppermute | solution.py:22
  653.7 22.3 %collective-permute-start = (f32[48,64,128]{2,1,0:T(8,128)}, f32[48,64,128]{2,1,0:T(8,128)}, u32[]{:S(2)}, u32[]{:S(2)}) collective-permute-start(f32[48,64,128]{2,1,0:T(8,128)} %multiply_add_fusion.4), channel_id=1, source_target_pairs={{4,0},{8,4},{12,8},{16,12},{20,16},{24,20},{28,24},{5,1},{9,5},{13... | collective-permute-start | bytes 4718600 | tf_op jit(solution)/shard_map/while/body/eval_jaxpr/ppermute | solution.py:22
  679.4 22.4 %collective-permute-start = (f32[48,64,128]{2,1,0:T(8,128)}, f32[48,64,128]{2,1,0:T(8,128)}, u32[]{:S(2)}, u32[]{:S(2)}) collective-permute-start(f32[48,64,128]{2,1,0:T(8,128)} %multiply_add_fusion.4), channel_id=1, source_target_pairs={{4,0},{8,4},{12,8},{16,12},{20,16},{24,20},{28,24},{5,1},{9,5},{13... | collective-permute-start | bytes 4718600 | tf_op jit(solution)/shard_map/while/body/eval_jaxpr/ppermute | solution.py:22
  705.1 22.3 %collective-permute-start = (f32[48,64,128]{2,1,0:T(8,128)}, f32[48,64,128]{2,1,0:T(8,128)}, u32[]{:S(2)}, u32[]{:S(2)}) collective-permute-start(f32[48,64,128]{2,1,0:T(8,128)} %multiply_add_fusion.4), channel_id=1, source_target_pairs={{4,0},{8,4},{12,8},{16,12},{20,16},{24,20},{28,24},{5,1},{9,5},{13... | collective-permute-start | bytes 4718600 | tf_op jit(solution)/shard_map/while/body/eval_jaxpr/ppermute | solution.py:22
  731.0 22.1 %collective-permute-start = (f32[48,64,128]{2,1,0:T(8,128)}, f32[48,64,128]{2,1,0:T(8,128)}, u32[]{:S(2)}, u32[]{:S(2)}) collective-permute-start(f32[48,64,128]{2,1,0:T(8,128)} %multiply_add_fusion.4), channel_id=1, source_target_pairs={{4,0},{8,4},{12,8},{16,12},{20,16},{24,20},{28,24},{5,1},{9,5},{13... | collective-permute-start | bytes 4718600 | tf_op jit(solution)/shard_map/while/body/eval_jaxpr/ppermute | solution.py:22
  756.5 22.3 %collective-permute-start = (f32[48,64,128]{2,1,0:T(8,128)}, f32[48,64,128]{2,1,0:T(8,128)}, u32[]{:S(2)}, u32[]{:S(2)}) collective-permute-start(f32[48,64,128]{2,1,0:T(8,128)} %multiply_add_fusion.4), channel_id=1, source_target_pairs={{4,0},{8,4},{12,8},{16,12},{20,16},{24,20},{28,24},{5,1},{9,5},{13... | collective-permute-start | bytes 4718600 | tf_op jit(solution)/shard_map/while/body/eval_jaxpr/ppermute | solution.py:22
  860.7 9.3 copy-start.23
  860.7 10.8 copy-start.1
  860.7 10.8 copy-start.27
  862.5 15.6 copy-start.10
  870.0 8.0 copy-start.8
  870.1 8.0 copy-start.44
  870.1 8.0 copy-start.45
  870.1 8.0 copy-start.46
  884.1 8.2 copy-start.49
  884.1 8.2 copy-start.60
  884.1 8.2 copy-start.63
  885.8 20.4 %collective-permute-start.3 = (bf16[3,3328]{1,0:T(4,128)(2,1)}, bf16[3,3328]{1,0:T(4,128)(2,1)}, u32[]{:S(2)}, u32[]{:S(2)}) collective-permute-start(bf16[3,3328]{1,0:T(4,128)(2,1)} %slice.240), channel_id=1, source_target_pairs={{4,0},{8,4},{12,8},{16,12},{20,16},{24,20},{28,24},{5,1},{9,5},{13... | collective-permute-start | bytes 59912 | tf_op jit(solution)/shard_map/ppermute | solution.py:22
  926.1 709.7 %reduce-scatter.10.cloned.1.call-start = ((), (), s32[]{:S(2)}) async-start(), calls=%async_computation.7 | async-start | bytes 2129920
  928.7 904.6 %all-reduce.23.cloned.1.call-start = ((), (), s32[]{:S(2)}) async-start(), calls=%async_computation.8 | async-start | bytes 29245440 | tf_op jit(solution)/shard_map/psum | solution.py:271
  1593.8 7.5 copy-start.13
  1593.8 7.5 copy-start.15
  1601.3 10.0 copy-start.36
  1601.3 10.0 copy-start.53
  1601.4 10.0 copy-start.73
  1601.4 32.8 %copy-start.14 = (bf16[1,256,1536]{2,1,0:T(8,128)(2,1)S(1)}, bf16[1,256,1536]{2,1,0:T(8,128)(2,1)}, u32[]{:S(2)}) copy-start(bf16[1,256,1536]{2,1,0:T(8,128)(2,1)} %param.16) | copy-start | bytes 2359300
  1601.4 32.8 %copy-start.19 = (bf16[1,256,1536]{2,1,0:T(8,128)(2,1)S(1)}, bf16[1,256,1536]{2,1,0:T(8,128)(2,1)}, u32[]{:S(2)}) copy-start(bf16[1,256,1536]{2,1,0:T(8,128)(2,1)} %param.18) | copy-start | bytes 2359300
  1601.4 32.8 %copy-start.67 = (f32[256]{0:T(256)S(1)}, f32[256]{0:T(256)}, u32[]{:S(2)}) copy-start(f32[256]{0:T(256)} %get-tuple-element.155) | copy-start | bytes 3076
  1833.2 8.5 copy-start.17
  (40 other events, 125.7 us)
Sparse Core Ops, SparseCore 0:
  9.7 341.6 all-gather.5
  353.0 165.5 all-gather.7
  565.2 328.2 reduce-scatter.7
  926.2 664.2 reduce-scatter.5
  1593.4 40.8 reduce-scatter.9
  1638.4 194.8 all-reduce.22
where the time goes:
time: 1860 us; the launch traced here: 1850 us
  waiting for transfers between devices  1240 us (67%)
  matrix products  158 us (8%)
  blocking collectives  134 us (7%)
  other arithmetic  131 us (7%)
  starting transfers between devices  88.2 us (5%)
  local copies, waits for them, and re-layouts  79.6 us (4%)
  between operations  19.7 us (1%)
    reduce_scatter x1, waiting for transfers between devices, on_device(): lax.psum_scatter(weight_grads[0], 'fsdp', scatter_dimension=0, tiled=True)  662 us
    all_gather x1, waiting for transfers between devices, on_device(): lax.all_gather(w_in, 'fsdp', axis=0, tiled=True)  244 us
    psum x1, waiting for transfers between devices, on_device(): totals = lax.psum(shares, 'seq')  172 us
    ppermute x16, waiting for transfers between devices, passed_along(): lax.ppermute(value, axis, [(source, source + steps) for source in range(f...  161 us
    ppermute x16, starting transfers between devices, passed_along(): lax.ppermute(value, axis, [(source, source + steps) for source in range(f...  87.9 us
    dot_general x3, matrix products, local_output(): jnp.einsum('chts,cshp->cthp', mixing, x_heads, precision=HIGHEST)  54.4 us
    unnamed x2, blocking collectives  52.7 us
  transfers between devices with their start and end apart: 22, of which 18 were waited for; matrix products, arithmetic and copies ran while one was open for 19% of the time, Pallas kernels for 0%

commit v1 on v0

--- a/solution.py
+++ b/solution.py
@@ -1,6 +1,8 @@
 import jax
 import jax.numpy as jnp
 from jax import lax
+from jax.experimental import pallas as pl
+from jax.experimental.pallas import tpu as pltpu
 from jax.sharding import PartitionSpec as P
 
 DI = 3072
@@ -9,6 +11,7 @@
 CONV = 4
 SPAN = 256
 HEADS = 48
+D = 1536
 CHAN = 3328
 
 
@@ -272,9 +275,447 @@
     return (layer_out, d_inputs[None]) + tuple(totals)
 
 
+F32 = jnp.float32
+BF = jnp.bfloat16
+BLK = 256
+TEAM = 8
+HPD = HEADS // TEAM
+CH = HPD * HEADDIM
+NZ, NX, NB, ND = CH, CH, 2 * STATE, 128
+COLS = NZ + NX + NB + ND
+CONVC = NX + NB
+TAIL = CONV - 1
+
+
+def dot(a, b):
+    return lax.dot_general(a, b, (((1,), (0,)), ((), ())), preferred_element_type=F32)
+
+
+def dot_nt(a, b):
+    return lax.dot_general(a, b, (((1,), (1,)), ((), ())), preferred_element_type=F32)
+
+
+def dot_tn(a, b):
+    return lax.dot_general(a, b, (((0,), (0,)), ((), ())), preferred_element_type=F32)
+
+
+def dot_exact(a, b):
+    return lax.dot_general(
+        a, b, (((1,), (0,)), ((), ())), precision=HIGHEST, preferred_element_type=F32
+    )
+
+
+def iota(shape, dim):
+    return lax.broadcasted_iota(jnp.int32, shape, dim)
+
+
+def split_dot(a, b):
+    high = a.astype(BF)
+    low = (a - high.astype(F32)).astype(BF)
+    return dot(high, b) + dot(low, b)
+
+
+def spread():
+    return (iota((128, CH), 1) // HEADDIM == iota((128, CH), 0)).astype(BF)
+
+
+def gather_heads():
+    return (iota((CH, 128), 0) // HEADDIM == iota((CH, 128), 1)).astype(BF)
+
+
+def lower_tri():
+    return (iota((BLK, BLK), 0) >= iota((BLK, BLK), 1)).astype(F32)
+
+
+def softplus(v):
+    return jnp.maximum(v, 0.0) + jnp.log1p(jnp.exp(-jnp.abs(v)))
+
+
+def sigmoid(v):
+    return 1.0 / (1.0 + jnp.exp(-v))
+
+
+def conv_taps(cbuf, cw, tok):
+    out = cw[CONV : CONV + 1, :] + cw[CONV - 1 : CONV, :] * cbuf[8 : 8 + BLK, :]
+    for back in range(1, CONV):
+        term = cw[CONV - 1 - back : CONV - back, :] * cbuf[8 - back : 8 - back + BLK, :]
+        out = out + term * tok[:, back : back + 1]
+    return out
+
+
+def pair_select(left, right):
+    return jnp.where(iota(left.shape, 1) % 128 < HEADDIM, left, right)
+
+
+def fwd_kernel(
+    u_ref, g_ref, w_ref, wo_ref, nw_ref, cw_ref, hp_ref, cp_ref, tok_ref, idr_ref,
+    nrm_ref, proj_ref, halo_ref, ssd_ref, dno_ref, st_ref, stat_ref, br_ref,
+    cbuf, state,
+):
+    step_id = pl.program_id(0)
+
+    @pl.when(step_id == 0)
+    def _():
+        state[...] = jnp.zeros_like(state)
+        cbuf[0:8, :] = jnp.zeros((8, CONVC), F32)
+
+    u = u_ref[...].astype(F32)
+    scale = lax.rsqrt(jnp.mean(u * u, axis=1, keepdims=True) + EPSILON)
+    nrm = (u * scale * nw_ref[...]).astype(BF)
+    nrm_ref[...] = nrm
+    proj = dot(nrm, w_ref[...]).astype(BF)
+    proj_ref[...] = proj
+    cbuf[8 : 8 + BLK, :] = proj[:, NZ : NZ + CONVC].astype(F32)
+    tok = tok_ref[...]
+    halo_ref[0] = cbuf[0:8, :]
+    conv_out = conv_taps(cbuf, cw_ref[...], tok)
+    cbuf[0:8, :] = cbuf[BLK : BLK + 8, :]
+    act = conv_out * sigmoid(conv_out)
+    x = act[:, :CH]
+    bm = act[:, CH : CH + STATE].astype(BF)
+    cm = act[:, CH + STATE :].astype(BF)
+    hp = hp_ref[...]
+    step = softplus(proj[:, NZ + CONVC :].astype(F32) + hp[0:1, :])
+    cum = dot_exact(lower_tri(), -step * hp[1:2, :])
+    cum_t = cum.T
+    mask = (iota((BLK, BLK), 0) >= iota((BLK, BLK), 1)) & (tok[:, 0:1] == idr_ref[0, 0:1, :])
+    gm = jnp.where(mask, dot_nt(cm, bm), 0.0)
+    ex = spread()
+    xs = (x * split_dot(step, ex)).astype(BF)
+    parts = []
+    for pair in range(HPD // 2):
+        xp = xs[:, 128 * pair : 128 * pair + 128]
+        both = []
+        for h in (2 * pair, 2 * pair + 1):
+            decay = jnp.exp(jnp.minimum(cum[:, h : h + 1] - cum_t[h : h + 1, :], 0.0))
+            both.append(dot((gm * decay).astype(BF), xp))
+        parts.append(pair_select(*both))
+    inner = jnp.concatenate(parts, axis=1)
+    old = state[...]
+    st_ref[0] = old
+    keep = tok[:, 7:8]
+    carried = split_dot(keep * jnp.exp(cum), ex) * dot(cm, old.astype(BF))
+    last = cum[BLK - 1 : BLK, :]
+    weights = jnp.exp(last - cum) * step * tok[:, 8:9]
+    through = split_dot(jnp.broadcast_to(keep[BLK - 1 :, :] * jnp.exp(last), (8, 128)), ex)[0:1, :]
+    state[...] = dot_tn(bm, (x * split_dot(weights, ex)).astype(BF)) + through * old
+    cp = cp_ref[...]
+    ssd = inner + carried + cp[1:2, :] * x
+    ssd_ref[...] = ssd
+    z = proj[:, :NZ].astype(F32)
+    gated = ssd * (z * sigmoid(z))
+    br_ref[...] = dot((gated * cp[0:1, :]).astype(BF), wo_ref[...]).astype(BF)
+    dno = dot_nt(g_ref[...], wo_ref[...])
+    dno_ref[...] = dno
+    ss = jnp.sum(gated * gated, axis=1, keepdims=True)
+    sa = jnp.sum(dno * cp[0:1, :] * gated, axis=1, keepdims=True)
+    lane = iota((BLK, 128), 1)
+    stat_ref[...] = jnp.where(lane == 0, ss, jnp.where(lane == 1, sa, 0.0))
+
+
+def bwd_kernel(
+    nrm_ref, g_ref, proj_ref, halo_ref, ssd_ref, dno_ref, st_ref, stat_ref, w_ref,
+    nw_ref, cw_ref, hp_ref, cp_ref, tok_ref, idr_ref,
+    no_ref, dproj_ref, dn_ref, cg_ref, hg_ref, cpg_ref, nwg_ref,
+    cbuf, dcbuf, dstate,
+):
+    step_id = pl.program_id(0)
+
+    @pl.when(step_id == 0)
+    def _():
+        dstate[...] = jnp.zeros_like(dstate)
+        dcbuf[BLK : BLK + 8, :] = jnp.zeros((8, CONVC), F32)
+        cg_ref[...] = jnp.zeros_like(cg_ref)
+        hg_ref[...] = jnp.zeros_like(hg_ref)
+        cpg_ref[...] = jnp.zeros_like(cpg_ref)
+        nwg_ref[...] = jnp.zeros_like(nwg_ref)
+
+    proj = proj_ref[...]
+    tok = tok_ref[...]
+    cw = cw_ref[...]
+    hp = hp_ref[...]
+    cp = cp_ref[...]
+    gate_w = cp[0:1, :]
+    z = proj[:, :NZ].astype(F32)
+    sig_z = sigmoid(z)
+    silu_z = z * sig_z
+    ssd = ssd_ref[...]
+    dno = dno_ref[...]
+    stat = stat_ref[...]
+    s2 = lax.rsqrt(stat[:, 0:1] * (1.0 / DI) + EPSILON)
+    mean_ag = stat[:, 1:2] * (1.0 / DI)
+    gated = ssd * silu_z
+    gs = gated * s2
+    no_ref[...] = (gs * gate_w).astype(BF)
+    d_gate_w = jnp.sum(dno * gs, axis=0, keepdims=True)
+    d_gated = s2 * (dno * gate_w) - gated * (s2 * s2 * s2 * mean_ag)
+    dy = d_gated * silu_z
+    dz = d_gated * ssd * sig_z * (1.0 + z * (1.0 - sig_z))
+    cbuf[0:8, :] = halo_ref[0]
+    cbuf[8 : 8 + BLK, :] = proj[:, NZ : NZ + CONVC].astype(F32)
+    conv_out = conv_taps(cbuf, cw, tok)
+    sig_c = sigmoid(conv_out)
+    act = conv_out * sig_c
+    x = act[:, :CH]
+    bm = act[:, CH : CH + STATE].astype(BF)
+    cm_f = act[:, CH + STATE :]
+    cm = cm_f.astype(BF)
+    dt_in = proj[:, NZ + CONVC :].astype(F32) + hp[0:1, :]
+    step = softplus(dt_in)
+    rate = hp[1:2, :]
+    tri = lower_tri()
+    cum = dot_exact(tri, -step * rate)
+    cum_t = cum.T
+    mask = (iota((BLK, BLK), 0) >= iota((BLK, BLK), 1)) & (tok[:, 0:1] == idr_ref[0, 0:1, :])
+    gm = jnp.where(mask, dot_nt(cm, bm), 0.0)
+    ex = spread()
+    gh = gather_heads()
+    step_x = split_dot(step, ex)
+    xs = (x * step_x).astype(BF)
+    dyb = dy.astype(BF)
+    dyt = dy.T.astype(BF)
+    lane = iota((BLK, 128), 1)
+    dg = jnp.zeros((BLK, BLK), F32)
+    row_sums = jnp.zeros((BLK, 128), F32)
+    col_sums = []
+    e_rows = []
+    for h in range(HPD):
+        pair = h // 2
+        decay = jnp.exp(jnp.minimum(cum[:, h : h + 1] - cum_t[h : h + 1, :], 0.0))
+        mixed = gm * decay
+        half = jnp.where((lane < HEADDIM) == (h % 2 == 0), dyb[:, 128 * pair : 128 * pair + 128], 0)
+        dms = dot_nt(half.astype(BF), xs[:, 128 * pair : 128 * pair + 128])
+        product = dms * mixed
+        row_sums = jnp.where(lane == h, jnp.sum(product, axis=1, keepdims=True), row_sums)
+        col_sums.append(jnp.sum(product, axis=0, keepdims=True))
+        dg = dg + dms * decay
+        e_rows.append(dot(dyt[HEADDIM * h : HEADDIM * h + HEADDIM, :], mixed.astype(BF)))
+    dg = jnp.where(mask, dg, 0.0).astype(BF)
+    e = jnp.concatenate(e_rows, axis=0).T
+    col_sums.append(jnp.zeros((128 - HPD, BLK), F32))
+    col = jnp.concatenate(col_sums, axis=0).T
+    keep = tok[:, 7:8]
+    same_last = tok[:, 8:9]
+    old = st_ref[0]
+    old_b = old.astype(BF)
+    dnew = dstate[...]
+    dnew_b = dnew.astype(BF)
+    carry_w = keep * jnp.exp(cum)
+    carry_x = split_dot(carry_w, ex)
+    dyk = (dy * carry_x).astype(BF)
+    carried = dot(cm, old_b)
+    last = cum[BLK - 1 : BLK, :]
+    fade = jnp.exp(last - cum) * same_last
+    weights = fade * step
+    weights_x = split_dot(weights, ex)
+    zt = dot(bm, dnew_b)
+    xw = (x * weights_x).astype(BF)
+    through = keep[BLK - 1 :, :] * jnp.exp(last)
+    through_x = split_dot(jnp.broadcast_to(through, (8, 128)), ex)[0:1, :]
+    k_term = split_dot(dy * carry_x * carried, gh)
+    r_term = split_dot(x * zt, gh)
+    q_term = split_dot(x * e, gh)
+    pass_term = jnp.sum(old * dnew, axis=0, keepdims=True) * through_x
+    pass_h = split_dot(jnp.broadcast_to(pass_term, (8, CH)), gh)[0:1, :]
+    wr = weights * r_term
+    d_cum = row_sums - col + k_term - wr
+    d_last = jnp.sum(wr, axis=0, keepdims=True) + pass_h
+    d_cum = d_cum + jnp.where(iota((BLK, 128), 0) == BLK - 1, d_last, 0.0)
+    upper = (iota((BLK, BLK), 0) <= iota((BLK, BLK), 1)).astype(F32)
+    d_log = dot_exact(upper, d_cum)
+    d_step = q_term + fade * r_term - d_log * rate
+    d_a = -jnp.sum(d_log * step, axis=0, keepdims=True) * rate
+    d_dt = d_step * sigmoid(dt_in)
+    d_bias = jnp.sum(d_dt, axis=0, keepdims=True)
+    dstate[...] = dot_tn(cm, dyk) + through_x * dnew
+    dx = step_x * e + weights_x * zt + cp[1:2, :] * dy
+    d_skip = jnp.sum(dy * x, axis=0, keepdims=True)
+    dc = dot(dg, bm) + dot_nt(dyk, old_b)
+    db = dot(cm_f.T.astype(BF), dg).T + dot_nt(xw, dnew_b)
+    d_act = jnp.concatenate([dx, db, dc], axis=1)
+    d_conv = d_act * (sig_c * (1.0 + conv_out * (1.0 - sig_c)))
+    dcbuf[0:BLK, :] = d_conv
+    d_in = cw[CONV - 1 : CONV, :] * d_conv
+    cg = [None] * CONV
+    cg[CONV - 1] = jnp.sum(d_conv * cbuf[8 : 8 + BLK, :], axis=0, keepdims=True)
+    for back in range(1, CONV):
+        tap = CONV - 1 - back
+        cg[tap] = jnp.sum(
+            d_conv * (cbuf[8 - back : 8 - back + BLK, :] * tok[:, back : back + 1]),
+            axis=0, keepdims=True,
+        )
+        d_in = d_in + cw[tap : tap + 1, :] * (
+            dcbuf[back : back + BLK, :] * tok[:, 3 + back : 4 + back]
+        )
+    dcbuf[BLK : BLK + 8, :] = dcbuf[0:8, :]
+    d_b = jnp.sum(d_conv, axis=0, keepdims=True)
+    cg_ref[...] += jnp.concatenate(cg + [d_b, jnp.zeros((3, CONVC), F32)], axis=0)
+    hg_ref[...] += jnp.concatenate([d_a, d_bias, jnp.zeros((6, 128), F32)], axis=0)
+    cpg_ref[...] += jnp.concatenate([d_gate_w, d_skip, jnp.zeros((6, CH), F32)], axis=0)
+    dproj = jnp.concatenate([dz, d_in, d_dt], axis=1).astype(BF)
+    dproj_ref[...] = dproj
+    dn = dot_nt(dproj, w_ref[...])
+    dn_ref[...] = dn.astype(BF)
+    nwg_ref[0:1, :] += jnp.sum(dn * nrm_ref[...].astype(F32), axis=0, keepdims=True) / nw_ref[...]
+
+
+def whole(shape):
+    return pl.BlockSpec(shape, lambda i: (0,) * len(shape), pipeline_mode=pl.Buffered(1))
+
+
+def forward_call(u, g, w, wo, nw, cw, hp, cp, tok, idr):
+    n = u.shape[0]
+    blocks = n // BLK
+    rows = lambda c: pl.BlockSpec((BLK, c), lambda i: (i, 0))
+    cube = lambda a, b: pl.BlockSpec((1, a, b), lambda i: (i, 0, 0))
+    sds = jax.ShapeDtypeStruct
+    return pl.pallas_call(
+        fwd_kernel,
+        grid=(blocks,),
+        in_specs=[rows(D), rows(D), whole((D, COLS)), whole((CH, D)), whole((1, D)),
+                  whole((8, CONVC)), whole((8, 128)), whole((8, CH)), rows(128), cube(8, BLK)],
+        out_specs=[rows(D), rows(COLS), cube(8, CONVC), rows(CH), rows(CH), cube(STATE, CH),
+                   rows(128), rows(D)],
+        out_shape=[sds((n, D), BF), sds((n, COLS), BF), sds((blocks, 8, CONVC), F32),
+                   sds((n, CH), F32), sds((n, CH), F32), sds((blocks, STATE, CH), F32),
+                   sds((n, 128), F32), sds((n, D), BF)],
+        scratch_shapes=[pltpu.VMEM((BLK + 8, CONVC), F32), pltpu.VMEM((STATE, CH), F32)],
+        compiler_params=pltpu.CompilerParams(vmem_limit_bytes=56 << 20),
+    )(u, g, w, wo, nw, cw, hp, cp, tok, idr)
+
+
+def backward_call(nrm, g, proj, halo, ssd, dno, st, stat, w, nw, cw, hp, cp, tok, idr):
+    n = nrm.shape[0]
+    blocks = n // BLK
+    back = blocks - 1
+    rows = lambda c: pl.BlockSpec((BLK, c), lambda i: (back - i, 0))
+    cube = lambda a, b: pl.BlockSpec((1, a, b), lambda i: (back - i, 0, 0))
+    keepb = lambda a, b: pl.BlockSpec((a, b), lambda i: (0, 0))
+    sds = jax.ShapeDtypeStruct
+    return pl.pallas_call(
+        bwd_kernel,
+        grid=(blocks,),
+        in_specs=[rows(D), rows(D), rows(COLS), cube(8, CONVC), rows(CH), rows(CH),
+                  cube(STATE, CH), rows(128), whole((D, COLS)), whole((1, D)), whole((8, CONVC)),
+                  whole((8, 128)), whole((8, CH)), rows(128), cube(8, BLK)],
+        out_specs=[rows(CH), rows(COLS), rows(D), keepb(8, CONVC), keepb(8, 128), keepb(8, CH),
+                   keepb(8, D)],
+        out_shape=[sds((n, CH), BF), sds((n, COLS), BF), sds((n, D), BF), sds((8, CONVC), F32),
+                   sds((8, 128), F32), sds((8, CH), F32), sds((8, D), F32)],
+        scratch_shapes=[pltpu.VMEM((BLK + 8, CONVC), F32), pltpu.VMEM((BLK + 8, CONVC), F32),
+                        pltpu.VMEM((STATE, CH), F32)],
+        compiler_params=pltpu.CompilerParams(vmem_limit_bytes=56 << 20),
+    )(nrm, g, proj, halo, ssd, dno, st, stat, w, nw, cw, hp, cp, tok, idr)
+
+
+def token_info(ids_full, first, n):
+    length = ids_full.shape[0]
+    pad = jnp.concatenate(
+        [jnp.full((8,), -1, jnp.int32), ids_full, jnp.full((8,), -2, jnp.int32)]
+    )
+    window = lax.dynamic_slice_in_dim(pad, first, n + 16)
+    own = window[8 : 8 + n]
+    blocks = own.reshape(-1, BLK)
+    before = window[7 : 7 + n].reshape(-1, BLK)[:, :1]
+    cols = [own]
+    for back in range(1, CONV):
+        cols.append((window[8 - back : 8 - back + n] == own))
+    for ahead in range(1, CONV):
+        cols.append((window[8 + ahead : 8 + ahead + n] == own))
+    cols.append((blocks == before).reshape(-1))
+    cols.append((blocks == blocks[:, -1:]).reshape(-1))
+    table = jnp.stack([c.astype(F32) for c in cols], axis=1)
+    tok = jnp.pad(table, ((0, 0), (0, 128 - table.shape[1])))
+    idr = jnp.broadcast_to(own.astype(F32).reshape(-1, 1, BLK), (n // BLK, 8, BLK))
+    return tok, idr
+
+
+def on_team(
+    tokens, segment_ids, cotangent, w_in, w_out, conv_w, conv_b, a_log, dt_bias, d_skip,
+    norm_w, gate_w,
+):
+    place = lax.axis_index("seq")
+    depth = lax.axis_index("fsdp")
+    shards = lax.axis_size("fsdp")
+    n = tokens.shape[1] * TEAM
+    ch0 = place * CH
+    cut = lambda a, start, size: lax.dynamic_slice_in_dim(a, start, size, a.ndim - 1)
+    w_shard = jnp.concatenate(
+        [cut(w_in, ch0, CH), cut(w_in, DI + ch0, CH), w_in[:, 2 * DI : 2 * DI + NB],
+         jnp.pad(cut(w_in, DI + CHAN + place * HPD, HPD), ((0, 0), (0, ND - HPD)))], axis=1)
+    w_loc = lax.all_gather(w_shard, "fsdp", axis=0, tiled=True)
+    rows_out = w_out.shape[0]
+    holder = ch0 // rows_out
+    w_out_mine = lax.dynamic_slice_in_dim(w_out, ch0 - holder * rows_out, CH, 0)
+    wo_loc = lax.psum(jnp.where(depth == holder, w_out_mine, 0), "fsdp")
+    small = jnp.concatenate([conv_w.reshape(-1), conv_b, a_log, dt_bias, d_skip, norm_w, gate_w])
+    small = lax.all_gather(small, "fsdp", axis=0, tiled=False).astype(F32)
+    sizes = [conv_w.size, conv_b.size, a_log.size, dt_bias.size, d_skip.size, norm_w.size, gate_w.size]
+    offs = [0]
+    for size in sizes:
+        offs.append(offs[-1] + size)
+    part = [small[:, offs[i] : offs[i + 1]] for i in range(7)]
+    taps = part[0].reshape(shards, CONV, -1).transpose(1, 0, 2).reshape(CONV, CHAN)
+    bias, alog, dtb, skip, normw, gatew = [p.reshape(1, -1) for p in part[1:]]
+    conv_all = jnp.concatenate([taps, bias, jnp.zeros((3, CHAN), F32)], axis=0)
+    cw = jnp.concatenate([cut(conv_all, ch0, CH), conv_all[:, DI:]], axis=1)
+    heads = jnp.concatenate([dtb, jnp.exp(alog), jnp.zeros((6, HEADS), F32)], axis=0)
+    hp = cut(heads, place * HPD, HPD)
+    hp = jnp.concatenate(
+        [hp, jnp.where(jnp.arange(8)[:, None] == 0, -100.0, 0.0) * jnp.ones((8, 128 - HPD), F32)], axis=1)
+    cp = jnp.concatenate([gatew, jnp.repeat(skip, HEADDIM, axis=1), jnp.zeros((6, DI), F32)], axis=0)
+    cp = cut(cp, ch0, CH)
+    tok, idr = token_info(segment_ids[0], 0, n)
+    u_own, g_own = tokens[0], cotangent[0]
+    u = lax.all_gather(u_own, "seq", axis=0, tiled=True)
+    g = lax.all_gather(g_own, "seq", axis=0, tiled=True)
+    nrm, proj, halo, ssd, dno, st, stat, br = forward_call(
+        u, g, w_loc, wo_loc, normw, cw, hp, cp, tok, idr)
+    stat = lax.psum(stat, "seq")
+    no, dproj, dn, cg, hg, cpg, nwg = backward_call(
+        nrm, g, proj, halo, ssd, dno, st, stat, w_loc, normw, cw, hp, cp, tok, idr)
+    branch = lax.psum_scatter(br, "seq", scatter_dimension=0, tiled=True).astype(F32)
+    d_normed = lax.psum_scatter(dn, "seq", scatter_dimension=0, tiled=True).astype(F32)
+    ss = lax.dynamic_slice_in_dim(stat[:, 0:1], place * BLK, BLK, 0)
+    uf = u_own.astype(F32)
+    layer_out = (uf + branch * lax.rsqrt(ss / DI + EPSILON)).astype(BF)
+    s1 = lax.rsqrt(jnp.mean(uf * uf, axis=1, keepdims=True) + EPSILON)
+    along = d_normed * normw
+    token_grad = g_own.astype(F32) + s1 * along - uf * (s1 * s1 * s1) * jnp.mean(along * uf, axis=1, keepdims=True)
+    wig = dot_tn(nrm, dproj).astype(BF)
+    wog = dot_tn(no, g).astype(BF)
+    wig = lax.psum_scatter(wig, "fsdp", scatter_dimension=0, tiled=True)
+    bc = lax.psum(wig[:, NZ + NX : NZ + NX + NB].astype(F32), "seq")
+    own_cols = jnp.concatenate([wig[:, : NZ + NX], wig[:, NZ + NX + NB :]], axis=1)
+    allc = lax.all_gather(own_cols, "seq", axis=0, tiled=False).astype(F32)
+    flat = lambda a: a.transpose(1, 0, 2).reshape(a.shape[1], -1)
+    w_in_grad = jnp.concatenate(
+        [flat(allc[:, :, :CH]), flat(allc[:, :, CH : 2 * CH]), bc,
+         flat(allc[:, :, 2 * CH : 2 * CH + HPD])], axis=1)
+    wog_z = lax.psum(wog, "fsdp")
+    wog_all = lax.all_gather(wog_z, "seq", axis=0, tiled=True)
+    w_out_grad = lax.dynamic_slice_in_dim(wog_all, depth * rows_out, rows_out, 0).astype(F32)
+    spot = lambda a, width, size: lax.dynamic_update_slice_in_dim(
+        jnp.zeros(a.shape[:-1] + (width,), F32), a, place * size, a.ndim - 1)
+    convg = jnp.concatenate([spot(cg[:5, :CH], DI, CH), cg[:5, CH:]], axis=1)
+    headg = spot(hg[:2, :HPD], HEADS, HPD)
+    chang = spot(cpg[:2], DI, CH)
+    convg, headg, chang, normg = lax.psum((convg, headg, chang, nwg[0]), ("seq", "fsdp"))
+    mine = lambda a, size: cut(a, depth * size, size)
+    conv_wg = mine(convg[:4], CHAN // shards)
+    conv_bg = mine(convg[4], CHAN // shards)
+    ag = mine(headg[0], HEADS // shards)
+    dg = mine(headg[1], HEADS // shards)
+    sg = mine(chang[1].reshape(HEADS, HEADDIM).sum(axis=1), HEADS // shards)
+    gg = mine(chang[0], DI // shards)
+    ng = mine(normg, D // shards)
+    return (layer_out[None], token_grad[None], w_in_grad, w_out_grad, conv_wg, conv_bg, ag, dg, sg, ng, gg)
+
+
 def solution(mesh):
+    body = on_team if mesh.shape["seq"] == TEAM else on_device
     return jax.shard_map(
-        on_device,
+        body,
         mesh=mesh,
         in_specs=(
             P("fsdp", "seq", None),

time: 1860 us -> 944 us (0.51)
  waiting for transfers between devices: 1240 us -> 684 us
  matrix products: 158 us -> 18.7 us
  other arithmetic: 131 us -> 36.3 us
  starting transfers between devices: 88.2 us -> 0.7 us
  Pallas kernels: 0 us -> 81 us
  blocking collectives: 134 us -> 64.2 us
  local copies, waits for them, and re-layouts: 79.6 us -> 43 us
    reduce_scatter x2 -> x3, waiting for transfers between devices: 662 us -> 184 us  [the longest x1 63.9 us: on_team(): lax.psum_scatter(br, 'seq', scatter_dimension=0, tiled=True).astype(F32)]
    ppermute x16 -> x0, waiting for transfers between devices: 161 us -> none  [passed_along(): lax.ppermute(value, axis, [(source, source + steps) for source in range(f...]
    dot_general x18 -> x2, matrix products: 158 us -> 18.7 us  [dot_tn(): lax.dot_general(a, b, (((0,), (0,)), ((), ())), preferred_element_type=F32)]
    psum x1 -> x5, waiting for transfers between devices: 172 us -> 270 us  [the longest x1 79.4 us: on_team(): lax.psum((convg, headg, chang, nwg[0]), ('seq', 'fsdp'))]
    ppermute x16 -> x0, starting transfers between devices: 87.9 us -> none  [passed_along(): lax.ppermute(value, axis, [(source, source + steps) for source in range(f...]
    pallas_call x0 -> x2, Pallas kernels: none -> 81 us  [the longest x1 43.6 us: backward_call(): pl.pallas_call(bwd_kernel, grid=(blocks,), in_specs=[rows(D), rows(D), ro...]
    all_gather x3 -> x0, blocking collectives: 57 us -> none  [the longest x1 30.3 us: on_device(): lax.all_gather(gate_w, 'fsdp', axis=0, tiled=True)]
    convert_element_type x21 -> x5, other arithmetic: 43.3 us -> 13.6 us  [the longest x1 7.42 us: on_team(): allc = lax.all_gather(own_cols, 'seq', axis=0, tiled=False).astype(F32)]
  transfers between devices with their start and end apart: 22 -> 13, of which waited for: 18 -> 13; matrix products, arithmetic and copies ran while one was open for 19% -> 8% of each run, Pallas kernels for 0% -> 0%
where the time goes in v1:
time: 944 us; the launch traced here: 943 us
  waiting for transfers between devices  684 us (72%)
  Pallas kernels  81 us (9%)
  blocking collectives  64.2 us (7%)
  local copies, waits for them, and re-layouts  43 us (5%)
  other arithmetic  36.3 us (4%)
  matrix products  18.7 us (2%)
  between operations  15.1 us (2%)
    psum x1, waiting for transfers between devices, on_team(): lax.psum((convg, headg, chang, nwg[0]), ('seq', 'fsdp'))  79.4 us
    all_gather x1, waiting for transfers between devices, on_team(): w_loc = lax.all_gather(w_shard, 'fsdp', axis=0, tiled=True)  71.7 us
    reduce_scatter x1, waiting for transfers between devices, on_team(): lax.psum_scatter(br, 'seq', scatter_dimension=0, tiled=True).astype(F32)  63.9 us
    reduce_scatter x1, waiting for transfers between devices, on_team(): lax.psum_scatter(dn, 'seq', scatter_dimension=0, tiled=True).astype(F32)  63.2 us
    reduce_scatter x1, waiting for transfers between devices, on_team(): wig = lax.psum_scatter(wig, 'fsdp', scatter_dimension=0, tiled=True)  56.9 us
    psum x1, waiting for transfers between devices, on_team(): stat = lax.psum(stat, 'seq')  56.5 us
    psum x1, waiting for transfers between devices, on_team(): bc = lax.psum(wig[:, NZ + NX:NZ + NX + NB].astype(F32), 'seq')  55.5 us
    psum x1, waiting for transfers between devices, on_team(): wog_z = lax.psum(wog, 'fsdp')  54.7 us
  transfers between devices with their start and end apart: 13, of which 13 were waited for; matrix products, arithmetic and copies ran while one was open for 8% of the time, Pallas kernels for 0%

profile of v1, /device:TPU:0, one launch (start us, length us, event | category | flops | bytes accessed | tf_op | source)
XLA Modules:
  0.0 943.1 jit_solution(16872729196702703843)
XLA Ops:
  7.3 2.5 dynamic-slice_select_fusion
  9.8 0.7 constant_dynamic-slice_fusion.7
  10.9 1.1 constant_dynamic-slice_fusion.9
  12.6 1.0 fusion.7
  13.6 0.7 all-gather.16.cloned.1.call-update
  14.4 0.5 all-gather.14.cloned.1.call-update
  14.9 0.5 broadcast.101
  15.5 0.7 fusion.29
  16.3 0.6 dynamic-slice.4
  17.7 0.4 dynamic-update-slice
  18.1 23.3 %all-reduce.4 = bf16[21392]{0:T(1024)(128)(2,1)S(1)} all-reduce(bf16[21392]{0:T(1024)(128)(2,1)S(1)} %dynamic-update-slice), channel_id=4, replica_groups=mesh['seq'=8,'fsdp'=4] {'fsdp'}, use_global_device_ids=true, to_apply=%add.4 | all-reduce | flops 21392 | bytes 85568
  42.7 0.6 copy.92
  44.5 1.0 pad.15.tok_ref
  45.7 0.7 pad_maximum_fusion.4.hp_ref
  46.4 0.6 pad_maximum_fusion.3.cw_ref
  47.0 0.7 fusion.10.cp_ref
  47.7 23.6 %all-reduce.12.cloned.1.call-done.wo_ref = bf16[384,1536]{1,0:T(8,128)(2,1)} async-done(((bf16[384,1536]{1,0:T(8,128)(2,1)}), bf16[384,1536]{1,0:T(8,128)(2,1)}) %all-reduce.12.cloned.1.call-update) | async-done | bytes 1179664 | tf_op jit(solution)/shard_map/psum | solution.py:650
  71.3 71.7 %all-gather.10.cloned.1.call-done.w_ref = bf16[1536,1152]{1,0:T(8,128)(2,1)} async-done(((bf16[384,1152]{1,0:T(8,128)(2,1)}), bf16[1536,1152]{1,0:T(8,128)(2,1)}) %all-gather.10.cloned.1.call-update) | async-done | bytes 3538960 | tf_op jit(solution)/shard_map/all_gather | solution.py:646
  143.0 46.0 %all-gather.16.cloned.1.call-done = bf16[1,2048,1536]{2,1,0:T(8,128)(2,1)} async-done(((bf16[1,256,1536]{2,1,0:T(8,128)(2,1)}), bf16[1,2048,1536]{2,1,0:T(8,128)(2,1)}) %all-gather.16.cloned.1.call-update) | async-done | bytes 6291472 | tf_op jit(solution)/shard_map/all_gather | solution.py:671
  189.0 47.3 %all-gather.14.cloned.1.call-done = bf16[1,2048,1536]{2,1,0:T(8,128)(2,1)} async-done(((bf16[1,256,1536]{2,1,0:T(8,128)(2,1)}), bf16[1,2048,1536]{2,1,0:T(8,128)(2,1)}) %all-gather.14.cloned.1.call-update) | async-done | bytes 6291472 | tf_op jit(solution)/shard_map/all_gather | solution.py:670
  236.3 0.6 broadcast_in_dim.57.idr_ref
  237.0 37.3 %shard_map.203 = (bf16[2048,1536]{1,0:T(8,128)(2,1)}, bf16[2048,1152]{1,0:T(8,128)(2,1)}, f32[8,8,640]{2,1,0:T(8,128)}, f32[2048,384]{1,0:T(8,128)}, f32[2048,38...) custom-call(bf16[2048,1536]{1,0:T(8,128)(2,1)} %bitcast.76, ...), custom_call_target="tpu_custom_call" | custom-call | tf_op jit(solution)/shard_map/pallas_call | solution.py:572
  274.6 56.5 %all-reduce.14.cloned.1.call-done.stat_ref = f32[2048,128]{1,0:T(8,128)} async-done(((f32[2048,128]{1,0:T(8,128)}), f32[2048,128]{1,0:T(8,128)}) %all-reduce.14.cloned.1.call-update) | async-done | bytes 1048592 | tf_op jit(solution)/shard_map/psum | solution.py:674
  331.1 43.6 %shard_map.204 = (bf16[2048,384]{1,0:T(8,128)(2,1)}, bf16[2048,1152]{1,0:T(8,128)(2,1)}, bf16[2048,1536]{1,0:T(8,128)(2,1)}, f32[8,640]{1,0:T(8,128)}, f32[8,128...) custom-call(bf16[2048,1536]{1,0:T(8,128)(2,1)} %get-tuple-element.28.nrm_ref, bf16[2048,1536]{1,0:T(8,128)(2,1)} %bitcast.71, ...), custom_call_target="tpu_custom_call" | custom-call | tf_op jit(solution)/shard_map/pallas_call | solution.py:595
  374.8 12.3 %convolution_convert_fusion = bf16[1536,1152]{1,0:T(8,128)(2,1)} fusion(bf16[2048,1536]{1,0:T(8,128)(2,1)S(1)} %bitcast.78, bf16[2048,1152]{1,0:T(8,128)(2,1)} %get-tuple-element.35), kind=kOutput, calls=%fused_computation.1 | convolution fusion | flops 7249526784 | bytes 14548992 | tf_op jit(solution)/shard_map/dot_general | solution.py:299
  387.1 1.3 copy-done.11
  388.5 6.5 convolution_convert_fusion.1
  395.1 0.7 pad_maximum_fusion.2
  395.8 56.9 %reduce-scatter.8.cloned.1.call-done = bf16[384,1152]{1,0:T(8,128)(2,1)} async-done(((bf16[1536,1152]{1,0:T(8,128)(2,1)}), bf16[384,1152]{1,0:T(8,128)(2,1)}) %reduce-scatter.8.cloned.1.call-update) | async-done | bytes 884752 | tf_op jit(solution)/shard_map/reduce_scatter | solution.py:687
  452.6 1.7 slice_convert_fusion
  454.4 0.5 reduce-scatter.6.cloned.1.call-update
  455.0 0.7 reduce-scatter.4.cloned.1.call-update
  456.1 0.9 pad_maximum_fusion.1
  457.1 54.7 %all-reduce.18.cloned.1.call-done = bf16[384,1536]{1,0:T(8,128)(2,1)} async-done(((bf16[384,1536]{1,0:T(8,128)(2,1)}), bf16[384,1536]{1,0:T(8,128)(2,1)}) %all-reduce.18.cloned.1.call-update) | async-done | bytes 1179664 | tf_op jit(solution)/shard_map/psum | solution.py:695
  511.9 0.7 slice.140
  512.6 0.8 slice_reduce_fusion.1
  513.5 0.7 constant_dynamic-update-slice_fusion
  514.2 40.9 %all-reduce.5 = (f32[2,48]{1,0:T(2,128)S(1)}, f32[2,3072]{1,0:T(2,128)S(1)}, f32[1536]{0:T(1024)S(1)}) all-reduce(f32[2,48]{1,0:T(2,128)S(1)} %dynamic_update_slice.10, f32[2,3072]{1,0:T(2,128)S(1)} %constant_dynamic-update-slice_fusion, f32[1536]{0:T(1024)S(1)} %slice_reduce_fusion.1), channel_id=1, replica_groups=mesh['seq'=8,'fsdp'=4] {'seq','fsdp'}, use_global_device_ids=true, to_apply=%region_10.11 | all-reduce | flops 7776 | bytes 62208 | tf_op jit(solution)/shard_map/psum | solution.py:703
  555.3 0.7 dynamic_slice.73
  556.0 0.6 dynamic_slice.72
  556.5 0.6 fusion.22
  557.2 1.0 rsqrt_reduce_fusion
  558.2 0.6 fusion.23
  558.8 79.4 %all-reduce.20.cloned.1.call-done = f32[5,3328]{1,0:T(8,128)} async-done(((f32[5,3328]{1,0:T(8,128)}), f32[5,3328]{1,0:T(8,128)}) %all-reduce.20.cloned.1.call-update) | async-done | bytes 66576 | tf_op jit(solution)/shard_map/psum | solution.py:703
  638.2 0.9 slice.165
  639.1 0.9 slice.164
  640.0 0.7 fusion.21
  640.7 0.7 constant_dynamic-slice_fusion.4
  641.4 55.5 %all-reduce.16.cloned.1.call-done = f32[384,256]{1,0:T(8,128)} async-done(((f32[384,256]{1,0:T(8,128)}), f32[384,256]{1,0:T(8,128)}) %all-reduce.16.cloned.1.call-update) | async-done | bytes 393232 | tf_op jit(solution)/shard_map/psum | solution.py:688
  696.9 1.2 copy.85
  698.1 63.2 %reduce-scatter.6.cloned.1.call-done = bf16[256,1536]{1,0:T(8,128)(2,1)} async-done(((bf16[2048,1536]{1,0:T(8,128)(2,1)}), bf16[256,1536]{1,0:T(8,128)(2,1)}) %reduce-scatter.6.cloned.1.call-update) | async-done | bytes 786448 | tf_op jit(solution)/shard_map/reduce_scatter | solution.py:678
  761.2 1.6 fusion.2
  762.8 63.9 %reduce-scatter.4.cloned.1.call-done = bf16[256,1536]{1,0:T(8,128)(2,1)} async-done(((bf16[2048,1536]{1,0:T(8,128)(2,1)}), bf16[256,1536]{1,0:T(8,128)(2,1)}) %reduce-scatter.4.cloned.1.call-update) | async-done | bytes 786448 | tf_op jit(solution)/shard_map/reduce_scatter | solution.py:677
  826.8 3.5 fusion.5
  830.3 41.0 %all-gather.18.cloned.1.call-done = bf16[3072,896]{1,0:T(8,128)(2,1)} async-done(((bf16[384,896]{1,0:T(8,128)(2,1)}), bf16[3072,896]{1,0:T(8,128)(2,1)}) %all-gather.18.cloned.1.call-update) | async-done | bytes 5505040 | tf_op jit(solution)/shard_map/all_gather | solution.py:690
  871.3 1.2 slice.163
  872.5 7.4 convert.7
  880.0 0.5 copy.91
  880.5 9.1 slice_bitcast_fusion.1
  889.5 6.1 copy.82
  895.6 6.0 copy.83
  901.7 8.6 pad_maximum_fusion
  910.2 21.8 %all-gather.12.cloned.1.call-done = bf16[3072,1536]{1,0:T(8,128)(2,1)} async-done(((bf16[384,1536]{1,0:T(8,128)(2,1)}), bf16[3072,1536]{1,0:T(8,128)(2,1)}) %all-gather.12.cloned.1.call-update) | async-done | bytes 9437200 | tf_op jit(solution)/shard_map/all_gather | solution.py:696
  932.0 4.5 dynamic-slice_convert_fusion
  (120 shorter events, 5.3 us)
Async XLA Ops:
  7.2 3.6 slice-start.4
  7.2 64.1 %all-reduce.12.cloned.1.call-start = ((), (), s32[]{:S(2)}) async-start(), calls=%async_computation.4 | async-start | bytes 2359296 | tf_op jit(solution)/shard_map/psum | solution.py:650
  9.8 133.2 %all-gather.10.cloned.1.call-start = ((), (), s32[]{:S(2)}) async-start(), calls=%async_computation.3 | async-start | bytes 4423680 | tf_op jit(solution)/shard_map/all_gather | solution.py:646
  12.2 3.2 copy-start.2
  12.2 4.0 copy-start.4
  12.3 4.1 copy-start.12
  12.3 5.3 copy-start.5
  12.3 5.3 copy-start.6
  12.3 5.3 copy-start.7
  12.3 5.3 copy-start.8
  12.3 5.3 copy-start.9
  12.3 5.3 copy-start.10
  13.6 175.5 %all-gather.16.cloned.1.call-start = ((), (), s32[]{:S(2)}) async-start(), calls=%async_computation.14 | async-start | bytes 7077888 | tf_op jit(solution)/shard_map/all_gather | solution.py:671
  14.3 222.0 %all-gather.14.cloned.1.call-start = ((), (), s32[]{:S(2)}) async-start(), calls=%async_computation.13 | async-start | bytes 7077888 | tf_op jit(solution)/shard_map/all_gather | solution.py:670
  14.9 316.2 %all-reduce.14.cloned.1.call-start = ((), (), s32[]{:S(2)}) async-start(), calls=%async_computation.6 | async-start | bytes 2097152 | tf_op jit(solution)/shard_map/psum | solution.py:674
  274.3 100.4 %slice-start = ((s8[6291456]{0:T(1024)(128)(4,1)}), s8[2097152]{0:T(1024)(128)(4,1)S(1)}, s32[]{:S(2)}) async-start(s8[6291456]{0:T(1024)(128)(4,1)} %bitcast.77), calls=%async_computation.16 | async-start | bytes 4194304
  274.3 178.3 %reduce-scatter.8.cloned.1.call-start = ((), (), s32[]{:S(2)}) async-start(), calls=%async_computation.8 | async-start | bytes 4423680 | tf_op jit(solution)/shard_map/reduce_scatter | solution.py:687
  331.1 43.7 %slice-start.1 = ((s8[6291456]{0:T(1024)(128)(4,1)}), s8[4194304]{0:T(1024)(128)(4,1)S(1)}, s32[]{:S(2)}) async-start(s8[6291456]{0:T(1024)(128)(4,1)} %bitcast.77), calls=%async_computation.17 | async-start | bytes 8388608
  387.1 1.4 copy-start.11
  387.1 124.7 %all-reduce.18.cloned.1.call-start = ((), (), s32[]{:S(2)}) async-start(), calls=%async_computation.10 | async-start | bytes 2359296 | tf_op jit(solution)/shard_map/psum | solution.py:695
  388.5 6.5 copy-start.3
  395.0 243.2 %all-reduce.20.cloned.1.call-start = ((), (), s32[]{:S(2)}) async-start(), calls=%async_computation.12 | async-start | bytes 212992 | tf_op jit(solution)/shard_map/psum | solution.py:703
  395.7 301.2 %all-reduce.16.cloned.1.call-start = ((), (), s32[]{:S(2)}) async-start(), calls=%async_computation.9 | async-start | bytes 786432 | tf_op jit(solution)/shard_map/psum | solution.py:688
  454.4 306.9 %reduce-scatter.6.cloned.1.call-start = ((), (), s32[]{:S(2)}) async-start(), calls=%async_computation.7 | async-start | bytes 7077888 | tf_op jit(solution)/shard_map/reduce_scatter | solution.py:678
  455.0 371.8 %reduce-scatter.4.cloned.1.call-start = ((), (), s32[]{:S(2)}) async-start(), calls=%async_computation.5 | async-start | bytes 7077888 | tf_op jit(solution)/shard_map/reduce_scatter | solution.py:677
  455.0 0.9 slice-start.2
  455.0 1.1 slice-start.3
  455.7 415.6 %all-gather.18.cloned.1.call-start = ((), (), s32[]{:S(2)}) async-start(), calls=%async_computation.15 | async-start | bytes 6193152 | tf_op jit(solution)/shard_map/all_gather | solution.py:690
  456.1 305.1 %copy-start = (bf16[1,256,1536]{2,1,0:T(8,128)(2,1)S(1)}, bf16[1,256,1536]{2,1,0:T(8,128)(2,1)}, u32[]{:S(2)}) copy-start(bf16[1,256,1536]{2,1,0:T(8,128)(2,1)} %param.12) | copy-start | bytes 2359300
  457.0 369.7 %copy-start.1 = (bf16[1,256,1536]{2,1,0:T(8,128)(2,1)S(1)}, bf16[1,256,1536]{2,1,0:T(8,128)(2,1)}, u32[]{:S(2)}) copy-start(bf16[1,256,1536]{2,1,0:T(8,128)(2,1)} %param.14) | copy-start | bytes 2359300
  457.1 475.0 %all-gather.12.cloned.1.call-start = ((), (), s32[]{:S(2)}) async-start(), calls=%async_computation.11 | async-start | bytes 10616832 | tf_op jit(solution)/shard_map/all_gather | solution.py:696
Sparse Core Ops, SparseCore 0:
  11.0 60.2 all-reduce.11
  73.4 69.5 all-gather.9
  144.9 44.1 all-gather.15
  190.8 45.5 all-gather.13
  274.5 56.5 all-reduce.13
  387.2 65.3 reduce-scatter.7
  455.6 56.1 all-reduce.17
  518.0 120.1 all-reduce.19
  641.9 54.9 all-reduce.15
  700.1 61.0 reduce-scatter.5
  765.0 61.7 reduce-scatter.3
  829.1 42.1 all-gather.17
  873.2 58.8 all-gather.11

commit v2 on v0

--- a/solution.py
+++ b/solution.py
@@ -1,6 +1,8 @@
 import jax
 import jax.numpy as jnp
 from jax import lax
+from jax.experimental import pallas as pl
+from jax.experimental.pallas import tpu as pltpu
 from jax.sharding import PartitionSpec as P
 
 DI = 3072
@@ -9,6 +11,8 @@
 CONV = 4
 SPAN = 256
 HEADS = 48
+D = 1536
+WIDTH = 6448
 CHAN = 3328
 
 
@@ -272,9 +276,1060 @@
     return (layer_out, d_inputs[None]) + tuple(totals)
 
 
+F32 = jnp.float32
+BF = jnp.bfloat16
+BLK = 256
+TEAM = 8
+HPD = HEADS // TEAM
+CH = HPD * HEADDIM
+NZ, NX, NB, ND = CH, CH, 2 * STATE, 64
+COLS = NZ + NX + NB + ND
+REST = NX + NB + ND
+CONVC = NX + NB
+TAIL = CONV - 1
+
+
+def dot(a, b):
+    return lax.dot_general(a, b, (((1,), (0,)), ((), ())), preferred_element_type=F32)
+
+
+def dot_nt(a, b):
+    return lax.dot_general(a, b, (((1,), (1,)), ((), ())), preferred_element_type=F32)
+
+
+def dot_tn(a, b):
+    return lax.dot_general(a, b, (((0,), (0,)), ((), ())), preferred_element_type=F32)
+
+
+def dot_exact(a, b):
+    return lax.dot_general(
+        a, b, (((1,), (0,)), ((), ())), precision=HIGHEST, preferred_element_type=F32
+    )
+
+
+def iota(shape, dim):
+    return lax.broadcasted_iota(jnp.int32, shape, dim)
+
+
+def split_dot(a, b):
+    high = a.astype(BF)
+    low = (a - high.astype(F32)).astype(BF)
+    return dot(high, b) + dot(low, b)
+
+
+def spread():
+    return (iota((128, CH), 1) // HEADDIM == iota((128, CH), 0)).astype(BF)
+
+
+def gather_heads():
+    return (iota((CH, 128), 0) // HEADDIM == iota((CH, 128), 1)).astype(BF)
+
+
+def lower_tri():
+    return (iota((BLK, BLK), 0) >= iota((BLK, BLK), 1)).astype(F32)
+
+
+def softplus(v):
+    return jnp.maximum(v, 0.0) + jnp.log1p(jnp.exp(-jnp.abs(v)))
+
+
+def sigmoid(v):
+    return 1.0 / (1.0 + jnp.exp(-v))
+
+
+def conv_taps(cbuf, cw, tok):
+    out = cw[CONV : CONV + 1, :] + cw[CONV - 1 : CONV, :] * cbuf[8 : 8 + BLK, :]
+    for back in range(1, CONV):
+        term = cw[CONV - 1 - back : CONV - back, :] * cbuf[8 - back : 8 - back + BLK, :]
+        out = out + term * tok[:, back : back + 1]
+    return out
+
+
+def pair_select(left, right):
+    return jnp.where(iota(left.shape, 1) % 128 < HEADDIM, left, right)
+
+
+def head_of(slot, chip, core):
+    first = 12 * slot + 3 * chip + 2 * core
+    second = 12 * (core + 2 * (slot - 4)) + 3 * chip + 1
+    return first, second
+
+
+def pick_heads():
+    seq = lax.axis_index("seq")
+    chip, core = lax.div(seq, 2), lax.rem(seq, 2)
+    slot = iota((128, 128), 1)
+    first, second = head_of(slot, chip, core)
+    head = jnp.where(slot < 4, first, jnp.where(slot < HPD, second, -1))
+    return (iota((128, 128), 0) == head).astype(BF)
+
+
+def own_heads(par, dt_cols):
+    pick = pick_heads()
+    pair = jnp.concatenate([par[5:6, CH : CH + 128], par[5:6, CH + 128 :], jnp.zeros((6, 128), F32)], axis=0)
+    pair = dot(pair.astype(BF), pick)
+    wide = jnp.concatenate([dt_cols, jnp.zeros((BLK, 128 - ND), BF)], axis=1)
+    return jnp.exp(pair[1:2, :]), dot(wide, pick) + pair[0:1, :], iota((BLK, 128), 1) < HPD, pick
+
+
+def norm_gain(par):
+    return jnp.concatenate([par[7 + i : 8 + i, :512] for i in range(3)], axis=1)
+
+
+def row_sum(q):
+    high = q.astype(BF)
+    low = (q - high.astype(F32)).astype(BF)
+    ones = jnp.ones((8, q.shape[1]), BF)
+    return (dot_nt(ones, high) + dot_nt(ones, low))[0:1, :]
+
+
+def scan_forward(j, nrm, w_v, par, tok, idr, cbuf, state, projc_ref, st_ref, ssd_v):
+    rows = pl.ds(pl.multiple_of(BLK * j, BLK), BLK)
+    proj = dot_nt(nrm, w_v[NZ:, :]).astype(BF)
+    projc_ref[...] = proj
+    cbuf[8 : 8 + BLK, :] = proj[:, :CONVC].astype(F32)
+    conv_out = conv_taps(cbuf, par, tok)
+    cbuf[0:8, :] = cbuf[BLK : BLK + 8, :]
+    act = conv_out * sigmoid(conv_out)
+    x = act[:, :CH]
+    bm = act[:, CH : CH + STATE].astype(BF)
+    cm = act[:, CH + STATE :].astype(BF)
+    rate, dt_in, own, pick = own_heads(par, proj[:, CONVC:])
+    step = jnp.where(own, softplus(dt_in), 0.0)
+    cum = dot_exact(lower_tri(), -step * rate)
+    cum_t = cum.T
+    mask = (iota((BLK, BLK), 0) >= iota((BLK, BLK), 1)) & (tok[:, 0:1] == idr)
+    gm = jnp.where(mask, dot_nt(cm, bm), 0.0)
+    ex = spread()
+    xs = (x * split_dot(step, ex)).astype(BF)
+    parts = []
+    for pair in range(HPD // 2):
+        xp = xs[:, 128 * pair : 128 * pair + 128]
+        both = []
+        for h in (2 * pair, 2 * pair + 1):
+            decay = jnp.exp(jnp.minimum(cum[:, h : h + 1] - cum_t[h : h + 1, :], 0.0))
+            both.append(dot((gm * decay).astype(BF), xp))
+        parts.append(pair_select(*both))
+    inner = jnp.concatenate(parts, axis=1)
+    old = state[...]
+    st_ref[0] = old
+    keep = tok[:, 7:8]
+    carried = split_dot(keep * jnp.exp(cum), ex) * dot(cm, old.astype(BF))
+    last = cum[BLK - 1 : BLK, :]
+    weights = jnp.exp(last - cum) * step * tok[:, 8:9]
+    through = split_dot(jnp.broadcast_to(keep[BLK - 1 :, :] * jnp.exp(last), (8, 128)), ex)[0:1, :]
+    state[...] = dot_tn(bm, (x * split_dot(weights, ex)).astype(BF)) + through * old
+    ssd_v[rows, :] = inner + carried + par[6:7, :CH] * x
+
+
+def gate_forward(j, nrm_v, g_v, w_v, wo_v, par, ssd_v, projz_ref, ssd_ref, dno_ref, br_ref, stat_v):
+    rows = pl.ds(pl.multiple_of(BLK * j, BLK), BLK)
+    projz = dot_nt(nrm_v[rows, :], w_v[:NZ, :]).astype(BF)
+    projz_ref[...] = projz
+    ssd = ssd_v[rows, :]
+    ssd_ref[...] = ssd
+    z = projz.astype(F32)
+    gate_w = par[5:6, :CH]
+    gated = ssd * (z * sigmoid(z))
+    br_ref[...] = dot((gated * gate_w).astype(BF), wo_v[...]).astype(BF)
+    dno = dot_nt(g_v[rows, :], wo_v[...])
+    dno_ref[...] = dno
+    stat_v[pl.ds(j, 1), 0:BLK] = row_sum(gated * gated)
+    stat_v[pl.ds(j, 1), BLK : 2 * BLK] = row_sum(dno * gate_w * gated)
+
+
+def gate_backward(j, z, ssd, dno, stat, gate_w, not_v, dy_v, dz_v, dzt_v, small_v):
+    rows = pl.ds(pl.multiple_of(BLK * j, BLK), BLK)
+    sig_z = sigmoid(z)
+    silu_z = z * sig_z
+    stat = jnp.where(iota((128, BLK), 0) == 0, stat[:, :BLK], stat[:, BLK:]).T
+    s2 = lax.rsqrt(stat[:, 0:1] * (1.0 / DI) + EPSILON)
+    mean_ag = stat[:, 1:2] * (1.0 / DI)
+    gated = ssd * silu_z
+    gs = gated * s2
+    not_v[:, rows] = (gs * gate_w).T.astype(BF)
+    d_gated = s2 * (dno * gate_w) - gated * (s2 * s2 * s2 * mean_ag)
+    dy_v[rows, :] = d_gated * silu_z
+    dz = d_gated * ssd * sig_z * (1.0 + z * (1.0 - sig_z))
+    dz_v[rows, :] = dz.astype(BF)
+    dzt_v[:, rows] = dz.T.astype(BF)
+    small_v[5:6, :CH] += jnp.sum(dno * gs, axis=0, keepdims=True)
+
+
+def scan_backward(proj, halo, tok, idr, old, par, dy, cbuf, dcbuf, dstate, small_v):
+    cbuf[0:8, :] = halo[8:16, :CONVC].astype(F32)
+    cbuf[8 : 8 + BLK, :] = proj[:, :CONVC].astype(F32)
+    conv_out = conv_taps(cbuf, par, tok)
+    sig_c = sigmoid(conv_out)
+    act = conv_out * sig_c
+    x = act[:, :CH]
+    bm = act[:, CH : CH + STATE].astype(BF)
+    cm_f = act[:, CH + STATE :]
+    cm = cm_f.astype(BF)
+    rate, dt_in, own, pick = own_heads(par, proj[:, CONVC:])
+    step = jnp.where(own, softplus(dt_in), 0.0)
+    cum = dot_exact(lower_tri(), -step * rate)
+    cum_t = cum.T
+    mask = (iota((BLK, BLK), 0) >= iota((BLK, BLK), 1)) & (tok[:, 0:1] == idr)
+    gm = jnp.where(mask, dot_nt(cm, bm), 0.0)
+    ex = spread()
+    gh = gather_heads()
+    step_x = split_dot(step, ex)
+    xs = (x * step_x).astype(BF)
+    dyb = dy.astype(BF)
+    dyt = dy.T.astype(BF)
+    lane = iota((BLK, 128), 1)
+    dg = jnp.zeros((BLK, BLK), F32)
+    row_sums = jnp.zeros((BLK, 128), F32)
+    col_sums = []
+    e_rows = []
+    for h in range(HPD):
+        pair = h // 2
+        decay = jnp.exp(jnp.minimum(cum[:, h : h + 1] - cum_t[h : h + 1, :], 0.0))
+        mixed = gm * decay
+        half = jnp.where((lane < HEADDIM) == (h % 2 == 0), dyb[:, 128 * pair : 128 * pair + 128], 0)
+        dms = dot_nt(half.astype(BF), xs[:, 128 * pair : 128 * pair + 128])
+        product = dms * mixed
+        row_sums = jnp.where(lane == h, jnp.sum(product, axis=1, keepdims=True), row_sums)
+        col_sums.append(jnp.sum(product, axis=0, keepdims=True))
+        dg = dg + dms * decay
+        e_rows.append(dot(dyt[HEADDIM * h : HEADDIM * h + HEADDIM, :], mixed.astype(BF)))
+    dg = jnp.where(mask, dg, 0.0).astype(BF)
+    e = jnp.concatenate(e_rows, axis=0).T
+    col_sums.append(jnp.zeros((128 - HPD, BLK), F32))
+    col = jnp.concatenate(col_sums, axis=0).T
+    keep = tok[:, 7:8]
+    old_b = old.astype(BF)
+    dnew = dstate[...]
+    dnew_b = dnew.astype(BF)
+    carry_x = split_dot(keep * jnp.exp(cum), ex)
+    dyk_f = dy * carry_x
+    dyk = dyk_f.astype(BF)
+    carried = dot(cm, old_b)
+    last = cum[BLK - 1 : BLK, :]
+    fade = jnp.exp(last - cum) * tok[:, 8:9]
+    weights = fade * step
+    weights_x = split_dot(weights, ex)
+    zt = dot(bm, dnew_b)
+    xw = (x * weights_x).astype(BF)
+    through = keep[BLK - 1 :, :] * jnp.exp(last)
+    through_x = split_dot(jnp.broadcast_to(through, (8, 128)), ex)[0:1, :]
+    k_term = split_dot(dyk_f * carried, gh)
+    r_term = split_dot(x * zt, gh)
+    q_term = split_dot(x * e, gh)
+    pass_term = jnp.sum(old * dnew, axis=0, keepdims=True) * through_x
+    pass_h = split_dot(jnp.broadcast_to(pass_term, (8, CH)), gh)[0:1, :]
+    wr = weights * r_term
+    d_cum = row_sums - col + k_term - wr
+    d_last = jnp.sum(wr, axis=0, keepdims=True) + pass_h
+    d_cum = d_cum + jnp.where(iota((BLK, 128), 0) == BLK - 1, d_last, 0.0)
+    upper = (iota((BLK, BLK), 0) <= iota((BLK, BLK), 1)).astype(F32)
+    d_log = dot_exact(upper, d_cum)
+    d_step = q_term + fade * r_term - d_log * rate
+    d_a = -jnp.sum(d_log * step, axis=0, keepdims=True) * rate
+    d_dt = jnp.where(own, d_step * sigmoid(dt_in), 0.0)
+    heads = jnp.concatenate([d_a, jnp.sum(d_dt, axis=0, keepdims=True), jnp.zeros((6, 128), F32)], axis=0)
+    high = heads.astype(BF)
+    heads = dot_nt(high, pick) + dot_nt((heads - high.astype(F32)).astype(BF), pick)
+    d_dt = dot_nt(d_dt.astype(BF), pick)
+    dstate[...] = dot_tn(cm, dyk) + through_x * dnew
+    dx = step_x * e + weights_x * zt + par[6:7, :CH] * dy
+    dc = dot(dg, bm) + dot_nt(dyk, old_b)
+    db = dot(cm_f.T.astype(BF), dg).T + dot_nt(xw, dnew_b)
+    d_act = jnp.concatenate([dx, db, dc], axis=1)
+    d_conv = d_act * (sig_c * (1.0 + conv_out * (1.0 - sig_c)))
+    dcbuf[0:BLK, :] = d_conv
+    d_in = par[CONV - 1 : CONV, :] * d_conv
+    cg = [None] * CONV
+    cg[CONV - 1] = jnp.sum(d_conv * cbuf[8 : 8 + BLK, :], axis=0, keepdims=True)
+    for back in range(1, CONV):
+        tap = CONV - 1 - back
+        cg[tap] = jnp.sum(
+            d_conv * (cbuf[8 - back : 8 - back + BLK, :] * tok[:, back : back + 1]),
+            axis=0, keepdims=True,
+        )
+        d_in = d_in + par[tap : tap + 1, :] * (
+            dcbuf[back : back + BLK, :] * tok[:, 3 + back : 4 + back]
+        )
+    dcbuf[BLK : BLK + 8, :] = dcbuf[0:8, :]
+    small_v[0:CONV, :] += jnp.concatenate(cg, axis=0)
+    small_v[CONV : CONV + 1, :] += jnp.sum(d_conv, axis=0, keepdims=True)
+    small_v[5:6, CH:] += jnp.concatenate([heads[0:1, :], heads[1:2, :]], axis=1)
+    small_v[6:7, :CH] += jnp.sum(dy * x, axis=0, keepdims=True)
+    return jnp.concatenate([d_in, d_dt[:, :ND]], axis=1)
+
+
+def token_info(ids_full, first, n):
+    length = ids_full.shape[0]
+    pad = jnp.concatenate(
+        [jnp.full((8,), -1, jnp.int32), ids_full, jnp.full((8,), -2, jnp.int32)]
+    )
+    window = lax.dynamic_slice_in_dim(pad, first, n + 16)
+    own = window[8 : 8 + n]
+    blocks = own.reshape(-1, BLK)
+    before = window[7 : 7 + n].reshape(-1, BLK)[:, :1]
+    cols = [own]
+    for back in range(1, CONV):
+        cols.append((window[8 - back : 8 - back + n] == own))
+    for ahead in range(1, CONV):
+        cols.append((window[8 + ahead : 8 + ahead + n] == own))
+    cols.append((blocks == before).reshape(-1))
+    cols.append((blocks == blocks[:, -1:]).reshape(-1))
+    table = jnp.stack([c.astype(F32) for c in cols], axis=1)
+    tok = jnp.pad(table, ((0, 0), (0, 128 - table.shape[1])))
+    idr = jnp.broadcast_to(own.astype(F32).reshape(-1, 1, BLK), (n // BLK, 8, BLK))
+    return tok, idr
+
+
+CHIPS = TEAM // 2
+DEPTH = 4
+KROWS = D // DEPTH
+BCD = NB + ND
+HALF = BCD // 2
+
+
+def places():
+    seq = lax.axis_index("seq")
+    return seq, lax.div(seq, 2), lax.rem(seq, 2), lax.axis_index("fsdp")
+
+
+def send(src, dst, send_sem, recv_sem, device):
+    return pltpu.make_async_remote_copy(
+        src_ref=src, dst_ref=dst, send_sem=send_sem, recv_sem=recv_sem,
+        device_id=device, device_id_type=pl.DeviceIdType.MESH,
+    )
+
+
+def greet(devices):
+    barrier = pltpu.get_barrier_semaphore()
+    for device in devices:
+        pl.semaphore_signal(
+            barrier, inc=1, device_id=device, device_id_type=pl.DeviceIdType.MESH
+        )
+    pl.semaphore_wait(barrier, len(devices))
+
+
+def forward_kernel(
+    tok_ref, cot_ref, win_ref, bcd_ref, wout_ref, small_ref, info_ref, idr_ref,
+    nrm_ref, projc_ref, projz_ref, st_ref, ssd_ref, dno_ref, br_ref, stat_ref, par_ref, w_ref, g_ref,
+    u_v, g_v, w_v, wo_v, smalls, ssd_v, cbuf, state, stat_v, stat_in,
+    loc, t_send, t_recv, f_send, f_recv, z_send, z_recv, b_send, b_recv, s_send, s_recv, r_send, r_recv,
+):
+    i = pl.program_id(0)
+    seq, chip, core, z = places()
+    sib = {"seq": 2 * chip + 1 - core}
+    peer = lambda k: {"seq": 2 * lax.rem(chip + k, CHIPS) + core}
+    under = lambda k: {"fsdp": lax.rem(z + k, DEPTH)}
+    around = lambda k: {"seq": lax.rem(seq + k, TEAM)}
+    behind = lambda k: lax.rem(chip + CHIPS - k, CHIPS)
+    block = lambda s: pl.ds(pl.multiple_of(BLK * s, BLK), BLK)
+    lanes = lambda o: pl.ds(pl.multiple_of(KROWS * o, KROWS), KROWS)
+    half = pl.ds(pl.multiple_of(NZ + NX + HALF * core, 16), HALF)
+    has = [z < DEPTH - 1, z > 0]
+    heads = [head_of(n, chip, core)[n // 4] for n in range(HPD)]
+    piece = lambda n: pl.ds(pl.multiple_of(HEADDIM * n, HEADDIM), HEADDIM)
+
+    def token_copy(n, k):
+        src, dst = ((tok_ref, u_v), (cot_ref, g_v))[n]
+        return send(src, dst.at[block(seq)], t_send.at[n, k], t_recv.at[n, k], sib if k == 0 else peer(k))
+
+    def token_next(n, k):
+        ref = (u_v, g_v)[n].at[block(2 * behind(k) + core)]
+        return send(ref, ref, f_send.at[n, k], f_recv.at[n, k], sib)
+
+    def place(p, o):
+        if p < 3:
+            return w_v.at[(pl.ds(NZ, NX), half, pl.ds(0, NZ))[p], lanes(o)]
+        return wo_v.at[piece(o if p == 3 else DEPTH + lax.div(o, 2))]
+
+    def hop(p, side, dist):
+        o = z - dist if side == 0 else z + dist
+        there = {"fsdp": z + 1} if side == 0 else {"fsdp": z - 1}
+        return send(place(p, o), place(p, o), z_send.at[p, side, dist], z_recv.at[p, side, dist], there)
+
+    def got(p, side, dist):
+        o = z - dist - 1 if side == 0 else z + dist + 1
+        there = {"fsdp": z + 1} if side == 0 else {"fsdp": z - 1}
+        return send(place(p, o), place(p, o), z_send.at[p, side, dist], z_recv.at[p, side, dist], there)
+
+    def share(side, dist):
+        o = z - dist - 1 if side == 0 else z + dist + 1
+        return send(place(1, o), place(1, o), b_send.at[side, dist], b_recv.at[side, dist], sib)
+
+    def exists(p, side, hops):
+        o = z - hops if side == 0 else z + hops
+        there = (o >= 0) if side == 0 else (o < DEPTH)
+        return there & (lax.rem(o + DEPTH, 2) == core) if p == 4 else there
+
+    def small_copy(k):
+        return send(small_ref, smalls.at[z], s_send.at[k], s_recv.at[k], under(k))
+
+    def stat_copy(k):
+        return send(stat_v, stat_in.at[k], r_send.at[k], r_recv.at[k], around(k))
+
+    def local_copies():
+        pairs = [(tok_ref, u_v.at[block(seq)]), (cot_ref, g_v.at[block(seq)]), (small_ref, smalls.at[z])]
+        return [pltpu.make_async_copy(src, dst, loc.at[n]) for n, (src, dst) in enumerate(pairs)]
+
+    def own_weights():
+        pairs = [(bcd_ref, w_v.at[pl.ds(NZ + NX, BCD), lanes(z)], 3)]
+        for n in range(HPD):
+            row = HEADDIM * heads[n]
+            pairs.append((win_ref.at[pl.ds(pl.multiple_of(row, HEADDIM), HEADDIM)],
+                          w_v.at[piece(n), lanes(z)], 4 + n))
+            pairs.append((win_ref.at[pl.ds(pl.multiple_of(DI + row, HEADDIM), HEADDIM)],
+                          w_v.at[piece(HPD + n), lanes(z)], 10 + n))
+        pairs.append((wout_ref.at[piece(3 * chip + 2 * core)], place(3, z), 16))
+        return [pltpu.make_async_copy(src, dst, loc.at[n]) for src, dst, n in pairs]
+
+    def own_extra():
+        return pltpu.make_async_copy(wout_ref.at[piece(3 * chip + 1)], place(4, z), loc.at[17])
+
+    def pass_on(parts, dist):
+        for p in parts:
+            for side in range(2):
+
+                @pl.when(exists(p, side, dist + 1))
+                def _():
+                    got(p, side, dist).wait_recv()
+                    if p == 1:
+                        share(side, dist).start()
+
+                if dist < DEPTH - 2:
+
+                    @pl.when(exists(p, side, dist + 1) & has[side])
+                    def _():
+                        hop(p, side, dist + 1).start()
+
+    def start_own(parts):
+        for p in parts:
+            for side in range(2):
+
+                @pl.when(exists(p, side, 0) & has[side])
+                def _():
+                    hop(p, side, 0).start()
+
+    @pl.when(i == 0)
+    def _():
+        greet([around(k) for k in range(1, TEAM)] + [under(k) for k in range(1, DEPTH)])
+        for k in range(1, DEPTH):
+            small_copy(k).start()
+        for k in range(CHIPS):
+            token_copy(0, k).start()
+        for copy in own_weights() + local_copies():
+            copy.start()
+
+        @pl.when(lax.rem(z, 2) == core)
+        def _():
+            own_extra().start()
+
+        for copy in own_weights():
+            copy.wait()
+        start_own((0, 1))
+        state[...] = jnp.zeros_like(state)
+        cbuf[0:8, :] = jnp.zeros((8, CONVC), F32)
+        pass_on((0, 1), 0)
+        pass_on((0, 1), 1)
+        start_own((2,))
+        for k in range(1, CHIPS):
+            token_copy(0, k).wait_recv()
+            token_next(0, k).start()
+        for k in range(CHIPS):
+            token_copy(1, k).start()
+        pass_on((0, 1), 2)
+        token_copy(0, 0).wait_recv()
+        for k in range(1, CHIPS):
+            token_next(0, k).wait()
+        for k in range(1, DEPTH):
+            small_copy(k).wait()
+        for copy in local_copies():
+            copy.wait()
+        for side in range(2):
+            for dist in range(DEPTH - 1):
+
+                @pl.when(exists(1, side, dist + 1))
+                def _():
+                    share(side, dist).wait()
+
+        total = smalls[0].astype(F32)
+        for o in range(1, DEPTH):
+            total = total + smalls[o].astype(F32)
+        par_ref[...] = total
+
+    @pl.when(i == 1)
+    def _():
+        @pl.when(lax.rem(z, 2) == core)
+        def _():
+            own_extra().wait()
+
+        pass_on((2,), 0)
+        start_own((3, 4))
+
+    @pl.when(i == 3)
+    def _():
+        pass_on((2,), 1)
+
+    @pl.when(i == 5)
+    def _():
+        pass_on((3, 4), 0)
+
+    @pl.when(i == 7)
+    def _():
+        pass_on((3, 4), 1)
+
+    @pl.when(i == TEAM)
+    def _():
+        pass_on((2, 3, 4), 2)
+        for k in range(1, CHIPS):
+            token_copy(1, k).wait_recv()
+            token_next(1, k).start()
+        token_copy(1, 0).wait_recv()
+        for k in range(1, CHIPS):
+            token_next(1, k).wait()
+        pltpu.make_async_copy(w_v, w_ref, loc.at[18]).start()
+        pltpu.make_async_copy(g_v, g_ref, loc.at[19]).start()
+
+    par = par_ref[...]
+
+    @pl.when(i < TEAM)
+    def _():
+        u = u_v[block(i), :].astype(F32)
+        scale = lax.rsqrt(jnp.mean(u * u, axis=1, keepdims=True) + EPSILON)
+        nrm = (u * scale * norm_gain(par)).astype(BF)
+        nrm_ref[...] = nrm
+        u_v[block(i), :] = nrm
+        scan_forward(i, nrm, w_v, par, info_ref[...], idr_ref[0, 0:1, :], cbuf, state,
+                     projc_ref, st_ref, ssd_v)
+
+    @pl.when(i >= TEAM)
+    def _():
+        gate_forward(i - TEAM, u_v, g_v, w_v, wo_v, par, ssd_v, projz_ref, ssd_ref, dno_ref,
+                     br_ref, stat_v)
+
+    @pl.when(i == 2 * TEAM - 1)
+    def _():
+        for k in range(1, TEAM):
+            stat_copy(k).start()
+        total = stat_v[...]
+        for k in range(1, TEAM):
+            stat_copy(k).wait_recv()
+            total = total + stat_in[k]
+        stat_ref[...] = total
+        for k in range(1, TEAM):
+            stat_copy(k).wait_send()
+        for n in range(2):
+            for k in range(CHIPS):
+                token_copy(n, k).wait_send()
+        for side in range(2):
+            for dist in range(DEPTH - 1):
+                for p in range(5):
+
+                    @pl.when(exists(p, side, dist) & has[side])
+                    def _():
+                        hop(p, side, dist).wait_send()
+
+        pltpu.make_async_copy(w_v, w_ref, loc.at[18]).wait()
+        pltpu.make_async_copy(g_v, g_ref, loc.at[19]).wait()
+
+
+def forward_call(tok, cot, win, bcd, wout, small, info, idr):
+    n = tok.shape[0] * TEAM
+    any_space = pl.BlockSpec(memory_space=pl.ANY)
+    sds = jax.ShapeDtypeStruct
+    dma = pltpu.SemaphoreType.DMA
+    one = lambda i: jnp.minimum(i, TEAM - 1)
+    two = lambda i: jnp.maximum(i - TEAM, 0)
+    rows = lambda c, turn: pl.BlockSpec((BLK, c), lambda i: (turn(i), 0))
+    cube = lambda a, b: pl.BlockSpec((1, a, b), lambda i: (one(i), 0, 0))
+    fixed = lambda a, b: pl.BlockSpec((a, b), lambda i: (0, 0))
+    return pl.pallas_call(
+        forward_kernel,
+        grid=(2 * TEAM,),
+        in_specs=[any_space] * 6 + [rows(128, one), cube(8, BLK)],
+        out_specs=[rows(D, one), rows(REST, one), rows(NZ, two), cube(STATE, CH), rows(CH, two),
+                   rows(CH, two), rows(D, two), fixed(TEAM, 2 * BLK), fixed(16, CONVC), any_space,
+                   any_space],
+        out_shape=[sds((n, D), BF), sds((n, REST), BF), sds((n, NZ), BF), sds((TEAM, STATE, CH), F32),
+                   sds((n, CH), F32), sds((n, CH), F32), sds((n, D), BF), sds((TEAM, 2 * BLK), F32),
+                   sds((16, CONVC), F32), sds((COLS, D), BF), sds((n, D), BF)],
+        scratch_shapes=[pltpu.VMEM((n, D), BF), pltpu.VMEM((n, D), BF), pltpu.VMEM((COLS, D), BF),
+                        pltpu.VMEM((CH, D), BF), pltpu.VMEM((DEPTH, 16, CONVC), BF),
+                        pltpu.VMEM((n, CH), F32), pltpu.VMEM((BLK + 8, CONVC), F32),
+                        pltpu.VMEM((STATE, CH), F32), pltpu.VMEM((TEAM, 2 * BLK), F32),
+                        pltpu.VMEM((TEAM, TEAM, 2 * BLK), F32),
+                        dma((20,)), dma((2, CHIPS)), dma((2, CHIPS)), dma((2, CHIPS)),
+                        dma((2, CHIPS)), dma((5, 2, DEPTH - 1)), dma((5, 2, DEPTH - 1)),
+                        dma((2, DEPTH - 1)), dma((2, DEPTH - 1)),
+                        dma((DEPTH,)), dma((DEPTH,)), dma((TEAM,)), dma((TEAM,))],
+        compiler_params=pltpu.CompilerParams(
+            collective_id=0, has_side_effects=True, vmem_limit_bytes=60 << 20),
+    )(tok, cot, win, bcd, wout, small, info, idr)
+
+
+def backward_kernel(
+    tok_ref, cot_ref, nrm_ref, br_ref, w_ref, g_ref,
+    projz_ref, ssd_ref, dno_ref, stat_ref, par_ref, projc_ref, halo_ref, st_ref, info_ref, idr_ref,
+    out_ref, tg_ref, wig_ref, wog_ref, smalls_ref,
+    nrm_v, g_v, w_v, not_v, dz_v, dzt_v, dy_v, rest_v, wig_v, wog_v, bcd_v, bcd_in,
+    zz_in, zx_in, zb_in, zw_in, zs_in, gz_v, gx_v, gb_v, gw_v, gb_in, gt_v, ob_v, rb_v, rr_v, rd_v,
+    tok_v, cot_v, small_v, small_s, cbuf, dcbuf, dstate,
+    loc, b_send, b_recv, p_send, p_recv, d_send, d_recv, q_send, q_recv, z_send, z_recv,
+    a_send, a_recv, f_send, f_recv, h_send, h_recv, free,
+):
+    i = pl.program_id(0)
+    seq, chip, core, z = places()
+    sib = {"seq": 2 * chip + 1 - core}
+    peer = lambda k: {"seq": 2 * lax.rem(chip + k, CHIPS) + core}
+    under = lambda k: {"fsdp": lax.rem(z + k, DEPTH)}
+    around = lambda k: {"seq": lax.rem(seq + k, TEAM)}
+    behind = lambda k: lax.rem(chip + CHIPS - k, CHIPS)
+    block = lambda s: pl.ds(pl.multiple_of(BLK * s, BLK), BLK)
+    lanes = lambda o: pl.ds(pl.multiple_of(KROWS * o, KROWS), KROWS)
+    piece = lambda n: pl.ds(pl.multiple_of(HEADDIM * n, HEADDIM), HEADDIM)
+    half = lambda c: pl.ds(pl.multiple_of(HALF * c, 16), HALF)
+    extra = lambda o: lax.rem(o, 2) == core
+    n_all = HEADDIM * HPD
+    give = lambda c: g_v.at[block(c)]
+    hold = lambda c: g_v.at[block(CHIPS + c)]
+
+    def load(n):
+        pairs = [(nrm_ref, nrm_v), (g_ref, g_v), (w_ref, w_v), (tok_ref, tok_v), (cot_ref, cot_v)]
+        return pltpu.make_async_copy(pairs[n][0], pairs[n][1], loc.at[n])
+
+    def load_own(c):
+        return pltpu.make_async_copy(br_ref.at[block(2 * c + core)], ob_v.at[c], loc.at[5 + c])
+
+    def br_pair(c):
+        return send(br_ref.at[block(2 * c + 1 - core)], rb_v.at[c], b_send.at[c], b_recv.at[c], sib)
+
+    def br_push(k):
+        return send(ob_v.at[lax.rem(chip + k, CHIPS)], rr_v.at[k - 1], p_send.at[k], p_recv.at[k], peer(k))
+
+    def dn_pair(c):
+        return send(give(c), rb_v.at[c], d_send.at[c], d_recv.at[c], sib)
+
+    def dn_push(c):
+        k = lax.rem(c + CHIPS - chip, CHIPS)
+        return send(hold(c), rd_v.at[k - 1], q_send.at[k], q_recv.at[k], {"seq": 2 * c + core})
+
+    def dn_pushed(k):
+        return send(hold(0), rd_v.at[k - 1], q_send.at[k], q_recv.at[k], peer(k))
+
+    def down(n, k):
+        o = lax.rem(z + k, DEPTH)
+        src, dst = [
+            (wig_v.at[:, lanes(o)], zz_in.at[k - 1]),
+            (wig_v.at[:, lanes(o)], zx_in.at[k - 1]),
+            (bcd_v.at[half(core), lanes(o)], zb_in.at[k - 1]),
+            (wog_v.at[piece(o)], zw_in.at[k - 1, 0:HEADDIM]),
+            (wog_v.at[piece(DEPTH + lax.div(o, 2))], zw_in.at[k - 1, HEADDIM:]),
+            (small_v, zs_in.at[k - 1]),
+        ][n]
+        return send(src, dst, z_send.at[n, k], z_recv.at[n, k], under(k))
+
+    def bcd_pair():
+        return send(bcd_v.at[half(1 - core)], bcd_in, h_send.at[0], h_recv.at[0], sib)
+
+    def bcd_push(k):
+        return send(gb_v, gb_in.at[k - 1], a_send.at[4, k], a_recv.at[4, k], peer(k))
+
+    def bcd_back():
+        return send(gt_v.at[core], gt_v.at[core], h_send.at[1], h_recv.at[1], sib)
+
+    def parts(n, c, cr):
+        if n < 2:
+            base = n * DI // HEADDIM
+            src = (gz_v, gx_v)[n]
+            return [(src.at[piece(s)], wig_ref.at[piece(base + head_of(s, c, cr)[s // 4])]) for s in range(HPD)]
+        if n == 2:
+            return [(gw_v.at[0:HEADDIM], wog_ref.at[piece(3 * c + 2 * cr)])]
+        if n == 3:
+            return [(gw_v.at[HEADDIM:], wog_ref.at[piece(3 * c + 1)])]
+        return [(small_s, smalls_ref.at[2 * c + cr])]
+
+    def all_of(n):
+        if n < 2:
+            return wig_ref.at[pl.ds(n * DI, n_all)]
+        return parts(n, 0, 0)[0][1]
+
+    def ag(n, k):
+        where = sib if k == 0 else peer(k)
+        return [send(src, dst, a_send.at[n, k], a_recv.at[n, k], where) for src, dst in parts(n, chip, core)]
+
+    def ag_wait(n, k):
+        return send(all_of(n), all_of(n), a_send.at[n, k], a_recv.at[n, k], sib)
+
+    def ag_next(n, k):
+        return [send(dst, dst, f_send.at[n, k], f_recv.at[n, k], sib) for _, dst in parts(n, behind(k), core)]
+
+    def ag_next_wait(n, k):
+        return send(all_of(n), all_of(n), f_send.at[n, k], f_recv.at[n, k], sib)
+
+    def ag_own(n):
+        return [pltpu.make_async_copy(src, dst, loc.at[9 + n]) for src, dst in parts(n, chip, core)]
+
+    def ag_own_wait(n):
+        return pltpu.make_async_copy(all_of(n), all_of(n), loc.at[9 + n])
+
+    def ag_start(n):
+        for k in range(1, CHIPS):
+            for copy in ag(n, k):
+                copy.start()
+        for copy in ag(n, 0) + ag_own(n):
+            copy.start()
+
+    def ag_forward(n):
+        for k in range(1, CHIPS):
+            ag_wait(n, k).wait_recv()
+            for copy in ag_next(n, k):
+                copy.start()
+
+    def ag_finish(n):
+        ag_wait(n, 0).wait_recv()
+        for k in range(CHIPS):
+            ag_wait(n, k).wait_send()
+        for k in range(1, CHIPS):
+            ag_next_wait(n, k).wait()
+        ag_own_wait(n).wait()
+
+    def reduce_z(own, arrived):
+        total = own.astype(F32)
+        for k in range(1, DEPTH):
+            total = total + arrived[k - 1].astype(F32)
+        return total
+
+    @pl.when(i == 0)
+    def _():
+        greet([around(k) for k in range(1, TEAM)] + [under(k) for k in range(1, DEPTH)])
+        for c in range(CHIPS):
+            br_pair(c).start()
+            load_own(c).start()
+        for n in range(5):
+            load(n).start()
+        small_v[...] = jnp.zeros_like(small_v)
+        dstate[...] = jnp.zeros_like(dstate)
+        dcbuf[BLK : BLK + 8, :] = jnp.zeros((8, CONVC), F32)
+
+    @pl.when(i < TEAM)
+    def _():
+        gate_backward(i, projz_ref[...].astype(F32), ssd_ref[...], dno_ref[...],
+                      stat_ref[pl.ds(i, 1), :], par_ref[5:6, :CH], not_v, dy_v, dz_v, dzt_v, small_v)
+
+    @pl.when(i == 1)
+    def _():
+        for c in range(CHIPS):
+            load_own(c).wait()
+            br_pair(c).wait_recv()
+            ob_v[c] = (ob_v[c].astype(F32) + rb_v[c].astype(F32)).astype(BF)
+        for k in range(1, CHIPS):
+            br_push(k).start()
+        pl.semaphore_signal(free, inc=1, device_id=sib, device_id_type=pl.DeviceIdType.MESH)
+
+    @pl.when(i == TEAM)
+    def _():
+        pl.semaphore_wait(free, 1)
+        for n in range(5):
+            load(n).wait()
+
+        @pl.loop(0, D // 256)
+        def _(n):
+            cols = pl.ds(pl.multiple_of(256 * n, 256), 256)
+            wig_v[:, cols] = dot(dzt_v[...], nrm_v[:, cols]).astype(BF)
+
+        for k in range(1, DEPTH):
+            down(0, k).start()
+
+        @pl.loop(0, D // 256)
+        def _(n):
+            cols = pl.ds(pl.multiple_of(256 * n, 256), 256)
+            wog_v[:, cols] = dot(not_v[...], g_v[:, cols]).astype(BF)
+
+        for k in range(1, DEPTH):
+            down(3, k).start()
+
+            @pl.when(extra(z + k))
+            def _():
+                down(4, k).start()
+
+    def combine(c):
+        dn_pair(c).wait_recv()
+        hold(c)[...] = (hold(c)[...].astype(F32) + rb_v[c].astype(F32)).astype(BF)
+
+        @pl.when(chip != c)
+        def _():
+            dn_push(c).start()
+
+    for c in range(CHIPS - 1, 0, -1):
+
+        @pl.when(i == TEAM + 1 + 2 * (CHIPS - c))
+        def _():
+            combine(c)
+
+    @pl.when((i > TEAM) & (i <= 2 * TEAM))
+    def _():
+        j = 2 * TEAM - i
+        rows = block(j)
+        d_rest = scan_backward(projc_ref[...], halo_ref[...], info_ref[...], idr_ref[0, 0:1, :], st_ref[0],
+                               par_ref[...], dy_v[rows, :], cbuf, dcbuf, dstate, small_v)
+        rest_v[:, rows] = d_rest.T.astype(BF)
+        dn = dot(dz_v[rows, :], w_v[:NZ, :]) + dot(d_rest.astype(BF), w_v[NZ:, :])
+        part = jnp.sum(dn * nrm_v[rows, :].astype(F32), axis=0, keepdims=True)
+        for n in range(3):
+            small_v[7 + n : 8 + n, :512] += part[:, 512 * n : 512 * n + 512]
+        dn = dn.astype(BF)
+        c = lax.div(j, 2)
+
+        @pl.when(lax.rem(j, 2) == core)
+        def _():
+            hold(c)[...] = dn
+
+        @pl.when(lax.rem(j, 2) != core)
+        def _():
+            give(c)[...] = dn
+            dn_pair(c).start()
+
+    @pl.when(i == 2 * TEAM - 1)
+    def _():
+        for k in range(1, CHIPS):
+            br_push(k).wait_recv()
+        total = ob_v[chip].astype(F32)
+        for k in range(1, CHIPS):
+            total = total + rr_v[k - 1].astype(F32)
+        stat = stat_ref[pl.ds(seq, 1), 0:BLK]
+        stat = jnp.broadcast_to(stat, (128, BLK)).T
+        s2 = lax.rsqrt(stat[:, 0:1] * (1.0 / DI) + EPSILON)
+        out_ref[...] = (tok_v[...].astype(F32) + total * s2).astype(BF)
+
+    @pl.when(i == 2 * TEAM)
+    def _():
+        for k in range(1, DEPTH):
+            down(0, k).wait_recv()
+        gz_v[...] = reduce_z(wig_v[:, lanes(z)], [zz_in[k - 1] for k in range(1, DEPTH)]).astype(BF)
+        ag_start(0)
+
+    @pl.when(i == 2 * TEAM + 1)
+    def _():
+        for n in range(3):
+            small_v[7 + n : 8 + n, :512] = small_v[7 + n : 8 + n, :512] / par_ref[7 + n : 8 + n, :512]
+        for k in range(1, DEPTH):
+            down(5, k).start()
+        combine(0)
+
+        @pl.loop(0, D // 256)
+        def _(n):
+            cols = pl.ds(pl.multiple_of(256 * n, 256), 256)
+            bcd_v[:, cols] = dot(rest_v[NX:, :], nrm_v[:, cols]).astype(BF)
+
+        bcd_pair().start()
+        for k in range(1, DEPTH):
+            down(0, k).wait_send()
+
+        @pl.loop(0, D // 256)
+        def _(n):
+            cols = pl.ds(pl.multiple_of(256 * n, 256), 256)
+            wig_v[:, cols] = dot(rest_v[:NX, :], nrm_v[:, cols]).astype(BF)
+
+        for k in range(1, DEPTH):
+            down(1, k).start()
+        bcd_pair().wait_recv()
+        bcd_v[half(core), :] = (bcd_v[half(core), :].astype(F32) + bcd_in[...].astype(F32)).astype(BF)
+        for k in range(1, DEPTH):
+            down(2, k).start()
+        for k in range(1, DEPTH):
+            down(3, k).wait_recv()
+        gw_v[0:HEADDIM, :] = reduce_z(wog_v[piece(z), :], [zw_in[k - 1, 0:HEADDIM] for k in range(1, DEPTH)]).astype(BF)
+        ag_start(2)
+
+        @pl.when(extra(z))
+        def _():
+            for k in range(1, DEPTH):
+                down(4, k).wait_recv()
+            gw_v[HEADDIM:, :] = reduce_z(
+                wog_v[piece(DEPTH + lax.div(z, 2)), :], [zw_in[k - 1, HEADDIM:] for k in range(1, DEPTH)]).astype(BF)
+            ag_start(3)
+
+        for k in range(1, DEPTH):
+            down(5, k).wait_recv()
+        small_s[...] = reduce_z(small_v[...], [zs_in[k - 1] for k in range(1, DEPTH)])
+        ag_start(5)
+        ag_forward(0)
+        for k in range(1, CHIPS):
+            dn_pushed(k).wait_recv()
+        total = hold(chip)[...].astype(F32)
+        for k in range(1, CHIPS):
+            total = total + rd_v[k - 1].astype(F32)
+        uf = tok_v[...].astype(F32)
+        along = total * norm_gain(par_ref[...])
+        s1 = lax.rsqrt(jnp.mean(uf * uf, axis=1, keepdims=True) + EPSILON)
+        tg_ref[...] = cot_v[...].astype(F32) + s1 * along - uf * (
+            s1 * s1 * s1 * jnp.mean(along * uf, axis=1, keepdims=True))
+        for k in range(1, DEPTH):
+            down(1, k).wait_recv()
+        gx_v[...] = reduce_z(wig_v[:, lanes(z)], [zx_in[k - 1] for k in range(1, DEPTH)]).astype(BF)
+        ag_start(1)
+        for k in range(1, DEPTH):
+            down(2, k).wait_recv()
+        gb_v[...] = reduce_z(bcd_v[half(core), lanes(z)], [zb_in[k - 1] for k in range(1, DEPTH)]).astype(BF)
+        for k in range(1, CHIPS):
+            bcd_push(k).start()
+        ag_forward(2)
+
+        @pl.when(extra(z))
+        def _():
+            ag_forward(3)
+
+        ag_forward(5)
+        for k in range(1, CHIPS):
+            bcd_push(k).wait_recv()
+        total = gb_v[...].astype(F32)
+        for k in range(1, CHIPS):
+            total = total + gb_in[k - 1].astype(F32)
+        gt_v[core] = total.astype(BF)
+        bcd_back().start()
+        ag_forward(1)
+        bcd_back().wait()
+        last = [
+            pltpu.make_async_copy(gt_v.at[0], wig_ref.at[pl.ds(2 * DI, HALF)], loc.at[15]),
+            pltpu.make_async_copy(gt_v.at[1, 0 : WIDTH - 2 * DI - HALF],
+                                  wig_ref.at[pl.ds(2 * DI + HALF, WIDTH - 2 * DI - HALF)], loc.at[16])]
+        for copy in last:
+            copy.start()
+        for n in (0, 1, 2, 5):
+            ag_finish(n)
+
+        @pl.when(extra(z))
+        def _():
+            for k in range(CHIPS):
+                ag_wait(3, k).wait_send()
+            for k in range(1, CHIPS):
+                ag_next_wait(3, k).wait_send()
+            ag_own_wait(3).wait()
+
+        @pl.when(jnp.logical_not(extra(z)))
+        def _():
+            ag_wait(3, 0).wait_recv()
+            for k in range(1, CHIPS):
+                ag_next_wait(3, k).wait_recv()
+
+        for c in range(CHIPS):
+            br_pair(c).wait_send()
+            dn_pair(c).wait_send()
+        for k in range(1, CHIPS):
+            br_push(k).wait_send()
+            dn_pushed(k).wait_send()
+            bcd_push(k).wait_send()
+        for k in range(1, DEPTH):
+            for n in (1, 2, 3, 5):
+                down(n, k).wait_send()
+
+            @pl.when(extra(z + k))
+            def _():
+                down(4, k).wait_send()
+
+        bcd_pair().wait_send()
+        for copy in last:
+            copy.wait()
+
+
+def backward_call(tok, cot, nrm, br, w, g, projz, ssd, dno, stat, par, projc, st, info, idr):
+    n = nrm.shape[0]
+    any_space = pl.BlockSpec(memory_space=pl.ANY)
+    sds = jax.ShapeDtypeStruct
+    dma = pltpu.SemaphoreType.DMA
+    one = lambda i: jnp.minimum(i, TEAM - 1)
+    two = lambda i: jnp.clip(2 * TEAM - i, 0, TEAM - 1)
+    rows = lambda c, turn: pl.BlockSpec((BLK, c), lambda i: (turn(i), 0))
+    cube = lambda a, b: pl.BlockSpec((1, a, b), lambda i: (two(i), 0, 0))
+    fixed = lambda a, b: pl.BlockSpec((a, b), lambda i: (0, 0), pipeline_mode=pl.Buffered(1))
+    vm = pltpu.VMEM
+    return pl.pallas_call(
+        backward_kernel,
+        grid=(2 * TEAM + 2,),
+        in_specs=[any_space] * 6 + [
+            rows(NZ, one), rows(CH, one), rows(CH, one), fixed(TEAM, 2 * BLK), fixed(16, CONVC), rows(REST, two),
+            pl.BlockSpec((16, REST), lambda i: (jnp.maximum(16 * two(i) - 1, 0), 0)),
+            cube(STATE, CH), rows(128, two), cube(8, BLK)],
+        out_specs=[fixed(BLK, D), fixed(BLK, D), any_space, any_space, any_space],
+        out_shape=[sds((BLK, D), BF), sds((BLK, D), F32), sds((WIDTH, KROWS), BF),
+                   sds((DI // DEPTH, D), BF), sds((TEAM, 16, CONVC), F32)],
+        scratch_shapes=[
+            vm((n, D), BF), vm((n, D), BF), vm((COLS, D), BF), vm((CH, n), BF), vm((n, CH), BF), vm((CH, n), BF),
+            vm((n, CH), F32), vm((REST, n), BF), vm((CH, D), BF), vm((CH, D), BF), vm((BCD, D), BF),
+            vm((HALF, D), BF),
+            vm((DEPTH - 1, CH, KROWS), BF), vm((DEPTH - 1, CH, KROWS), BF), vm((DEPTH - 1, HALF, KROWS), BF),
+            vm((DEPTH - 1, 2 * HEADDIM, D), BF), vm((DEPTH - 1, 16, CONVC), F32), vm((CH, KROWS), BF), vm((CH, KROWS), BF),
+            vm((HALF, KROWS), BF), vm((2 * HEADDIM, D), BF), vm((CHIPS - 1, HALF, KROWS), BF), vm((2, HALF, KROWS), BF),
+            vm((CHIPS, BLK, D), BF), vm((CHIPS, BLK, D), BF), vm((CHIPS - 1, BLK, D), BF), vm((CHIPS - 1, BLK, D), BF),
+            vm((BLK, D), BF), vm((BLK, D), BF), vm((16, CONVC), F32), vm((16, CONVC), F32),
+            vm((BLK + 8, CONVC), F32), vm((BLK + 8, CONVC), F32), vm((STATE, CH), F32),
+            dma((17,)), dma((CHIPS,)), dma((CHIPS,)), dma((CHIPS,)), dma((CHIPS,)), dma((CHIPS,)), dma((CHIPS,)),
+            dma((CHIPS,)), dma((CHIPS,)), dma((6, DEPTH)), dma((6, DEPTH)),
+            dma((6, CHIPS)), dma((6, CHIPS)), dma((6, CHIPS)), dma((6, CHIPS)), dma((2,)), dma((2,)),
+            pltpu.SemaphoreType.REGULAR],
+        compiler_params=pltpu.CompilerParams(
+            collective_id=1, has_side_effects=True, vmem_limit_bytes=63 << 20),
+    )(tok, cot, nrm, br, w, g, projz, ssd, dno, stat, par, projc, projc, st, info, idr)
+
+
+def on_team(
+    tokens, segment_ids, cotangent, w_in, w_out, conv_w, conv_b, a_log, dt_bias, d_skip,
+    norm_w, gate_w,
+):
+    place = lax.axis_index("seq")
+    chip, core = place // 2, place % 2
+    depth = lax.axis_index("fsdp")
+    shards = DEPTH
+    n = tokens.shape[1] * TEAM
+    w_t = w_in.T
+    bcd = jnp.pad(w_t[2 * DI :], ((0, BCD - (WIDTH - 2 * DI)), (0, 0)))
+
+    def put(a, whole_size):
+        return lax.dynamic_update_slice_in_dim(
+            jnp.zeros(a.shape[:-1] + (whole_size,), BF), a, depth * a.shape[-1], a.ndim - 1)
+
+    def own_part(a):
+        a = a.reshape(a.shape[0], 4, 12, HEADDIM)
+        a = lax.dynamic_slice_in_dim(a, 3 * chip, 3, 2)
+        first = lax.dynamic_index_in_dim(a, 2 * core, 2, keepdims=False)
+        second = a[:, :, 1].reshape(-1, 2, 2, HEADDIM)
+        second = lax.dynamic_index_in_dim(second, core, 2, keepdims=False)
+        return jnp.concatenate([first, second], axis=1).reshape(a.shape[0], CH)
+
+    wide = lambda a, size: jnp.pad(a, (0, size - a.shape[0]))
+    conv_rows = put(jnp.concatenate([conv_w, conv_b[None]], axis=0), CHAN)
+    chan_rows = own_part(jnp.concatenate(
+        [conv_rows[:, :DI], put(gate_w, DI)[None], jnp.repeat(put(d_skip, HEADS), HEADDIM)[None]], axis=0))
+    heads_row = jnp.concatenate([wide(put(dt_bias, HEADS), 128), wide(put(a_log, HEADS), 128)])
+    side = jnp.concatenate([conv_rows[:, DI:], heads_row[None], jnp.zeros((1, NB), BF)], axis=0)
+    gain_rows = jnp.pad(put(norm_w, D).reshape(3, D // 3), ((0, 0), (0, CONVC - D // 3)))
+    small = jnp.concatenate(
+        [jnp.concatenate([chan_rows, side], axis=1), gain_rows, jnp.zeros((6, CONVC), BF)], axis=0)
+    tok, idr = token_info(segment_ids[0], 0, n)
+    u_own, g_own = tokens[0], cotangent[0]
+    nrm, projc, projz, st, ssd, dno, br, stat, par, w_loc, g = forward_call(
+        u_own, g_own, w_t, bcd, w_out, small, tok, idr)
+    layer_out, token_grad, wig, wog, smalls = backward_call(
+        u_own, g_own, nrm, br, w_loc, g, projz, ssd, dno, stat, par, projc, st, tok, idr)
+    w_in_grad = wig.astype(F32).T
+    w_out_grad = wog.astype(F32)
+    parts = smalls[:, :7, :CH].reshape(CHIPS, 2, 7, HPD, HEADDIM)
+    first = parts[:, :, :, :4].transpose(1, 2, 3, 0, 4)
+    second = parts[:, :, :, 4:].transpose(2, 3, 1, 0, 4).reshape(7, 4, CHIPS, HEADDIM)
+    chang = jnp.stack([first[0], second, first[1]], axis=3).reshape(7, DI)
+    sideg = jnp.sum(smalls[:, :6, CH:], axis=0)
+    normg = jnp.sum(smalls[:, 7:10, :512], axis=0).reshape(D)
+    convg = jnp.concatenate([chang[:5], sideg[:5]], axis=1)
+    mine = lambda a: lax.dynamic_slice_in_dim(a, depth * (a.shape[-1] // shards), a.shape[-1] // shards, a.ndim - 1)
+    convg = mine(convg)
+    skipg = jnp.sum(chang[6].reshape(HEADS, HEADDIM), axis=1)
+    return (layer_out[None], token_grad[None], w_in_grad, w_out_grad, convg[:4], convg[4],
+            mine(sideg[5, :HEADS]), mine(sideg[5, 128 : 128 + HEADS]), mine(skipg), mine(normg), mine(chang[5]))
+
+
 def solution(mesh):
+    body = on_team if (mesh.shape["seq"], mesh.shape["fsdp"]) == (TEAM, DEPTH) else on_device
     return jax.shard_map(
-        on_device,
+        body,
         mesh=mesh,
         in_specs=(
             P("fsdp", "seq", None),

time: 1860 us -> 303 us (0.16)
  waiting for transfers between devices: 1240 us -> 0 us
  Pallas kernels: 0 us -> 265 us
  matrix products: 158 us -> 0 us
  blocking collectives: 134 us -> 0 us
  other arithmetic: 131 us -> 14.4 us
  starting transfers between devices: 88.2 us -> 0 us
  local copies, waits for them, and re-layouts: 79.6 us -> 19.8 us
  between operations: 19.7 us -> 0.98 us
    reduce_scatter x2 -> x0, waiting for transfers between devices: 662 us -> none  [the longest x1 662 us: on_device(): lax.psum_scatter(weight_grads[0], 'fsdp', scatter_dimension=0, tiled=True)]
    pallas_call x0 -> x2, Pallas kernels: none -> 265 us  [the longest x1 157 us: backward_call(): pl.pallas_call(backward_kernel, grid=(2 * TEAM + 2,), in_specs=[any_space...]
    all_gather x2 -> x0, waiting for transfers between devices: 244 us -> none  [the longest x1 244 us: on_device(): lax.all_gather(w_in, 'fsdp', axis=0, tiled=True)]
    psum x1 -> x0, waiting for transfers between devices: 172 us -> none  [on_device(): totals = lax.psum(shares, 'seq')]
    ppermute x16 -> x0, waiting for transfers between devices: 161 us -> none  [passed_along(): lax.ppermute(value, axis, [(source, source + steps) for source in range(f...]
    dot_general x18 -> x0, matrix products: 158 us -> none  [the longest x3 54.4 us: local_output(): jnp.einsum('chts,cshp->cthp', mixing, x_heads, precision=HIGHEST)]
    ppermute x16 -> x0, starting transfers between devices: 87.9 us -> none  [passed_along(): lax.ppermute(value, axis, [(source, source + steps) for source in range(f...]
    all_gather x3 -> x0, blocking collectives: 57 us -> none  [the longest x1 30.3 us: on_device(): lax.all_gather(gate_w, 'fsdp', axis=0, tiled=True)]
  transfers between devices with their start and end apart: 22 -> 0, of which waited for: 18 -> 0; matrix products, arithmetic and copies ran while one was open for 19% -> 0% of each run, Pallas kernels for 0% -> 0%
where the time goes in v2:
time: 303 us; the launch traced here: 300 us
  Pallas kernels  265 us (87%)
  local copies, waits for them, and re-layouts  19.8 us (7%)
  other arithmetic  14.4 us (5%)
    pallas_call x1, Pallas kernels, backward_call(): pl.pallas_call(backward_kernel, grid=(2 * TEAM + 2,), in_specs=[any_space...  157 us
    pallas_call x1, Pallas kernels, forward_call(): pl.pallas_call(forward_kernel, grid=(2 * TEAM,), in_specs=[any_space] * 6...  108 us

profile of v2, /device:TPU:0, one launch (start us, length us, event | category | flops | bytes accessed | tf_op | source)
XLA Modules:
  0.0 299.9 jit_solution(15802746183642866911)
XLA Ops:
  0.7 0.9 dynamic_update_slice.22
  1.6 0.8 dynamic_update_slice.23
  2.4 0.1 pad.40.clone
  2.5 0.8 dynamic_update_slice.21
  3.4 0.1 broadcast_in_dim.44
  3.4 0.7 broadcast_in_dim.41
  4.1 0.9 dynamic_update_slice.24
  5.0 0.8 pad_slice_fusion.5
  5.8 0.1 slice_reduce_fusion.2
  5.9 0.1 broadcast_bitcast_fusion.1
  6.0 0.7 pad_maximum_fusion.3
  6.7 0.7 reshape_dynamic-update-slice_fusion
  7.5 0.1 concatenate.42
  7.6 0.1 broadcast_in_dim.45
  7.6 0.5 broadcast.48
  8.2 1.4 fusion.19
  9.5 0.1 slice.125
  9.6 0.1 copy.74
  9.7 0.1 broadcast_bitcast_fusion
  9.8 0.7 compare_convert_fusion
  10.5 1.0 fusion.10
  11.6 0.3 dynamic_update_slice.19
  11.9 0.1 concatenate.41
  12.2 0.1 reshape.119
  12.3 0.7 fusion.4.small_ref
  13.0 0.6 broadcast_in_dim.50.idr_ref
  13.6 0.1 stack.57
  13.7 1.0 slice.121
  14.7 0.7 pad.25.bcd_ref
  15.4 0.4 copy.63
  15.8 1.0 pad.29.info_ref
  16.8 108.1 %shard_map.203 = (bf16[2048,1536]{1,0:T(8,128)(2,1)}, bf16[2048,704]{1,0:T(8,128)(2,1)}, bf16[2048,384]{1,0:T(8,128)(2,1)}, f32[8,128,384]{2,1,0:T(8,128)}, f32[...) custom-call(bf16[256,1536]{1,0:T(8,128)(2,1)} %bitcast.56, ...), custom_call_target="tpu_custom_call" | custom-call | tf_op jit(solution)/shard_map/pallas_call | solution.py:845
  125.0 156.6 %shard_map.204 = (bf16[256,1536]{1,0:T(8,128)(2,1)}, f32[256,1536]{1,0:T(8,128)}, bf16[6448,384]{1,0:T(8,128)(2,1)}, bf16[768,1536]{1,0:T(8,128)(2,1)}, f32[8,16,640]{2,1,0:T(8,128)}) custom-call(bf16[256,1536]{1,0:T(8,128)(2,1)} %bitcast.57, bf16[256,1536]{1,0:T(8,128)(2,1)} %bitcast.59, bf16[2048,1536]{1,0:T(8,128)(2,1)} %get-tuple-element.27.nrm_ref, ...), custom_call_target="tpu_custom_call" | custom-call | tf_op jit(solution)/shard_map/pallas_call | solution.py:1245
  281.6 0.0 copy-start.1
  281.6 1.0 slice_reduce_fusion.1
  282.6 0.6 fusion.16
  283.2 1.0 slice_reduce_fusion
  284.2 0.9 slice.105
  285.1 0.7 dynamic_slice.46
  285.7 0.1 reshape.122
  286.0 0.1 pad_maximum_fusion.2
  286.2 0.1 squeeze.34
  286.3 0.7 dynamic_slice.47
  286.9 0.1 copy.69
  287.0 0.1 reduce_sum.31
  287.1 0.6 dynamic_slice.45
  287.7 0.1 copy.68
  287.8 0.1 slice.111
  287.9 0.1 fusion.2
  288.0 0.6 slice_reduce_fusion.3
  288.6 0.6 slice.132
  289.2 0.0 copy-done.1
  289.2 0.0 copy-start
  289.2 3.0 %convert_element_type.60 = f32[768,1536]{1,0:T(8,128)} convert(bf16[768,1536]{1,0:T(8,128)(2,1)S(1)} %copy-done.1) | non-fusion elementwise | flops 1179648 | bytes 7077888 | tf_op jit(solution)/shard_map/convert_element_type | solution.py:1314
  292.3 1.1 copy-done
  293.4 0.0 copy-start.3
  293.4 0.0 copy-start.2
  293.4 4.5 %convert_bitcast_fusion = f32[384,6448]{0,1:T(8,128)} fusion(bf16[6448,384]{1,0:T(8,128)(2,1)S(1)} %copy-done), kind=kLoop, calls=%fused_computation | loop fusion | flops 2476032 | bytes 14856192 | tf_op jit(solution)/shard_map/transpose | solution.py:1313
  297.9 0.0 copy-done.3
  297.9 0.9 copy.91
  298.8 0.0 copy-done.2
  298.8 1.1 copy.92
  (37 shorter events, 0.5 us)
Async XLA Ops:
  281.6 7.7 %copy-start.1 = (bf16[768,1536]{1,0:T(8,128)(2,1)S(1)}, bf16[768,1536]{1,0:T(8,128)(2,1)}, u32[]{:S(2)}) copy-start(bf16[768,1536]{1,0:T(8,128)(2,1)} %get-tuple-element.41) | copy-start | bytes 7077892
  289.2 4.1 %copy-start = (bf16[6448,384]{1,0:T(8,128)(2,1)S(1)}, bf16[6448,384]{1,0:T(8,128)(2,1)}, u32[]{:S(2)}) copy-start(bf16[6448,384]{1,0:T(8,128)(2,1)} %get-tuple-element.40) | copy-start | bytes 14856196
  293.4 4.5 %copy-start.3 = (bf16[256,1536]{1,0:T(8,128)(2,1)S(1)}, bf16[256,1536]{1,0:T(8,128)(2,1)}, u32[]{:S(2)}) copy-start(bf16[256,1536]{1,0:T(8,128)(2,1)} %get-tuple-element.38) | copy-start | bytes 2359300
  293.4 5.4 %copy-start.2 = (f32[256,1536]{1,0:T(8,128)S(1)}, f32[256,1536]{1,0:T(8,128)}, u32[]{:S(2)}) copy-start(f32[256,1536]{1,0:T(8,128)} %get-tuple-element.39) | copy-start | bytes 4718596

commit v3 on v2

--- a/solution.py
+++ b/solution.py
@@ -593,6 +593,10 @@
     return seq, lax.div(seq, 2), lax.rem(seq, 2), lax.axis_index("fsdp")
 
 
+def neighbours(chip):
+    return [chip, chip + 1 - 2 * lax.rem(chip, 2), lax.rem(chip + 2, CHIPS), CHIPS - 1 - chip]
+
+
 def send(src, dst, send_sem, recv_sem, device):
     return pltpu.make_async_remote_copy(
         src_ref=src, dst_ref=dst, send_sem=send_sem, recv_sem=recv_sem,
@@ -613,15 +617,15 @@
     tok_ref, cot_ref, win_ref, bcd_ref, wout_ref, small_ref, info_ref, idr_ref,
     nrm_ref, projc_ref, projz_ref, st_ref, ssd_ref, dno_ref, br_ref, stat_ref, par_ref, w_ref, g_ref,
     u_v, g_v, w_v, wo_v, smalls, ssd_v, cbuf, state, stat_v, stat_in,
-    loc, t_send, t_recv, f_send, f_recv, z_send, z_recv, b_send, b_recv, s_send, s_recv, r_send, r_recv,
+    loc, t_send, t_recv, y_send, y_recv, f_send, f_recv, z_send, z_recv, b_send, b_recv, s_send, s_recv, r_send, r_recv,
 ):
     i = pl.program_id(0)
     seq, chip, core, z = places()
     sib = {"seq": 2 * chip + 1 - core}
-    peer = lambda k: {"seq": 2 * lax.rem(chip + k, CHIPS) + core}
+    near = neighbours(chip)
+    peer = lambda k: {"seq": 2 * near[k] + core}
     under = lambda k: {"fsdp": lax.rem(z + k, DEPTH)}
     around = lambda k: {"seq": lax.rem(seq + k, TEAM)}
-    behind = lambda k: lax.rem(chip + CHIPS - k, CHIPS)
     block = lambda s: pl.ds(pl.multiple_of(BLK * s, BLK), BLK)
     lanes = lambda o: pl.ds(pl.multiple_of(KROWS * o, KROWS), KROWS)
     half = pl.ds(pl.multiple_of(NZ + NX + HALF * core, 16), HALF)
@@ -633,9 +637,39 @@
         src, dst = ((tok_ref, u_v), (cot_ref, g_v))[n]
         return send(src, dst.at[block(seq)], t_send.at[n, k], t_recv.at[n, k], sib if k == 0 else peer(k))
 
+    def token_part(n, k, h):
+        return (u_v, g_v)[n].at[pl.ds(pl.multiple_of(BLK * (2 * near[k] + core) + h * (BLK // 2), BLK // 2), BLK // 2)]
+
+    def token_relay(n, h):
+        part = token_part(n, 1 + h, h)
+        return send(part, part, y_send.at[n, h], y_recv.at[n, h], peer(2 - h))
+
     def token_next(n, k):
-        ref = (u_v, g_v)[n].at[block(2 * behind(k) + core)]
+        if k < 3:
+            ref = (u_v, g_v)[n].at[block(2 * near[k] + core)]
+        else:
+            ref = token_part(n, 3, k - 3)
         return send(ref, ref, f_send.at[n, k], f_recv.at[n, k], sib)
+
+    def token_start(n):
+        for k in range(3):
+            token_copy(n, k).start()
+
+    def token_turn(n):
+        for k in (1, 2):
+            token_copy(n, k).wait_recv()
+            token_relay(n, k - 1).start()
+            token_next(n, k).start()
+
+    def token_end(n):
+        for h in range(2):
+            token_relay(n, h).wait_recv()
+            token_next(n, 3 + h).start()
+        token_copy(n, 0).wait_recv()
+        for k in range(1, 5):
+            token_next(n, k).wait()
+        for h in range(2):
+            token_relay(n, h).wait_send()
 
     def place(p, o):
         if p < 3:
@@ -714,8 +748,7 @@
         greet([around(k) for k in range(1, TEAM)] + [under(k) for k in range(1, DEPTH)])
         for k in range(1, DEPTH):
             small_copy(k).start()
-        for k in range(CHIPS):
-            token_copy(0, k).start()
+        token_start(0)
         for copy in own_weights() + local_copies():
             copy.start()
 
@@ -729,17 +762,12 @@
         state[...] = jnp.zeros_like(state)
         cbuf[0:8, :] = jnp.zeros((8, CONVC), F32)
         pass_on((0, 1), 0)
+        token_turn(0)
+        token_start(1)
         pass_on((0, 1), 1)
         start_own((2,))
-        for k in range(1, CHIPS):
-            token_copy(0, k).wait_recv()
-            token_next(0, k).start()
-        for k in range(CHIPS):
-            token_copy(1, k).start()
+        token_end(0)
         pass_on((0, 1), 2)
-        token_copy(0, 0).wait_recv()
-        for k in range(1, CHIPS):
-            token_next(0, k).wait()
         for k in range(1, DEPTH):
             small_copy(k).wait()
         for copy in local_copies():
@@ -769,6 +797,10 @@
     def _():
         pass_on((2,), 1)
 
+    @pl.when(i == 4)
+    def _():
+        token_turn(1)
+
     @pl.when(i == 5)
     def _():
         pass_on((3, 4), 0)
@@ -780,12 +812,7 @@
     @pl.when(i == TEAM)
     def _():
         pass_on((2, 3, 4), 2)
-        for k in range(1, CHIPS):
-            token_copy(1, k).wait_recv()
-            token_next(1, k).start()
-        token_copy(1, 0).wait_recv()
-        for k in range(1, CHIPS):
-            token_next(1, k).wait()
+        token_end(1)
         pltpu.make_async_copy(w_v, w_ref, loc.at[18]).start()
         pltpu.make_async_copy(g_v, g_ref, loc.at[19]).start()
 
@@ -818,7 +845,7 @@
         for k in range(1, TEAM):
             stat_copy(k).wait_send()
         for n in range(2):
-            for k in range(CHIPS):
+            for k in range(3):
                 token_copy(n, k).wait_send()
         for side in range(2):
             for dist in range(DEPTH - 1):
@@ -857,8 +884,8 @@
                         pltpu.VMEM((n, CH), F32), pltpu.VMEM((BLK + 8, CONVC), F32),
                         pltpu.VMEM((STATE, CH), F32), pltpu.VMEM((TEAM, 2 * BLK), F32),
                         pltpu.VMEM((TEAM, TEAM, 2 * BLK), F32),
-                        dma((20,)), dma((2, CHIPS)), dma((2, CHIPS)), dma((2, CHIPS)),
-                        dma((2, CHIPS)), dma((5, 2, DEPTH - 1)), dma((5, 2, DEPTH - 1)),
+                        dma((20,)), dma((2, 3)), dma((2, 3)), dma((2, 2)), dma((2, 2)), dma((2, 5)),
+                        dma((2, 5)), dma((5, 2, DEPTH - 1)), dma((5, 2, DEPTH - 1)),
                         dma((2, DEPTH - 1)), dma((2, DEPTH - 1)),
                         dma((DEPTH,)), dma((DEPTH,)), dma((TEAM,)), dma((TEAM,))],
         compiler_params=pltpu.CompilerParams(
@@ -871,7 +898,7 @@
     projz_ref, ssd_ref, dno_ref, stat_ref, par_ref, projc_ref, halo_ref, st_ref, info_ref, idr_ref,
     out_ref, tg_ref, wig_ref, wog_ref, smalls_ref,
     nrm_v, g_v, w_v, not_v, dz_v, dzt_v, dy_v, rest_v, wig_v, wog_v, bcd_v, bcd_in,
-    zz_in, zx_in, zb_in, zw_in, zs_in, gz_v, gx_v, gb_v, gw_v, gb_in, gt_v, ob_v, rb_v, rr_v, rd_v,
+    zz_in, zx_in, zb_in, zw_in, zs_in, gz_v, gx_v, gb_v, gw_v, gb_in, gt_v, ob_v, rb_v, in_v, rel_v,
     tok_v, cot_v, small_v, small_s, cbuf, dcbuf, dstate,
     loc, b_send, b_recv, p_send, p_recv, d_send, d_recv, q_send, q_recv, z_send, z_recv,
     a_send, a_recv, f_send, f_recv, h_send, h_recv, free,
@@ -879,10 +906,10 @@
     i = pl.program_id(0)
     seq, chip, core, z = places()
     sib = {"seq": 2 * chip + 1 - core}
-    peer = lambda k: {"seq": 2 * lax.rem(chip + k, CHIPS) + core}
+    near = neighbours(chip)
+    peer = lambda k: {"seq": 2 * near[k] + core}
     under = lambda k: {"fsdp": lax.rem(z + k, DEPTH)}
     around = lambda k: {"seq": lax.rem(seq + k, TEAM)}
-    behind = lambda k: lax.rem(chip + CHIPS - k, CHIPS)
     block = lambda s: pl.ds(pl.multiple_of(BLK * s, BLK), BLK)
     lanes = lambda o: pl.ds(pl.multiple_of(KROWS * o, KROWS), KROWS)
     piece = lambda n: pl.ds(pl.multiple_of(HEADDIM * n, HEADDIM), HEADDIM)
@@ -902,18 +929,37 @@
     def br_pair(c):
         return send(br_ref.at[block(2 * c + 1 - core)], rb_v.at[c], b_send.at[c], b_recv.at[c], sib)
 
-    def br_push(k):
-        return send(ob_v.at[lax.rem(chip + k, CHIPS)], rr_v.at[k - 1], p_send.at[k], p_recv.at[k], peer(k))
+    def block_of(n, c):
+        return ob_v.at[c] if n == 0 else hold(c)
+
+    def rs(n, kind):
+        h = pl.ds((0, BLK // 2, BLK // 2, 0, 0, BLK // 2)[kind], BLK // 2)
+        src = block_of(n, near[(1, 1, 2, 2, 3, 3)[kind]]).at[h]
+        if kind < 4:
+            dst = in_v.at[n, kind // 2, h]
+        else:
+            dst = rel_v.at[n, 5 - kind]
+        return send(src, dst, p_send.at[n, kind], p_recv.at[n, kind], peer((1, 1, 2, 2, 1, 2)[kind]))
+
+    def rs_first(n, role):
+        for kind in ((), (0,), (2,), (4, 5))[role]:
+            rs(n, kind).start()
+
+    def rs_second(n, role):
+        kind, came = ((1, 5), (3, 4))[role - 1]
+        rs(n, came).wait_recv()
+        h = pl.ds((BLK // 2, 0)[role - 1], BLK // 2)
+        ref = block_of(n, near[role]).at[h]
+        ref[...] = (ref[...].astype(F32) + rel_v[n, role - 1].astype(F32)).astype(BF)
+        rs(n, kind).start()
+
+    def rs_total(n):
+        for kind in range(4):
+            rs(n, kind).wait_recv()
+        return block_of(n, chip)[...].astype(F32) + in_v[n, 0].astype(F32) + in_v[n, 1].astype(F32)
 
     def dn_pair(c):
         return send(give(c), rb_v.at[c], d_send.at[c], d_recv.at[c], sib)
-
-    def dn_push(c):
-        k = lax.rem(c + CHIPS - chip, CHIPS)
-        return send(hold(c), rd_v.at[k - 1], q_send.at[k], q_recv.at[k], {"seq": 2 * c + core})
-
-    def dn_pushed(k):
-        return send(hold(0), rd_v.at[k - 1], q_send.at[k], q_recv.at[k], peer(k))
 
     def down(n, k):
         o = lax.rem(z + k, DEPTH)
@@ -931,39 +977,49 @@
         return send(bcd_v.at[half(1 - core)], bcd_in, h_send.at[0], h_recv.at[0], sib)
 
     def bcd_push(k):
-        return send(gb_v, gb_in.at[k - 1], a_send.at[4, k], a_recv.at[4, k], peer(k))
+        return send(gb_v, gb_in.at[k - 1], q_send.at[k], q_recv.at[k], peer(k))
 
     def bcd_back():
         return send(gt_v.at[core], gt_v.at[core], h_send.at[1], h_recv.at[1], sib)
 
-    def parts(n, c, cr):
+    def parts(n, c, cr, h=None):
         if n < 2:
             base = n * DI // HEADDIM
             src = (gz_v, gx_v)[n]
-            return [(src.at[piece(s)], wig_ref.at[piece(base + head_of(s, c, cr)[s // 4])]) for s in range(HPD)]
-        if n == 2:
-            return [(gw_v.at[0:HEADDIM], wog_ref.at[piece(3 * c + 2 * cr)])]
-        if n == 3:
-            return [(gw_v.at[HEADDIM:], wog_ref.at[piece(3 * c + 1)])]
-        return [(small_s, smalls_ref.at[2 * c + cr])]
-
-    def all_of(n):
+            slots = range(HPD) if h is None else range(3 * h, 3 * h + 3)
+            return [(src.at[piece(s)], wig_ref.at[piece(base + head_of(s, c, cr)[s // 4])]) for s in slots]
+        if n < 4:
+            row = HEADDIM * (3 * c + 2 * cr if n == 2 else 3 * c + 1)
+            first, size = (0, HEADDIM) if h is None else (h * HEADDIM // 2, HEADDIM // 2)
+            return [(gw_v.at[pl.ds(HEADDIM * (n - 2) + first, size)],
+                     wog_ref.at[pl.ds(pl.multiple_of(row + first, HEADDIM // 2), size)])]
+        if h is None:
+            return [(small_s, smalls_ref.at[2 * c + cr])]
+        return [(small_s.at[8 * h : 8 * h + 8], smalls_ref.at[2 * c + cr, 8 * h : 8 * h + 8])]
+
+    def all_of(n, h=None):
         if n < 2:
-            return wig_ref.at[pl.ds(n * DI, n_all)]
-        return parts(n, 0, 0)[0][1]
+            return wig_ref.at[pl.ds(n * DI, n_all if h is None else n_all // 2)]
+        return parts(n, 0, 0, h)[0][1]
 
     def ag(n, k):
-        where = sib if k == 0 else peer(k)
-        return [send(src, dst, a_send.at[n, k], a_recv.at[n, k], where) for src, dst in parts(n, chip, core)]
+        if k < 3:
+            return [send(src, dst, a_send.at[n, k], a_recv.at[n, k], sib if k == 0 else peer(k))
+                    for src, dst in parts(n, chip, core)]
+        return [send(dst, dst, a_send.at[n, k], a_recv.at[n, k], peer(5 - k))
+                for _, dst in parts(n, near[k - 2], core, k - 3)]
 
     def ag_wait(n, k):
-        return send(all_of(n), all_of(n), a_send.at[n, k], a_recv.at[n, k], sib)
+        ref = all_of(n, None if k < 3 else k - 3)
+        return send(ref, ref, a_send.at[n, k], a_recv.at[n, k], sib)
 
     def ag_next(n, k):
-        return [send(dst, dst, f_send.at[n, k], f_recv.at[n, k], sib) for _, dst in parts(n, behind(k), core)]
+        which = parts(n, near[k], core) if k < 3 else parts(n, near[3], core, k - 3)
+        return [send(dst, dst, f_send.at[n, k], f_recv.at[n, k], sib) for _, dst in which]
 
     def ag_next_wait(n, k):
-        return send(all_of(n), all_of(n), f_send.at[n, k], f_recv.at[n, k], sib)
+        ref = all_of(n, None if k < 3 else k - 3)
+        return send(ref, ref, f_send.at[n, k], f_recv.at[n, k], sib)
 
     def ag_own(n):
         return [pltpu.make_async_copy(src, dst, loc.at[9 + n]) for src, dst in parts(n, chip, core)]
@@ -972,25 +1028,35 @@
         return pltpu.make_async_copy(all_of(n), all_of(n), loc.at[9 + n])
 
     def ag_start(n):
-        for k in range(1, CHIPS):
+        for k in (1, 2, 0):
             for copy in ag(n, k):
                 copy.start()
-        for copy in ag(n, 0) + ag_own(n):
+        for copy in ag_own(n):
             copy.start()
 
-    def ag_forward(n):
-        for k in range(1, CHIPS):
+    def ag_turn(n):
+        for k in (1, 2):
+            ag_wait(n, k).wait_recv()
+            for copy in ag(n, k + 2) + ag_next(n, k):
+                copy.start()
+
+    def ag_end(n):
+        for k in (3, 4):
             ag_wait(n, k).wait_recv()
             for copy in ag_next(n, k):
                 copy.start()
 
-    def ag_finish(n):
-        ag_wait(n, 0).wait_recv()
-        for k in range(CHIPS):
-            ag_wait(n, k).wait_send()
-        for k in range(1, CHIPS):
-            ag_next_wait(n, k).wait()
-        ag_own_wait(n).wait()
+    def ag_close(n, sends=True, receives=True):
+        if receives:
+            ag_wait(n, 0).wait_recv()
+            for k in range(1, 5):
+                ag_next_wait(n, k).wait_recv()
+        if sends:
+            for k in range(5):
+                ag_wait(n, k).wait_send()
+            for k in range(1, 5):
+                ag_next_wait(n, k).wait_send()
+            ag_own_wait(n).wait()
 
     def reduce_z(own, arrived):
         total = own.astype(F32)
@@ -1021,8 +1087,8 @@
             load_own(c).wait()
             br_pair(c).wait_recv()
             ob_v[c] = (ob_v[c].astype(F32) + rb_v[c].astype(F32)).astype(BF)
-        for k in range(1, CHIPS):
-            br_push(k).start()
+        for role in (3, 1, 2):
+            rs_first(0, role)
         pl.semaphore_signal(free, inc=1, device_id=sib, device_id_type=pl.DeviceIdType.MESH)
 
     @pl.when(i == TEAM)
@@ -1054,16 +1120,31 @@
     def combine(c):
         dn_pair(c).wait_recv()
         hold(c)[...] = (hold(c)[...].astype(F32) + rb_v[c].astype(F32)).astype(BF)
-
-        @pl.when(chip != c)
-        def _():
-            dn_push(c).start()
+        for role in (1, 2, 3):
+
+            @pl.when(near[role] == c)
+            def _():
+                rs_first(1, role)
+
+    def relay(c):
+        for role in (1, 2):
+
+            @pl.when(near[role] == c)
+            def _():
+                rs_second(1, role)
 
     for c in range(CHIPS - 1, 0, -1):
 
         @pl.when(i == TEAM + 1 + 2 * (CHIPS - c))
         def _():
             combine(c)
+            if c < CHIPS - 1:
+                relay(c + 1)
+
+    @pl.when(i == TEAM + 2)
+    def _():
+        rs_second(0, 1)
+        rs_second(0, 2)
 
     @pl.when((i > TEAM) & (i <= 2 * TEAM))
     def _():
@@ -1090,11 +1171,7 @@
 
     @pl.when(i == 2 * TEAM - 1)
     def _():
-        for k in range(1, CHIPS):
-            br_push(k).wait_recv()
-        total = ob_v[chip].astype(F32)
-        for k in range(1, CHIPS):
-            total = total + rr_v[k - 1].astype(F32)
+        total = rs_total(0)
         stat = stat_ref[pl.ds(seq, 1), 0:BLK]
         stat = jnp.broadcast_to(stat, (128, BLK)).T
         s2 = lax.rsqrt(stat[:, 0:1] * (1.0 / DI) + EPSILON)
@@ -1114,6 +1191,7 @@
         for k in range(1, DEPTH):
             down(5, k).start()
         combine(0)
+        relay(1)
 
         @pl.loop(0, D // 256)
         def _(n):
@@ -1135,6 +1213,8 @@
         bcd_v[half(core), :] = (bcd_v[half(core), :].astype(F32) + bcd_in[...].astype(F32)).astype(BF)
         for k in range(1, DEPTH):
             down(2, k).start()
+        relay(0)
+        ag_turn(0)
         for k in range(1, DEPTH):
             down(3, k).wait_recv()
         gw_v[0:HEADDIM, :] = reduce_z(wog_v[piece(z), :], [zw_in[k - 1, 0:HEADDIM] for k in range(1, DEPTH)]).astype(BF)
@@ -1151,18 +1231,21 @@
         for k in range(1, DEPTH):
             down(5, k).wait_recv()
         small_s[...] = reduce_z(small_v[...], [zs_in[k - 1] for k in range(1, DEPTH)])
-        ag_start(5)
-        ag_forward(0)
-        for k in range(1, CHIPS):
-            dn_pushed(k).wait_recv()
-        total = hold(chip)[...].astype(F32)
-        for k in range(1, CHIPS):
-            total = total + rd_v[k - 1].astype(F32)
+        ag_start(4)
+        ag_end(0)
+        total = rs_total(1)
         uf = tok_v[...].astype(F32)
         along = total * norm_gain(par_ref[...])
         s1 = lax.rsqrt(jnp.mean(uf * uf, axis=1, keepdims=True) + EPSILON)
         tg_ref[...] = cot_v[...].astype(F32) + s1 * along - uf * (
             s1 * s1 * s1 * jnp.mean(along * uf, axis=1, keepdims=True))
+        ag_turn(2)
+
+        @pl.when(extra(z))
+        def _():
+            ag_turn(3)
+
+        ag_turn(4)
         for k in range(1, DEPTH):
             down(1, k).wait_recv()
         gx_v[...] = reduce_z(wig_v[:, lanes(z)], [zx_in[k - 1] for k in range(1, DEPTH)]).astype(BF)
@@ -1172,13 +1255,14 @@
         gb_v[...] = reduce_z(bcd_v[half(core), lanes(z)], [zb_in[k - 1] for k in range(1, DEPTH)]).astype(BF)
         for k in range(1, CHIPS):
             bcd_push(k).start()
-        ag_forward(2)
+        ag_end(2)
 
         @pl.when(extra(z))
         def _():
-            ag_forward(3)
-
-        ag_forward(5)
+            ag_end(3)
+
+        ag_end(4)
+        ag_turn(1)
         for k in range(1, CHIPS):
             bcd_push(k).wait_recv()
         total = gb_v[...].astype(F32)
@@ -1186,7 +1270,7 @@
             total = total + gb_in[k - 1].astype(F32)
         gt_v[core] = total.astype(BF)
         bcd_back().start()
-        ag_forward(1)
+        ag_end(1)
         bcd_back().wait()
         last = [
             pltpu.make_async_copy(gt_v.at[0], wig_ref.at[pl.ds(2 * DI, HALF)], loc.at[15]),
@@ -1194,29 +1278,24 @@
                                   wig_ref.at[pl.ds(2 * DI + HALF, WIDTH - 2 * DI - HALF)], loc.at[16])]
         for copy in last:
             copy.start()
-        for n in (0, 1, 2, 5):
-            ag_finish(n)
+        for n in (0, 1, 2, 4):
+            ag_close(n)
 
         @pl.when(extra(z))
         def _():
-            for k in range(CHIPS):
-                ag_wait(3, k).wait_send()
-            for k in range(1, CHIPS):
-                ag_next_wait(3, k).wait_send()
-            ag_own_wait(3).wait()
+            ag_close(3, receives=False)
 
         @pl.when(jnp.logical_not(extra(z)))
         def _():
-            ag_wait(3, 0).wait_recv()
-            for k in range(1, CHIPS):
-                ag_next_wait(3, k).wait_recv()
+            ag_close(3, sends=False)
 
         for c in range(CHIPS):
             br_pair(c).wait_send()
             dn_pair(c).wait_send()
+        for n in range(2):
+            for kind in range(6):
+                rs(n, kind).wait_send()
         for k in range(1, CHIPS):
-            br_push(k).wait_send()
-            dn_pushed(k).wait_send()
             bcd_push(k).wait_send()
         for k in range(1, DEPTH):
             for n in (1, 2, 3, 5):
@@ -1259,12 +1338,12 @@
             vm((DEPTH - 1, CH, KROWS), BF), vm((DEPTH - 1, CH, KROWS), BF), vm((DEPTH - 1, HALF, KROWS), BF),
             vm((DEPTH - 1, 2 * HEADDIM, D), BF), vm((DEPTH - 1, 16, CONVC), F32), vm((CH, KROWS), BF), vm((CH, KROWS), BF),
             vm((HALF, KROWS), BF), vm((2 * HEADDIM, D), BF), vm((CHIPS - 1, HALF, KROWS), BF), vm((2, HALF, KROWS), BF),
-            vm((CHIPS, BLK, D), BF), vm((CHIPS, BLK, D), BF), vm((CHIPS - 1, BLK, D), BF), vm((CHIPS - 1, BLK, D), BF),
+            vm((CHIPS, BLK, D), BF), vm((CHIPS, BLK, D), BF), vm((2, 2, BLK, D), BF), vm((2, 2, BLK // 2, D), BF),
             vm((BLK, D), BF), vm((BLK, D), BF), vm((16, CONVC), F32), vm((16, CONVC), F32),
             vm((BLK + 8, CONVC), F32), vm((BLK + 8, CONVC), F32), vm((STATE, CH), F32),
-            dma((17,)), dma((CHIPS,)), dma((CHIPS,)), dma((CHIPS,)), dma((CHIPS,)), dma((CHIPS,)), dma((CHIPS,)),
+            dma((17,)), dma((CHIPS,)), dma((CHIPS,)), dma((2, 6)), dma((2, 6)), dma((CHIPS,)), dma((CHIPS,)),
             dma((CHIPS,)), dma((CHIPS,)), dma((6, DEPTH)), dma((6, DEPTH)),
-            dma((6, CHIPS)), dma((6, CHIPS)), dma((6, CHIPS)), dma((6, CHIPS)), dma((2,)), dma((2,)),
+            dma((5, 5)), dma((5, 5)), dma((5, 5)), dma((5, 5)), dma((2,)), dma((2,)),
             pltpu.SemaphoreType.REGULAR],
         compiler_params=pltpu.CompilerParams(
             collective_id=1, has_side_effects=True, vmem_limit_bytes=63 << 20),

time: 303 us -> 266 us (0.88)
  Pallas kernels: 265 us -> 230 us
    pallas_call x1, Pallas kernels: 157 us -> 131 us  [backward_call(): pl.pallas_call(backward_kernel, grid=(2 * TEAM + 2,), in_specs=[any_space...]
    pallas_call x1, Pallas kernels: 108 us -> 98.7 us  [forward_call(): pl.pallas_call(forward_kernel, grid=(2 * TEAM,), in_specs=[any_space] * 6...]
where the time goes in v3:
time: 266 us; the launch traced here: 265 us
  Pallas kernels  230 us (86%)
  local copies, waits for them, and re-layouts  19.8 us (7%)
  other arithmetic  14.4 us (5%)
    pallas_call x1, Pallas kernels, backward_call(): pl.pallas_call(backward_kernel, grid=(2 * TEAM + 2,), in_specs=[any_space...  131 us
    pallas_call x1, Pallas kernels, forward_call(): pl.pallas_call(forward_kernel, grid=(2 * TEAM,), in_specs=[any_space] * 6...  98.7 us

profile of v3, /device:TPU:0, one launch (start us, length us, event | category | flops | bytes accessed | tf_op | source)
XLA Modules:
  0.0 264.8 jit_solution(17916549076917288144)
XLA Ops:
  0.7 0.9 dynamic_update_slice.22
  1.6 0.8 dynamic_update_slice.23
  2.4 0.1 pad.40.clone
  2.5 0.8 dynamic_update_slice.21
  3.4 0.1 broadcast_in_dim.44
  3.4 0.7 broadcast_in_dim.41
  4.1 0.9 dynamic_update_slice.24
  5.0 0.8 pad_slice_fusion.5
  5.8 0.1 slice_reduce_fusion.2
  5.9 0.1 broadcast_bitcast_fusion.1
  6.0 0.7 pad_maximum_fusion.3
  6.7 0.7 reshape_dynamic-update-slice_fusion
  7.5 0.1 concatenate.42
  7.6 0.1 broadcast_in_dim.45
  7.6 0.5 broadcast.48
  8.2 1.4 fusion.19
  9.5 0.1 slice.125
  9.6 0.1 copy.74
  9.7 0.1 broadcast_bitcast_fusion
  9.8 0.7 compare_convert_fusion
  10.5 1.0 fusion.10
  11.6 0.3 dynamic_update_slice.19
  11.9 0.1 concatenate.41
  12.2 0.1 reshape.119
  12.3 0.7 fusion.4.small_ref
  13.0 0.6 broadcast_in_dim.50.idr_ref
  13.6 0.1 stack.57
  13.7 1.0 slice.121
  14.7 0.7 pad.25.bcd_ref
  15.4 0.4 copy.63
  15.8 1.0 pad.29.info_ref
  16.8 98.7 %shard_map.203 = (bf16[2048,1536]{1,0:T(8,128)(2,1)}, bf16[2048,704]{1,0:T(8,128)(2,1)}, bf16[2048,384]{1,0:T(8,128)(2,1)}, f32[8,128,384]{2,1,0:T(8,128)}, f32[...) custom-call(bf16[256,1536]{1,0:T(8,128)(2,1)} %bitcast.56, ...), custom_call_target="tpu_custom_call" | custom-call | tf_op jit(solution)/shard_map/pallas_call | solution.py:872
  115.6 130.9 %shard_map.204 = (bf16[256,1536]{1,0:T(8,128)(2,1)}, f32[256,1536]{1,0:T(8,128)}, bf16[6448,384]{1,0:T(8,128)(2,1)}, bf16[768,1536]{1,0:T(8,128)(2,1)}, f32[8,16,640]{2,1,0:T(8,128)}) custom-call(bf16[256,1536]{1,0:T(8,128)(2,1)} %bitcast.57, bf16[256,1536]{1,0:T(8,128)(2,1)} %bitcast.59, bf16[2048,1536]{1,0:T(8,128)(2,1)} %get-tuple-element.27.nrm_ref, ...), custom_call_target="tpu_custom_call" | custom-call | tf_op jit(solution)/shard_map/pallas_call | solution.py:1324
  246.4 0.0 copy-start.1
  246.4 1.0 slice_reduce_fusion.1
  247.4 0.6 fusion.16
  248.0 1.0 slice_reduce_fusion
  249.0 0.9 slice.105
  249.9 0.7 dynamic_slice.46
  250.6 0.1 reshape.122
  250.9 0.1 pad_maximum_fusion.2
  251.0 0.1 squeeze.34
  251.1 0.7 dynamic_slice.47
  251.8 0.1 copy.69
  251.9 0.1 reduce_sum.31
  252.0 0.6 dynamic_slice.45
  252.6 0.1 copy.68
  252.7 0.1 slice.111
  252.8 0.1 fusion.2
  252.9 0.6 slice_reduce_fusion.3
  253.5 0.6 slice.132
  254.1 0.0 copy-done.1
  254.1 0.0 copy-start
  254.1 3.0 %convert_element_type.60 = f32[768,1536]{1,0:T(8,128)} convert(bf16[768,1536]{1,0:T(8,128)(2,1)S(1)} %copy-done.1) | non-fusion elementwise | flops 1179648 | bytes 7077888 | tf_op jit(solution)/shard_map/convert_element_type | solution.py:1393
  257.2 1.1 copy-done
  258.2 0.0 copy-start.3
  258.2 0.0 copy-start.2
  258.2 4.5 %convert_bitcast_fusion = f32[384,6448]{0,1:T(8,128)} fusion(bf16[6448,384]{1,0:T(8,128)(2,1)S(1)} %copy-done), kind=kLoop, calls=%fused_computation | loop fusion | flops 2476032 | bytes 14856192 | tf_op jit(solution)/shard_map/transpose | solution.py:1392
  262.8 0.0 copy-done.3
  262.8 0.9 copy.91
  263.6 0.0 copy-done.2
  263.6 1.1 copy.92
  (37 shorter events, 0.5 us)
Async XLA Ops:
  246.4 7.7 %copy-start.1 = (bf16[768,1536]{1,0:T(8,128)(2,1)S(1)}, bf16[768,1536]{1,0:T(8,128)(2,1)}, u32[]{:S(2)}) copy-start(bf16[768,1536]{1,0:T(8,128)(2,1)} %get-tuple-element.41) | copy-start | bytes 7077892
  254.1 4.1 %copy-start = (bf16[6448,384]{1,0:T(8,128)(2,1)S(1)}, bf16[6448,384]{1,0:T(8,128)(2,1)}, u32[]{:S(2)}) copy-start(bf16[6448,384]{1,0:T(8,128)(2,1)} %get-tuple-element.40) | copy-start | bytes 14856196
  258.2 4.5 %copy-start.3 = (bf16[256,1536]{1,0:T(8,128)(2,1)S(1)}, bf16[256,1536]{1,0:T(8,128)(2,1)}, u32[]{:S(2)}) copy-start(bf16[256,1536]{1,0:T(8,128)(2,1)} %get-tuple-element.38) | copy-start | bytes 2359300
  258.2 5.4 %copy-start.2 = (f32[256,1536]{1,0:T(8,128)S(1)}, f32[256,1536]{1,0:T(8,128)}, u32[]{:S(2)}) copy-start(f32[256,1536]{1,0:T(8,128)} %get-tuple-element.39) | copy-start | bytes 4718596

commit v4 on v3

--- a/solution.py
+++ b/solution.py
@@ -13,6 +13,7 @@
 HEADS = 48
 D = 1536
 WIDTH = 6448
+DEPTH = 4
 CHAN = 3328
 
 
@@ -373,7 +374,7 @@
 
 
 def norm_gain(par):
-    return jnp.concatenate([par[7 + i : 8 + i, :512] for i in range(3)], axis=1)
+    return jnp.concatenate([par[7 + i : 8 + i, :CH] for i in range(D // CH)], axis=1)
 
 
 def row_sum(q):
@@ -528,7 +529,10 @@
     d_step = q_term + fade * r_term - d_log * rate
     d_a = -jnp.sum(d_log * step, axis=0, keepdims=True) * rate
     d_dt = jnp.where(own, d_step * sigmoid(dt_in), 0.0)
-    heads = jnp.concatenate([d_a, jnp.sum(d_dt, axis=0, keepdims=True), jnp.zeros((6, 128), F32)], axis=0)
+    d_skip = split_dot(jnp.broadcast_to(jnp.sum(dy * x, axis=0, keepdims=True), (8, CH)), gh)[0:1, :]
+    d_skip = jnp.where(own[0:1, :], d_skip, 0.0)
+    heads = jnp.concatenate(
+        [d_a, jnp.sum(d_dt, axis=0, keepdims=True), d_skip, jnp.zeros((5, 128), F32)], axis=0)
     high = heads.astype(BF)
     heads = dot_nt(high, pick) + dot_nt((heads - high.astype(F32)).astype(BF), pick)
     d_dt = dot_nt(d_dt.astype(BF), pick)
@@ -555,34 +559,68 @@
     small_v[0:CONV, :] += jnp.concatenate(cg, axis=0)
     small_v[CONV : CONV + 1, :] += jnp.sum(d_conv, axis=0, keepdims=True)
     small_v[5:6, CH:] += jnp.concatenate([heads[0:1, :], heads[1:2, :]], axis=1)
-    small_v[6:7, :CH] += jnp.sum(dy * x, axis=0, keepdims=True)
+    small_v[6:7, CH : CH + 128] += heads[2:3, :]
     return jnp.concatenate([d_in, d_dt[:, :ND]], axis=1)
 
 
-def token_info(ids_full, first, n):
-    length = ids_full.shape[0]
-    pad = jnp.concatenate(
-        [jnp.full((8,), -1, jnp.int32), ids_full, jnp.full((8,), -2, jnp.int32)]
-    )
-    window = lax.dynamic_slice_in_dim(pad, first, n + 16)
-    own = window[8 : 8 + n]
-    blocks = own.reshape(-1, BLK)
-    before = window[7 : 7 + n].reshape(-1, BLK)[:, :1]
-    cols = [own]
+def id_row(ids_ref, j):
+    return ids_ref[0:1, pl.ds(pl.multiple_of(BLK * j, BLK), BLK)].astype(F32)
+
+
+def token_info(ids_ref, j, blocks):
+    row = id_row(ids_ref, j)
+    left = jnp.where(j > 0, id_row(ids_ref, jnp.maximum(j - 1, 0)), -1.0)
+    right = jnp.where(j < blocks - 1, id_row(ids_ref, jnp.minimum(j + 1, blocks - 1)), -2.0)
+    lane = iota((1, BLK), 1)
+    wide = lambda a: jnp.broadcast_to(a, (8, BLK))
+    rows = [row]
     for back in range(1, CONV):
-        cols.append((window[8 - back : 8 - back + n] == own))
+        shifted = jnp.where(lane < back, pltpu.roll(wide(left), back, 1)[0:1], pltpu.roll(wide(row), back, 1)[0:1])
+        rows.append((shifted == row).astype(F32))
     for ahead in range(1, CONV):
-        cols.append((window[8 + ahead : 8 + ahead + n] == own))
-    cols.append((blocks == before).reshape(-1))
-    cols.append((blocks == blocks[:, -1:]).reshape(-1))
-    table = jnp.stack([c.astype(F32) for c in cols], axis=1)
-    tok = jnp.pad(table, ((0, 0), (0, 128 - table.shape[1])))
-    idr = jnp.broadcast_to(own.astype(F32).reshape(-1, 1, BLK), (n // BLK, 8, BLK))
-    return tok, idr
+        turn = BLK - ahead
+        shifted = jnp.where(lane >= turn, pltpu.roll(wide(right), turn, 1)[0:1], pltpu.roll(wide(row), turn, 1)[0:1])
+        rows.append((shifted == row).astype(F32))
+    rows.append((row == left[:, BLK - 1 :]).astype(F32))
+    rows.append((row == row[:, BLK - 1 :]).astype(F32))
+    rows.append(jnp.zeros((128 - len(rows), BLK), F32))
+    return row, jnp.concatenate(rows, axis=0).T
+
+
+def pack_small(convw, convb, alog, dtb, dskip, normw, gatew, chip, core, z):
+    def channel(m):
+        slot = m // HEADDIM
+        first, second = head_of(slot, chip, core)
+        return jnp.where(slot < 4, first, second) * HEADDIM + m % HEADDIM
+
+    row = lambda a: a.astype(F32).reshape(1, a.shape[0])
+    pad = lambda a: jnp.concatenate([row(a), jnp.zeros((1, 128 - HEADS // DEPTH), F32)], axis=1)
+    heads = jnp.concatenate([pad(dtb), pad(alog), pad(dskip), jnp.zeros((5, 128), F32)], axis=0).astype(BF)
+    m = iota((CHAN // DEPTH, CONVC), 1)
+    want = jnp.where(m < CH, channel(m), DI + m - CH)
+    chosen = (iota((CHAN // DEPTH, CONVC), 0) + z * (CHAN // DEPTH) == want).astype(BF)
+    conv = jnp.concatenate([convw.astype(F32), row(convb), jnp.zeros((3, CHAN // DEPTH), F32)], axis=0)
+    conv = dot(conv.astype(BF), chosen)
+    n = DI // DEPTH
+    chosen = (iota((n, CH), 0) + z * n == channel(iota((n, CH), 1))).astype(BF)
+    gate = dot(jnp.broadcast_to(row(gatew), (8, n)).astype(BF), chosen)[0:1]
+    n = HEADS // DEPTH
+    k = iota((128, CH), 0)
+    chosen = ((k < n) & (k + z * n == channel(iota((128, CH), 1)) // HEADDIM)).astype(BF)
+    skip = dot(heads, chosen)[2:3]
+    k = iota((128, 128), 0)
+    chosen = ((k < n) & (k + z * n == iota((128, 128), 1))).astype(BF)
+    heads = dot(heads, chosen)
+    gain = jnp.where(iota((DEPTH, CH), 0) == z, jnp.broadcast_to(row(normw), (DEPTH, CH)), 0.0)
+    return jnp.concatenate([
+        conv[0:5],
+        jnp.concatenate([gate, heads[0:1], heads[1:2]], axis=1),
+        jnp.concatenate([skip, jnp.zeros((1, NB), F32)], axis=1),
+        jnp.concatenate([gain, jnp.zeros((DEPTH, NB), F32)], axis=1),
+        jnp.zeros((5, CONVC), F32)], axis=0).astype(BF)
 
 
 CHIPS = TEAM // 2
-DEPTH = 4
 KROWS = D // DEPTH
 BCD = NB + ND
 HALF = BCD // 2
@@ -614,9 +652,9 @@
 
 
 def forward_kernel(
-    tok_ref, cot_ref, win_ref, bcd_ref, wout_ref, small_ref, info_ref, idr_ref,
-    nrm_ref, projc_ref, projz_ref, st_ref, ssd_ref, dno_ref, br_ref, stat_ref, par_ref, w_ref, g_ref,
-    u_v, g_v, w_v, wo_v, smalls, ssd_v, cbuf, state, stat_v, stat_in,
+    tok_ref, cot_ref, win_ref, wout_ref, ids_ref, convw_ref, convb_ref, alog_ref, dtb_ref, skip_ref, normw_ref, gatew_ref,
+    nrm_ref, projc_ref, projz_ref, st_ref, ssd_ref, dno_ref, br_ref, info_ref, stat_ref, par_ref, w_ref, g_ref,
+    u_v, g_v, w_v, wo_v, small_v, smalls, ssd_v, cbuf, state, stat_v, stat_in,
     loc, t_send, t_recv, y_send, y_recv, f_send, f_recv, z_send, z_recv, b_send, b_recv, s_send, s_recv, r_send, r_recv,
 ):
     i = pl.program_id(0)
@@ -696,17 +734,17 @@
         return there & (lax.rem(o + DEPTH, 2) == core) if p == 4 else there
 
     def small_copy(k):
-        return send(small_ref, smalls.at[z], s_send.at[k], s_recv.at[k], under(k))
+        return send(small_v, smalls.at[k - 1], s_send.at[k], s_recv.at[k], under(k))
 
     def stat_copy(k):
         return send(stat_v, stat_in.at[k], r_send.at[k], r_recv.at[k], around(k))
 
     def local_copies():
-        pairs = [(tok_ref, u_v.at[block(seq)]), (cot_ref, g_v.at[block(seq)]), (small_ref, smalls.at[z])]
+        pairs = [(tok_ref, u_v.at[block(seq)]), (cot_ref, g_v.at[block(seq)])]
         return [pltpu.make_async_copy(src, dst, loc.at[n]) for n, (src, dst) in enumerate(pairs)]
 
     def own_weights():
-        pairs = [(bcd_ref, w_v.at[pl.ds(NZ + NX, BCD), lanes(z)], 3)]
+        pairs = [(win_ref.at[pl.ds(2 * DI, WIDTH - 2 * DI)], w_v.at[pl.ds(NZ + NX, WIDTH - 2 * DI), lanes(z)], 3)]
         for n in range(HPD):
             row = HEADDIM * heads[n]
             pairs.append((win_ref.at[pl.ds(pl.multiple_of(row, HEADDIM), HEADDIM)],
@@ -746,8 +784,6 @@
     @pl.when(i == 0)
     def _():
         greet([around(k) for k in range(1, TEAM)] + [under(k) for k in range(1, DEPTH)])
-        for k in range(1, DEPTH):
-            small_copy(k).start()
         token_start(0)
         for copy in own_weights() + local_copies():
             copy.start()
@@ -756,9 +792,14 @@
         def _():
             own_extra().start()
 
+        w_v[NZ + NX + WIDTH - 2 * DI :, lanes(z)] = jnp.zeros((BCD - (WIDTH - 2 * DI), KROWS), BF)
         for copy in own_weights():
             copy.wait()
         start_own((0, 1))
+        small_v[...] = pack_small(convw_ref[...], convb_ref[...], alog_ref[...], dtb_ref[...], skip_ref[...],
+                                  normw_ref[...], gatew_ref[...], chip, core, z)
+        for k in range(1, DEPTH):
+            small_copy(k).start()
         state[...] = jnp.zeros_like(state)
         cbuf[0:8, :] = jnp.zeros((8, CONVC), F32)
         pass_on((0, 1), 0)
@@ -779,9 +820,9 @@
                 def _():
                     share(side, dist).wait()
 
-        total = smalls[0].astype(F32)
-        for o in range(1, DEPTH):
-            total = total + smalls[o].astype(F32)
+        total = small_v[...].astype(F32)
+        for k in range(1, DEPTH):
+            total = total + smalls[k - 1].astype(F32)
         par_ref[...] = total
 
     @pl.when(i == 1)
@@ -825,7 +866,9 @@
         nrm = (u * scale * norm_gain(par)).astype(BF)
         nrm_ref[...] = nrm
         u_v[block(i), :] = nrm
-        scan_forward(i, nrm, w_v, par, info_ref[...], idr_ref[0, 0:1, :], cbuf, state,
+        row, info = token_info(ids_ref, i, TEAM)
+        info_ref[...] = info
+        scan_forward(i, nrm, w_v, par, info, row, cbuf, state,
                      projc_ref, st_ref, ssd_v)
 
     @pl.when(i >= TEAM)
@@ -859,7 +902,7 @@
         pltpu.make_async_copy(g_v, g_ref, loc.at[19]).wait()
 
 
-def forward_call(tok, cot, win, bcd, wout, small, info, idr):
+def forward_call(tok, cot, win, wout, ids, small):
     n = tok.shape[0] * TEAM
     any_space = pl.BlockSpec(memory_space=pl.ANY)
     sds = jax.ShapeDtypeStruct
@@ -872,15 +915,16 @@
     return pl.pallas_call(
         forward_kernel,
         grid=(2 * TEAM,),
-        in_specs=[any_space] * 6 + [rows(128, one), cube(8, BLK)],
+        in_specs=[any_space] * 4 + [
+            pl.BlockSpec(a.shape, lambda i, n=a.ndim: (0,) * n, pipeline_mode=pl.Buffered(1)) for a in (ids, *small)],
         out_specs=[rows(D, one), rows(REST, one), rows(NZ, two), cube(STATE, CH), rows(CH, two),
-                   rows(CH, two), rows(D, two), fixed(TEAM, 2 * BLK), fixed(16, CONVC), any_space,
-                   any_space],
+                   rows(CH, two), rows(D, two), rows(128, one), fixed(TEAM, 2 * BLK), fixed(16, CONVC),
+                   any_space, any_space],
         out_shape=[sds((n, D), BF), sds((n, REST), BF), sds((n, NZ), BF), sds((TEAM, STATE, CH), F32),
-                   sds((n, CH), F32), sds((n, CH), F32), sds((n, D), BF), sds((TEAM, 2 * BLK), F32),
+                   sds((n, CH), F32), sds((n, CH), F32), sds((n, D), BF), sds((n, 128), F32), sds((TEAM, 2 * BLK), F32),
                    sds((16, CONVC), F32), sds((COLS, D), BF), sds((n, D), BF)],
         scratch_shapes=[pltpu.VMEM((n, D), BF), pltpu.VMEM((n, D), BF), pltpu.VMEM((COLS, D), BF),
-                        pltpu.VMEM((CH, D), BF), pltpu.VMEM((DEPTH, 16, CONVC), BF),
+                        pltpu.VMEM((CH, D), BF), pltpu.VMEM((16, CONVC), BF), pltpu.VMEM((DEPTH - 1, 16, CONVC), BF),
                         pltpu.VMEM((n, CH), F32), pltpu.VMEM((BLK + 8, CONVC), F32),
                         pltpu.VMEM((STATE, CH), F32), pltpu.VMEM((TEAM, 2 * BLK), F32),
                         pltpu.VMEM((TEAM, TEAM, 2 * BLK), F32),
@@ -890,12 +934,12 @@
                         dma((DEPTH,)), dma((DEPTH,)), dma((TEAM,)), dma((TEAM,))],
         compiler_params=pltpu.CompilerParams(
             collective_id=0, has_side_effects=True, vmem_limit_bytes=60 << 20),
-    )(tok, cot, win, bcd, wout, small, info, idr)
+    )(tok, cot, win, wout, ids, *small)
 
 
 def backward_kernel(
     tok_ref, cot_ref, nrm_ref, br_ref, w_ref, g_ref,
-    projz_ref, ssd_ref, dno_ref, stat_ref, par_ref, projc_ref, halo_ref, st_ref, info_ref, idr_ref,
+    projz_ref, ssd_ref, dno_ref, stat_ref, par_ref, projc_ref, halo_ref, st_ref, info_ref, ids_ref,
     out_ref, tg_ref, wig_ref, wog_ref, smalls_ref,
     nrm_v, g_v, w_v, not_v, dz_v, dzt_v, dy_v, rest_v, wig_v, wog_v, bcd_v, bcd_in,
     zz_in, zx_in, zb_in, zw_in, zs_in, gz_v, gx_v, gb_v, gw_v, gb_in, gt_v, ob_v, rb_v, in_v, rel_v,
@@ -1150,13 +1194,13 @@
     def _():
         j = 2 * TEAM - i
         rows = block(j)
-        d_rest = scan_backward(projc_ref[...], halo_ref[...], info_ref[...], idr_ref[0, 0:1, :], st_ref[0],
+        d_rest = scan_backward(projc_ref[...], halo_ref[...], info_ref[...], id_row(ids_ref, j), st_ref[0],
                                par_ref[...], dy_v[rows, :], cbuf, dcbuf, dstate, small_v)
         rest_v[:, rows] = d_rest.T.astype(BF)
         dn = dot(dz_v[rows, :], w_v[:NZ, :]) + dot(d_rest.astype(BF), w_v[NZ:, :])
         part = jnp.sum(dn * nrm_v[rows, :].astype(F32), axis=0, keepdims=True)
-        for n in range(3):
-            small_v[7 + n : 8 + n, :512] += part[:, 512 * n : 512 * n + 512]
+        for n in range(D // CH):
+            small_v[7 + n : 8 + n, :CH] += part[:, CH * n : CH * n + CH]
         dn = dn.astype(BF)
         c = lax.div(j, 2)
 
@@ -1186,8 +1230,8 @@
 
     @pl.when(i == 2 * TEAM + 1)
     def _():
-        for n in range(3):
-            small_v[7 + n : 8 + n, :512] = small_v[7 + n : 8 + n, :512] / par_ref[7 + n : 8 + n, :512]
+        for n in range(D // CH):
+            small_v[7 + n : 8 + n, :CH] = small_v[7 + n : 8 + n, :CH] / par_ref[7 + n : 8 + n, :CH]
         for k in range(1, DEPTH):
             down(5, k).start()
         combine(0)
@@ -1310,7 +1354,7 @@
             copy.wait()
 
 
-def backward_call(tok, cot, nrm, br, w, g, projz, ssd, dno, stat, par, projc, st, info, idr):
+def backward_call(tok, cot, nrm, br, w, g, projz, ssd, dno, stat, par, projc, st, info, ids):
     n = nrm.shape[0]
     any_space = pl.BlockSpec(memory_space=pl.ANY)
     sds = jax.ShapeDtypeStruct
@@ -1327,7 +1371,7 @@
         in_specs=[any_space] * 6 + [
             rows(NZ, one), rows(CH, one), rows(CH, one), fixed(TEAM, 2 * BLK), fixed(16, CONVC), rows(REST, two),
             pl.BlockSpec((16, REST), lambda i: (jnp.maximum(16 * two(i) - 1, 0), 0)),
-            cube(STATE, CH), rows(128, two), cube(8, BLK)],
+            cube(STATE, CH), rows(128, two), fixed(1, n)],
         out_specs=[fixed(BLK, D), fixed(BLK, D), any_space, any_space, any_space],
         out_shape=[sds((BLK, D), BF), sds((BLK, D), F32), sds((WIDTH, KROWS), BF),
                    sds((DI // DEPTH, D), BF), sds((TEAM, 16, CONVC), F32)],
@@ -1347,62 +1391,91 @@
             pltpu.SemaphoreType.REGULAR],
         compiler_params=pltpu.CompilerParams(
             collective_id=1, has_side_effects=True, vmem_limit_bytes=63 << 20),
-    )(tok, cot, nrm, br, w, g, projz, ssd, dno, stat, par, projc, projc, st, info, idr)
+    )(tok, cot, nrm, br, w, g, projz, ssd, dno, stat, par, projc, projc, st, info, ids)
+
+
+def finish_kernel(
+    lo_ref, tg_ref, wig_ref, wog_ref, smalls_ref,
+    out_ref, grad_ref, win_ref, wout_ref, convw_ref, convb_ref, alog_ref, dtb_ref, skip_ref, normw_ref, gatew_ref,
+    all_v, in_v, in_f, wo_v, wo_f, lo_v, tg_v, sems,
+):
+    rows_in, rows_wo = WIDTH // 13, DI // DEPTH // 4
+    chunks = [(wig_ref, in_v, in_f, win_ref, slice(rows_in * n, rows_in * n + rows_in)) for n in range(13)]
+    chunks += [(wog_ref, wo_v, wo_f, wout_ref, slice(rows_wo * n, rows_wo * n + rows_wo)) for n in range(4)]
+    come = [pltpu.make_async_copy(a.at[r], b.at[r], sems.at[0, n]) for n, (a, b, _, _, r) in enumerate(chunks)]
+    go = [pltpu.make_async_copy(a.at[r], b.at[r], sems.at[1, n]) for n, (_, _, a, b, r) in enumerate(chunks)]
+    last = len(chunks)
+    enter = [pltpu.make_async_copy(lo_ref, lo_v, sems.at[0, last]), pltpu.make_async_copy(tg_ref, tg_v, sems.at[0, last + 1])]
+    leave = [pltpu.make_async_copy(lo_v, out_ref, sems.at[1, last]), pltpu.make_async_copy(tg_v, grad_ref, sems.at[1, last + 1])]
+    for copy in come + enter:
+        copy.start()
+    for n, (_, src, dst, _, r) in enumerate(chunks):
+        come[n].wait()
+        dst[r] = src[r].astype(F32)
+        go[n].start()
+    for n in range(2):
+        enter[n].wait()
+        leave[n].start()
+    for d in range(TEAM):
+        for slot in range(HPD):
+            head = head_of(slot, d // 2, d % 2)[slot // 4]
+            all_v[:, HEADDIM * head : HEADDIM * head + HEADDIM] = smalls_ref[
+                d, 0:8, HEADDIM * slot : HEADDIM * slot + HEADDIM]
+    side = smalls_ref[0, :, CH:]
+    gain = smalls_ref[0, :, :CH]
+    for d in range(1, TEAM):
+        side = side + smalls_ref[d, :, CH:]
+        gain = gain + smalls_ref[d, :, :CH]
+    all_v[:, DI:] = side[0:8]
+    z = lax.axis_index("fsdp")
+    nc, ng, nh = CHAN // DEPTH, DI // DEPTH, HEADS // DEPTH
+    for o in range(DEPTH):
+
+        @pl.when(z == o)
+        def _():
+            convw_ref[...] = all_v[0:CONV, nc * o : nc * o + nc]
+            convb_ref[...] = all_v[CONV : CONV + 1, nc * o : nc * o + nc].reshape(nc)
+            gatew_ref[...] = all_v[5:6, ng * o : ng * o + ng].reshape(ng)
+            alog_ref[...] = side[5:6, nh * o : nh * o + nh].reshape(nh)
+            dtb_ref[...] = side[5:6, 128 + nh * o : 128 + nh * o + nh].reshape(nh)
+            skip_ref[...] = side[6:7, nh * o : nh * o + nh].reshape(nh)
+            normw_ref[...] = gain[7 + o : 8 + o, :].reshape(KROWS)
+
+    for copy in go + leave:
+        copy.wait()
+
+
+def finish_call(lo, tg, wig, wog, smalls):
+    any_space = pl.BlockSpec(memory_space=pl.ANY)
+    vmem = pl.BlockSpec(memory_space=pltpu.VMEM)
+    sizes = [(CONV, CHAN // DEPTH), (CHAN // DEPTH,)] + [(HEADS // DEPTH,)] * 3 + [(KROWS,), (DI // DEPTH,)]
+    sds = jax.ShapeDtypeStruct
+    rows = DI // DEPTH
+    return pl.pallas_call(
+        finish_kernel,
+        in_specs=[any_space] * 4 + [vmem],
+        out_specs=[any_space] * 4 + [vmem] * len(sizes),
+        out_shape=[sds((BLK, D), BF), sds((BLK, D), F32), sds((WIDTH, KROWS), F32), sds((rows, D), F32)]
+        + [sds(s, F32) for s in sizes],
+        scratch_shapes=[pltpu.VMEM((8, CHAN), F32), pltpu.VMEM((WIDTH, KROWS), BF), pltpu.VMEM((WIDTH, KROWS), F32),
+                        pltpu.VMEM((rows, D), BF), pltpu.VMEM((rows, D), F32), pltpu.VMEM((BLK, D), BF), pltpu.VMEM((BLK, D), F32),
+                        pltpu.SemaphoreType.DMA((2, 19))],
+        compiler_params=pltpu.CompilerParams(vmem_limit_bytes=62 << 20),
+    )(lo, tg, wig, wog, smalls)
 
 
 def on_team(
     tokens, segment_ids, cotangent, w_in, w_out, conv_w, conv_b, a_log, dt_bias, d_skip,
     norm_w, gate_w,
 ):
-    place = lax.axis_index("seq")
-    chip, core = place // 2, place % 2
-    depth = lax.axis_index("fsdp")
-    shards = DEPTH
-    n = tokens.shape[1] * TEAM
-    w_t = w_in.T
-    bcd = jnp.pad(w_t[2 * DI :], ((0, BCD - (WIDTH - 2 * DI)), (0, 0)))
-
-    def put(a, whole_size):
-        return lax.dynamic_update_slice_in_dim(
-            jnp.zeros(a.shape[:-1] + (whole_size,), BF), a, depth * a.shape[-1], a.ndim - 1)
-
-    def own_part(a):
-        a = a.reshape(a.shape[0], 4, 12, HEADDIM)
-        a = lax.dynamic_slice_in_dim(a, 3 * chip, 3, 2)
-        first = lax.dynamic_index_in_dim(a, 2 * core, 2, keepdims=False)
-        second = a[:, :, 1].reshape(-1, 2, 2, HEADDIM)
-        second = lax.dynamic_index_in_dim(second, core, 2, keepdims=False)
-        return jnp.concatenate([first, second], axis=1).reshape(a.shape[0], CH)
-
-    wide = lambda a, size: jnp.pad(a, (0, size - a.shape[0]))
-    conv_rows = put(jnp.concatenate([conv_w, conv_b[None]], axis=0), CHAN)
-    chan_rows = own_part(jnp.concatenate(
-        [conv_rows[:, :DI], put(gate_w, DI)[None], jnp.repeat(put(d_skip, HEADS), HEADDIM)[None]], axis=0))
-    heads_row = jnp.concatenate([wide(put(dt_bias, HEADS), 128), wide(put(a_log, HEADS), 128)])
-    side = jnp.concatenate([conv_rows[:, DI:], heads_row[None], jnp.zeros((1, NB), BF)], axis=0)
-    gain_rows = jnp.pad(put(norm_w, D).reshape(3, D // 3), ((0, 0), (0, CONVC - D // 3)))
-    small = jnp.concatenate(
-        [jnp.concatenate([chan_rows, side], axis=1), gain_rows, jnp.zeros((6, CONVC), BF)], axis=0)
-    tok, idr = token_info(segment_ids[0], 0, n)
-    u_own, g_own = tokens[0], cotangent[0]
-    nrm, projc, projz, st, ssd, dno, br, stat, par, w_loc, g = forward_call(
-        u_own, g_own, w_t, bcd, w_out, small, tok, idr)
-    layer_out, token_grad, wig, wog, smalls = backward_call(
-        u_own, g_own, nrm, br, w_loc, g, projz, ssd, dno, stat, par, projc, st, tok, idr)
-    w_in_grad = wig.astype(F32).T
-    w_out_grad = wog.astype(F32)
-    parts = smalls[:, :7, :CH].reshape(CHIPS, 2, 7, HPD, HEADDIM)
-    first = parts[:, :, :, :4].transpose(1, 2, 3, 0, 4)
-    second = parts[:, :, :, 4:].transpose(2, 3, 1, 0, 4).reshape(7, 4, CHIPS, HEADDIM)
-    chang = jnp.stack([first[0], second, first[1]], axis=3).reshape(7, DI)
-    sideg = jnp.sum(smalls[:, :6, CH:], axis=0)
-    normg = jnp.sum(smalls[:, 7:10, :512], axis=0).reshape(D)
-    convg = jnp.concatenate([chang[:5], sideg[:5]], axis=1)
-    mine = lambda a: lax.dynamic_slice_in_dim(a, depth * (a.shape[-1] // shards), a.shape[-1] // shards, a.ndim - 1)
-    convg = mine(convg)
-    skipg = jnp.sum(chang[6].reshape(HEADS, HEADDIM), axis=1)
-    return (layer_out[None], token_grad[None], w_in_grad, w_out_grad, convg[:4], convg[4],
-            mine(sideg[5, :HEADS]), mine(sideg[5, 128 : 128 + HEADS]), mine(skipg), mine(normg), mine(chang[5]))
+    tok, cot = tokens[0], cotangent[0]
+    small = (conv_w, conv_b, a_log, dt_bias, d_skip, norm_w, gate_w)
+    nrm, projc, projz, st, ssd, dno, br, info, stat, par, w_loc, g = forward_call(
+        tok, cot, w_in.T, w_out, segment_ids, small)
+    lo, tg, wig, wog, smalls = backward_call(
+        tok, cot, nrm, br, w_loc, g, projz, ssd, dno, stat, par, projc, st, info, segment_ids)
+    lo, tg, wig, wog, convw, convb, alog, dtb, skip, normw, gatew = finish_call(lo, tg, wig, wog, smalls)
+    return (lo[None], tg[None], wig.T, wog, convw, convb, alog, dtb, skip, normw, gatew)
 
 
 def solution(mesh):

time: 266 us -> 242 us (0.910)
  local copies, waits for them, and re-layouts: 19.8 us -> 0 us
  other arithmetic: 14.4 us -> 0 us
  Pallas kernels: 230 us -> 241 us
    pallas_call x1 -> x2, Pallas kernels: 98.7 us -> 110 us  [the longest x1 99.3 us: forward_call(): pl.pallas_call(forward_kernel, grid=(2 * TEAM,), in_specs=[any_space] * 4...]
    transpose x1 -> x0, other arithmetic: 4.53 us -> none  [on_team(): w_in_grad = wig.astype(F32).T]
    dynamic_update_slice x6 -> x0, local copies, waits for them, and re-layouts: 4.43 us -> none  [put(): lax.dynamic_update_slice_in_dim(jnp.zeros(a.shape[:-1] + (whole_size,), B...]
    slice x15 -> x0, local copies, waits for them, and re-layouts: 4.29 us -> none  [the longest x1 0.97 us: on_team(): bcd = jnp.pad(w_t[2 * DI:], ((0, BCD - (WIDTH - 2 * DI)), (0, 0)))]
    unnamed x19 -> x0, local copies, waits for them, and re-layouts: 3.88 us -> none
    convert_element_type x3 -> x0, other arithmetic: 3.77 us -> none  [the longest x1 3.05 us: on_team(): w_out_grad = wog.astype(F32)]
where the time goes in v4:
time: 242 us
  Pallas kernels  241 us (100%)
    pallas_call x1, Pallas kernels, backward_call(): pl.pallas_call(backward_kernel, grid=(2 * TEAM + 2,), in_specs=[any_space...  130 us
    pallas_call x1, Pallas kernels, forward_call(): pl.pallas_call(forward_kernel, grid=(2 * TEAM,), in_specs=[any_space] * 4...  99.3 us
    pallas_call x1, Pallas kernels, finish_call(): pl.pallas_call(finish_kernel, in_specs=[any_space] * 4 + [vmem], out_spec...  11.2 us

profile of v4, /device:TPU:0, one launch (start us, length us, event | category | flops | bytes accessed | tf_op | source)
XLA Modules:
  0.0 241.5 jit_solution(9846208047473910831)
XLA Ops:
  0.6 99.3 %shard_map.203 = (bf16[2048,1536]{1,0:T(8,128)(2,1)}, bf16[2048,704]{1,0:T(8,128)(2,1)}, bf16[2048,384]{1,0:T(8,128)(2,1)}, f32[8,128,384]{2,1,0:T(8,128)}, f32[...) custom-call(bf16[256,1536]{1,0:T(8,128)(2,1)} %bitcast.7, ...), custom_call_target="tpu_custom_call" | custom-call | tf_op jit(solution)/shard_map/pallas_call | solution.py:915
  100.0 130.2 %shard_map.204 = (bf16[256,1536]{1,0:T(8,128)(2,1)}, f32[256,1536]{1,0:T(8,128)}, bf16[6448,384]{1,0:T(8,128)(2,1)}, bf16[768,1536]{1,0:T(8,128)(2,1)}, f32[8,16,640]{2,1,0:T(8,128)}) custom-call(bf16[256,1536]{1,0:T(8,128)(2,1)} %bitcast.8, bf16[256,1536]{1,0:T(8,128)(2,1)} %bitcast.10, bf16[2048,1536]{1,0:T(8,128)(2,1)} %get-tuple-element.39.nrm_ref, ...), custom_call_target="tpu_custom_call" | custom-call | tf_op jit(solution)/shard_map/pallas_call | solution.py:1368
  230.2 11.2 %shard_map.205 = (bf16[256,1536]{1,0:T(8,128)(2,1)}, f32[256,1536]{1,0:T(8,128)}, f32[6448,384]{1,0:T(8,128)}, f32[768,1536]{1,0:T(8,128)}, f32[4,832]{1,0:T(4,1...) custom-call(bf16[256,1536]{1,0:T(8,128)(2,1)} %get-tuple-element.51.l, ...), custom_call_target="tpu_custom_call" | custom-call | tf_op jit(solution)/shard_map/pallas_call | solution.py:1454

commit v5 on v4

--- a/solution.py
+++ b/solution.py
@@ -303,9 +303,13 @@
 
 
 def dot_exact(a, b):
-    return lax.dot_general(
-        a, b, (((1,), (0,)), ((), ())), precision=HIGHEST, preferred_element_type=F32
-    )
+    high = b.astype(BF)
+    left = b - high.astype(F32)
+    middle = left.astype(BF)
+    low = (left - middle.astype(F32)).astype(BF)
+    n = b.shape[1]
+    p = dot(a.astype(BF), jnp.concatenate([high, middle, low], axis=1))
+    return p[:, :n] + p[:, n : 2 * n] + p[:, 2 * n :]
 
 
 def iota(shape, dim):
@@ -942,9 +946,9 @@
     projz_ref, ssd_ref, dno_ref, stat_ref, par_ref, projc_ref, halo_ref, st_ref, info_ref, ids_ref,
     out_ref, tg_ref, wig_ref, wog_ref, smalls_ref,
     nrm_v, g_v, w_v, not_v, dz_v, dzt_v, dy_v, rest_v, wig_v, wog_v, bcd_v, bcd_in,
-    zz_in, zx_in, zb_in, zw_in, zs_in, gz_v, gx_v, gb_v, gw_v, gb_in, gt_v, ob_v, rb_v, in_v, rel_v,
+    zz_in, zx_in, zb_in, zw_in, zs_in, zz_rel, zx_rel, zb_rel, zw_rel, gz_v, gx_v, gb_v, gw_v, gb_in, gt_v, ob_v, rb_v, in_v, rel_v,
     tok_v, cot_v, small_v, small_s, cbuf, dcbuf, dstate,
-    loc, b_send, b_recv, p_send, p_recv, d_send, d_recv, q_send, q_recv, z_send, z_recv,
+    loc, b_send, b_recv, p_send, p_recv, d_send, d_recv, q_send, q_recv, z_send, z_recv, s_send, s_recv,
     a_send, a_recv, f_send, f_recv, h_send, h_recv, free,
 ):
     i = pl.program_id(0)
@@ -1005,17 +1009,70 @@
     def dn_pair(c):
         return send(give(c), rb_v.at[c], d_send.at[c], d_recv.at[c], sib)
 
-    def down(n, k):
-        o = lax.rem(z + k, DEPTH)
-        src, dst = [
-            (wig_v.at[:, lanes(o)], zz_in.at[k - 1]),
-            (wig_v.at[:, lanes(o)], zx_in.at[k - 1]),
-            (bcd_v.at[half(core), lanes(o)], zb_in.at[k - 1]),
-            (wog_v.at[piece(o)], zw_in.at[k - 1, 0:HEADDIM]),
-            (wog_v.at[piece(DEPTH + lax.div(o, 2))], zw_in.at[k - 1, HEADDIM:]),
-            (small_v, zs_in.at[k - 1]),
-        ][n]
-        return send(src, dst, z_send.at[n, k], z_recv.at[n, k], under(k))
+    mate = z + 1 - 2 * lax.rem(z, 2)
+    outer = (z == 0) | (z == DEPTH - 1)
+    far = lambda j: (2 + j) - lax.div(z, 2) * (1 + 2 * j)
+    rest = [slice(None)] * 3 + [slice(0, HEADDIM), slice(HEADDIM, 2 * HEADDIM)]
+    z_in = [zz_in, zx_in, zb_in, zw_in, zw_in]
+    z_rel = [zz_rel, zx_rel, zb_rel, zw_rel, zw_rel]
+
+    def z_part(n, o):
+        if n < 2:
+            return wig_v.at[:, lanes(o)]
+        if n == 2:
+            return bcd_v.at[half(core), lanes(o)]
+        return wog_v.at[piece(o if n == 3 else DEPTH + lax.div(o, 2))]
+
+    def z_mate(n):
+        return send(z_part(n, mate), z_in[n].at[0, rest[n]], z_send.at[n, 0], z_recv.at[n, 0], {"fsdp": mate})
+
+    def z_hand(n, j):
+        return send(z_part(n, far(j)), z_rel[n].at[j, rest[n]], z_send.at[n, 2 + j], z_recv.at[n, 2 + j], {"fsdp": mate})
+
+    def z_far(n, j):
+        return send(z_part(n, far(j)), z_in[n].at[1, rest[n]], z_send.at[n, 2 + j], z_recv.at[n, 1], {"fsdp": far(j)})
+
+    def held(n, o, also=None):
+        if n == 4:
+            return extra(o) if also is None else extra(o) & also
+        return also
+
+    def under_cond(cond, body):
+        if cond is None:
+            body()
+        else:
+            pl.when(cond)(body)
+
+    def z_start(n):
+        for j in (1, 0):
+            under_cond(held(n, far(j), outer), lambda: z_hand(n, j).start())
+
+    def z_start_mate(n):
+        under_cond(held(n, mate), lambda: z_mate(n).start())
+
+    def z_relay(n):
+        for j in (1, 0):
+
+            def body():
+                z_hand(n, j).wait_recv()
+                ref = z_part(n, far(j))
+                ref[...] = (ref[...].astype(F32) + z_rel[n][j, rest[n]].astype(F32)).astype(BF)
+                z_far(n, j).start()
+
+            under_cond(held(n, far(j), jnp.logical_not(outer)), body)
+
+    def z_total(n):
+        z_mate(n).wait_recv()
+        z_far(n, 0).wait_recv()
+        return z_part(n, z)[...].astype(F32) + z_in[n][0, rest[n]].astype(F32) + z_in[n][1, rest[n]].astype(F32)
+
+    def z_close(n):
+        under_cond(held(n, mate), lambda: z_mate(n).wait_send())
+        for j in range(2):
+            under_cond(held(n, far(j)), lambda: z_far(n, j).wait_send())
+
+    def small_copy(k):
+        return send(small_v, zs_in.at[k - 1], s_send.at[k], s_recv.at[k], under(k))
 
     def bcd_pair():
         return send(bcd_v.at[half(1 - core)], bcd_in, h_send.at[0], h_recv.at[0], sib)
@@ -1102,12 +1159,6 @@
                 ag_next_wait(n, k).wait_send()
             ag_own_wait(n).wait()
 
-    def reduce_z(own, arrived):
-        total = own.astype(F32)
-        for k in range(1, DEPTH):
-            total = total + arrived[k - 1].astype(F32)
-        return total
-
     @pl.when(i == 0)
     def _():
         greet([around(k) for k in range(1, TEAM)] + [under(k) for k in range(1, DEPTH)])
@@ -1146,20 +1197,17 @@
             cols = pl.ds(pl.multiple_of(256 * n, 256), 256)
             wig_v[:, cols] = dot(dzt_v[...], nrm_v[:, cols]).astype(BF)
 
-        for k in range(1, DEPTH):
-            down(0, k).start()
+        z_start(0)
 
         @pl.loop(0, D // 256)
         def _(n):
             cols = pl.ds(pl.multiple_of(256 * n, 256), 256)
             wog_v[:, cols] = dot(not_v[...], g_v[:, cols]).astype(BF)
 
-        for k in range(1, DEPTH):
-            down(3, k).start()
-
-            @pl.when(extra(z + k))
-            def _():
-                down(4, k).start()
+        z_start(3)
+        z_start(4)
+        for n in (0, 3, 4):
+            z_start_mate(n)
 
     def combine(c):
         dn_pair(c).wait_recv()
@@ -1189,6 +1237,11 @@
     def _():
         rs_second(0, 1)
         rs_second(0, 2)
+
+    @pl.when(i == 2 * TEAM)
+    def _():
+        gz_v[...] = z_total(0).astype(BF)
+        ag_start(0)
 
     @pl.when((i > TEAM) & (i <= 2 * TEAM))
     def _():
@@ -1221,21 +1274,22 @@
         s2 = lax.rsqrt(stat[:, 0:1] * (1.0 / DI) + EPSILON)
         out_ref[...] = (tok_v[...].astype(F32) + total * s2).astype(BF)
 
-    @pl.when(i == 2 * TEAM)
-    def _():
-        for k in range(1, DEPTH):
-            down(0, k).wait_recv()
-        gz_v[...] = reduce_z(wig_v[:, lanes(z)], [zz_in[k - 1] for k in range(1, DEPTH)]).astype(BF)
-        ag_start(0)
+    @pl.when(i == TEAM + 4)
+    def _():
+        z_relay(0)
+
+    @pl.when(i == TEAM + 6)
+    def _():
+        z_relay(3)
+        z_relay(4)
 
     @pl.when(i == 2 * TEAM + 1)
     def _():
         for n in range(D // CH):
             small_v[7 + n : 8 + n, :CH] = small_v[7 + n : 8 + n, :CH] / par_ref[7 + n : 8 + n, :CH]
         for k in range(1, DEPTH):
-            down(5, k).start()
+            small_copy(k).start()
         combine(0)
-        relay(1)
 
         @pl.loop(0, D // 256)
         def _(n):
@@ -1243,39 +1297,45 @@
             bcd_v[:, cols] = dot(rest_v[NX:, :], nrm_v[:, cols]).astype(BF)
 
         bcd_pair().start()
-        for k in range(1, DEPTH):
-            down(0, k).wait_send()
+        relay(1)
+        z_close(0)
 
         @pl.loop(0, D // 256)
         def _(n):
             cols = pl.ds(pl.multiple_of(256 * n, 256), 256)
             wig_v[:, cols] = dot(rest_v[:NX, :], nrm_v[:, cols]).astype(BF)
 
-        for k in range(1, DEPTH):
-            down(1, k).start()
+        z_start(1)
+        z_start_mate(1)
         bcd_pair().wait_recv()
         bcd_v[half(core), :] = (bcd_v[half(core), :].astype(F32) + bcd_in[...].astype(F32)).astype(BF)
-        for k in range(1, DEPTH):
-            down(2, k).start()
-        relay(0)
-        ag_turn(0)
-        for k in range(1, DEPTH):
-            down(3, k).wait_recv()
-        gw_v[0:HEADDIM, :] = reduce_z(wog_v[piece(z), :], [zw_in[k - 1, 0:HEADDIM] for k in range(1, DEPTH)]).astype(BF)
+        z_start(2)
+        z_start_mate(2)
+        gw_v[0:HEADDIM, :] = z_total(3).astype(BF)
         ag_start(2)
 
         @pl.when(extra(z))
         def _():
-            for k in range(1, DEPTH):
-                down(4, k).wait_recv()
-            gw_v[HEADDIM:, :] = reduce_z(
-                wog_v[piece(DEPTH + lax.div(z, 2)), :], [zw_in[k - 1, HEADDIM:] for k in range(1, DEPTH)]).astype(BF)
+            gw_v[HEADDIM:, :] = z_total(4).astype(BF)
             ag_start(3)
 
+        relay(0)
+        total = small_v[...]
         for k in range(1, DEPTH):
-            down(5, k).wait_recv()
-        small_s[...] = reduce_z(small_v[...], [zs_in[k - 1] for k in range(1, DEPTH)])
+            small_copy(k).wait_recv()
+            total = total + zs_in[k - 1]
+        small_s[...] = total
         ag_start(4)
+        ag_turn(0)
+        z_relay(1)
+        z_relay(2)
+        ag_turn(2)
+
+        @pl.when(extra(z))
+        def _():
+            ag_turn(3)
+
+        ag_turn(4)
         ag_end(0)
         total = rs_total(1)
         uf = tok_v[...].astype(F32)
@@ -1283,22 +1343,8 @@
         s1 = lax.rsqrt(jnp.mean(uf * uf, axis=1, keepdims=True) + EPSILON)
         tg_ref[...] = cot_v[...].astype(F32) + s1 * along - uf * (
             s1 * s1 * s1 * jnp.mean(along * uf, axis=1, keepdims=True))
-        ag_turn(2)
-
-        @pl.when(extra(z))
-        def _():
-            ag_turn(3)
-
-        ag_turn(4)
-        for k in range(1, DEPTH):
-            down(1, k).wait_recv()
-        gx_v[...] = reduce_z(wig_v[:, lanes(z)], [zx_in[k - 1] for k in range(1, DEPTH)]).astype(BF)
+        gx_v[...] = z_total(1).astype(BF)
         ag_start(1)
-        for k in range(1, DEPTH):
-            down(2, k).wait_recv()
-        gb_v[...] = reduce_z(bcd_v[half(core), lanes(z)], [zb_in[k - 1] for k in range(1, DEPTH)]).astype(BF)
-        for k in range(1, CHIPS):
-            bcd_push(k).start()
         ag_end(2)
 
         @pl.when(extra(z))
@@ -1306,6 +1352,9 @@
             ag_end(3)
 
         ag_end(4)
+        gb_v[...] = z_total(2).astype(BF)
+        for k in range(1, CHIPS):
+            bcd_push(k).start()
         ag_turn(1)
         for k in range(1, CHIPS):
             bcd_push(k).wait_recv()
@@ -1342,13 +1391,9 @@
         for k in range(1, CHIPS):
             bcd_push(k).wait_send()
         for k in range(1, DEPTH):
-            for n in (1, 2, 3, 5):
-                down(n, k).wait_send()
-
-            @pl.when(extra(z + k))
-            def _():
-                down(4, k).wait_send()
-
+            small_copy(k).wait_send()
+        for n in (1, 2, 3, 4):
+            z_close(n)
         bcd_pair().wait_send()
         for copy in last:
             copy.wait()
@@ -1379,14 +1424,15 @@
             vm((n, D), BF), vm((n, D), BF), vm((COLS, D), BF), vm((CH, n), BF), vm((n, CH), BF), vm((CH, n), BF),
             vm((n, CH), F32), vm((REST, n), BF), vm((CH, D), BF), vm((CH, D), BF), vm((BCD, D), BF),
             vm((HALF, D), BF),
-            vm((DEPTH - 1, CH, KROWS), BF), vm((DEPTH - 1, CH, KROWS), BF), vm((DEPTH - 1, HALF, KROWS), BF),
-            vm((DEPTH - 1, 2 * HEADDIM, D), BF), vm((DEPTH - 1, 16, CONVC), F32), vm((CH, KROWS), BF), vm((CH, KROWS), BF),
+            vm((2, CH, KROWS), BF), vm((2, CH, KROWS), BF), vm((2, HALF, KROWS), BF), vm((2, 2 * HEADDIM, D), BF),
+            vm((DEPTH - 1, 16, CONVC), F32),
+            vm((2, CH, KROWS), BF), vm((2, CH, KROWS), BF), vm((2, HALF, KROWS), BF), vm((2, 2 * HEADDIM, D), BF), vm((CH, KROWS), BF), vm((CH, KROWS), BF),
             vm((HALF, KROWS), BF), vm((2 * HEADDIM, D), BF), vm((CHIPS - 1, HALF, KROWS), BF), vm((2, HALF, KROWS), BF),
             vm((CHIPS, BLK, D), BF), vm((CHIPS, BLK, D), BF), vm((2, 2, BLK, D), BF), vm((2, 2, BLK // 2, D), BF),
             vm((BLK, D), BF), vm((BLK, D), BF), vm((16, CONVC), F32), vm((16, CONVC), F32),
             vm((BLK + 8, CONVC), F32), vm((BLK + 8, CONVC), F32), vm((STATE, CH), F32),
             dma((17,)), dma((CHIPS,)), dma((CHIPS,)), dma((2, 6)), dma((2, 6)), dma((CHIPS,)), dma((CHIPS,)),
-            dma((CHIPS,)), dma((CHIPS,)), dma((6, DEPTH)), dma((6, DEPTH)),
+            dma((CHIPS,)), dma((CHIPS,)), dma((5, 4)), dma((5, 4)), dma((DEPTH,)), dma((DEPTH,)),
             dma((5, 5)), dma((5, 5)), dma((5, 5)), dma((5, 5)), dma((2,)), dma((2,)),
             pltpu.SemaphoreType.REGULAR],
         compiler_params=pltpu.CompilerParams(

time: 242 us -> 237 us (0.979)
  Pallas kernels: 241 us -> 236 us
    pallas_call x1, Pallas kernels: 130 us -> 125 us  [backward_call(): pl.pallas_call(backward_kernel, grid=(2 * TEAM + 2,), in_specs=[any_space...]
where the time goes in v5:
time: 237 us; the launch traced here: 236 us
  Pallas kernels  236 us (100%)
    pallas_call x1, Pallas kernels, backward_call(): pl.pallas_call(backward_kernel, grid=(2 * TEAM + 2,), in_specs=[any_space...  125 us
    pallas_call x1, Pallas kernels, forward_call(): pl.pallas_call(forward_kernel, grid=(2 * TEAM,), in_specs=[any_space] * 4...  99.3 us
    pallas_call x1, Pallas kernels, finish_call(): pl.pallas_call(finish_kernel, in_specs=[any_space] * 4 + [vmem], out_spec...  11.2 us

profile of v5, /device:TPU:0, one launch (start us, length us, event | category | flops | bytes accessed | tf_op | source)
XLA Modules:
  0.0 236.4 jit_solution(7797392335563837761)
XLA Ops:
  0.6 99.3 %shard_map.203 = (bf16[2048,1536]{1,0:T(8,128)(2,1)}, bf16[2048,704]{1,0:T(8,128)(2,1)}, bf16[2048,384]{1,0:T(8,128)(2,1)}, f32[8,128,384]{2,1,0:T(8,128)}, f32[...) custom-call(bf16[256,1536]{1,0:T(8,128)(2,1)} %bitcast.7, ...), custom_call_target="tpu_custom_call" | custom-call | tf_op jit(solution)/shard_map/pallas_call | solution.py:919
  100.0 125.1 %shard_map.204 = (bf16[256,1536]{1,0:T(8,128)(2,1)}, f32[256,1536]{1,0:T(8,128)}, bf16[6448,384]{1,0:T(8,128)(2,1)}, bf16[768,1536]{1,0:T(8,128)(2,1)}, f32[8,16,640]{2,1,0:T(8,128)}) custom-call(bf16[256,1536]{1,0:T(8,128)(2,1)} %bitcast.8, bf16[256,1536]{1,0:T(8,128)(2,1)} %bitcast.10, bf16[2048,1536]{1,0:T(8,128)(2,1)} %get-tuple-element.39.nrm_ref, ...), custom_call_target="tpu_custom_call" | custom-call | tf_op jit(solution)/shard_map/pallas_call | solution.py:1413
  225.1 11.2 %shard_map.205 = (bf16[256,1536]{1,0:T(8,128)(2,1)}, f32[256,1536]{1,0:T(8,128)}, f32[6448,384]{1,0:T(8,128)}, f32[768,1536]{1,0:T(8,128)}, f32[4,832]{1,0:T(4,1...) custom-call(bf16[256,1536]{1,0:T(8,128)(2,1)} %get-tuple-element.51.l, ...), custom_call_target="tpu_custom_call" | custom-call | tf_op jit(solution)/shard_map/pallas_call | solution.py:1500

commit v6 on v5

--- a/solution.py
+++ b/solution.py
@@ -998,7 +998,7 @@
         rs(n, came).wait_recv()
         h = pl.ds((BLK // 2, 0)[role - 1], BLK // 2)
         ref = block_of(n, near[role]).at[h]
-        ref[...] = (ref[...].astype(F32) + rel_v[n, role - 1].astype(F32)).astype(BF)
+        ref[...] = ref[...] + rel_v[n, role - 1]
         rs(n, kind).start()
 
     def rs_total(n):
@@ -1056,7 +1056,7 @@
             def body():
                 z_hand(n, j).wait_recv()
                 ref = z_part(n, far(j))
-                ref[...] = (ref[...].astype(F32) + z_rel[n][j, rest[n]].astype(F32)).astype(BF)
+                ref[...] = ref[...] + z_rel[n][j, rest[n]]
                 z_far(n, j).start()
 
             under_cond(held(n, far(j), jnp.logical_not(outer)), body)
@@ -1181,7 +1181,7 @@
         for c in range(CHIPS):
             load_own(c).wait()
             br_pair(c).wait_recv()
-            ob_v[c] = (ob_v[c].astype(F32) + rb_v[c].astype(F32)).astype(BF)
+            ob_v[c] = ob_v[c] + rb_v[c]
         for role in (3, 1, 2):
             rs_first(0, role)
         pl.semaphore_signal(free, inc=1, device_id=sib, device_id_type=pl.DeviceIdType.MESH)
@@ -1192,16 +1192,16 @@
         for n in range(5):
             load(n).wait()
 
-        @pl.loop(0, D // 256)
+        @pl.loop(0, D // 512)
         def _(n):
-            cols = pl.ds(pl.multiple_of(256 * n, 256), 256)
+            cols = pl.ds(pl.multiple_of(512 * n, 512), 512)
             wig_v[:, cols] = dot(dzt_v[...], nrm_v[:, cols]).astype(BF)
 
         z_start(0)
 
-        @pl.loop(0, D // 256)
+        @pl.loop(0, D // 512)
         def _(n):
-            cols = pl.ds(pl.multiple_of(256 * n, 256), 256)
+            cols = pl.ds(pl.multiple_of(512 * n, 512), 512)
             wog_v[:, cols] = dot(not_v[...], g_v[:, cols]).astype(BF)
 
         z_start(3)
@@ -1211,7 +1211,7 @@
 
     def combine(c):
         dn_pair(c).wait_recv()
-        hold(c)[...] = (hold(c)[...].astype(F32) + rb_v[c].astype(F32)).astype(BF)
+        hold(c)[...] = hold(c)[...] + rb_v[c]
         for role in (1, 2, 3):
 
             @pl.when(near[role] == c)
@@ -1250,7 +1250,7 @@
         d_rest = scan_backward(projc_ref[...], halo_ref[...], info_ref[...], id_row(ids_ref, j), st_ref[0],
                                par_ref[...], dy_v[rows, :], cbuf, dcbuf, dstate, small_v)
         rest_v[:, rows] = d_rest.T.astype(BF)
-        dn = dot(dz_v[rows, :], w_v[:NZ, :]) + dot(d_rest.astype(BF), w_v[NZ:, :])
+        dn = dot(jnp.concatenate([dz_v[rows, :], d_rest.astype(BF)], axis=1), w_v[...])
         part = jnp.sum(dn * nrm_v[rows, :].astype(F32), axis=0, keepdims=True)
         for n in range(D // CH):
             small_v[7 + n : 8 + n, :CH] += part[:, CH * n : CH * n + CH]
@@ -1291,24 +1291,21 @@
             small_copy(k).start()
         combine(0)
 
-        @pl.loop(0, D // 256)
-        def _(n):
-            cols = pl.ds(pl.multiple_of(256 * n, 256), 256)
-            bcd_v[:, cols] = dot(rest_v[NX:, :], nrm_v[:, cols]).astype(BF)
-
-        bcd_pair().start()
         relay(1)
         z_close(0)
 
-        @pl.loop(0, D // 256)
+        @pl.loop(0, D // 512)
         def _(n):
-            cols = pl.ds(pl.multiple_of(256 * n, 256), 256)
-            wig_v[:, cols] = dot(rest_v[:NX, :], nrm_v[:, cols]).astype(BF)
-
+            cols = pl.ds(pl.multiple_of(512 * n, 512), 512)
+            both = dot(rest_v[...], nrm_v[:, cols]).astype(BF)
+            wig_v[:, cols] = both[:NX]
+            bcd_v[:, cols] = both[NX:]
+
+        bcd_pair().start()
         z_start(1)
         z_start_mate(1)
         bcd_pair().wait_recv()
-        bcd_v[half(core), :] = (bcd_v[half(core), :].astype(F32) + bcd_in[...].astype(F32)).astype(BF)
+        bcd_v[half(core), :] = bcd_v[half(core), :] + bcd_in[...]
         z_start(2)
         z_start_mate(2)
         gw_v[0:HEADDIM, :] = z_total(3).astype(BF)

time: 237 us -> 235 us (level)
  no operation moved by 1% of the time
where the time goes in v6:
time: 235 us
  Pallas kernels  234 us (100%)
    pallas_call x1, Pallas kernels, backward_call(): pl.pallas_call(backward_kernel, grid=(2 * TEAM + 2,), in_specs=[any_space...  123 us
    pallas_call x1, Pallas kernels, forward_call(): pl.pallas_call(forward_kernel, grid=(2 * TEAM,), in_specs=[any_space] * 4...  99.3 us
    pallas_call x1, Pallas kernels, finish_call(): pl.pallas_call(finish_kernel, in_specs=[any_space] * 4 + [vmem], out_spec...  11.2 us

profile of v6, /device:TPU:0, one launch (start us, length us, event | category | flops | bytes accessed | tf_op | source)
XLA Modules:
  0.0 234.6 jit_solution(16606899186462867066)
XLA Ops:
  0.6 99.3 %shard_map.203 = (bf16[2048,1536]{1,0:T(8,128)(2,1)}, bf16[2048,704]{1,0:T(8,128)(2,1)}, bf16[2048,384]{1,0:T(8,128)(2,1)}, f32[8,128,384]{2,1,0:T(8,128)}, f32[...) custom-call(bf16[256,1536]{1,0:T(8,128)(2,1)} %bitcast.7, ...), custom_call_target="tpu_custom_call" | custom-call | tf_op jit(solution)/shard_map/pallas_call | solution.py:919
  100.0 123.3 %shard_map.204 = (bf16[256,1536]{1,0:T(8,128)(2,1)}, f32[256,1536]{1,0:T(8,128)}, bf16[6448,384]{1,0:T(8,128)(2,1)}, bf16[768,1536]{1,0:T(8,128)(2,1)}, f32[8,16,640]{2,1,0:T(8,128)}) custom-call(bf16[256,1536]{1,0:T(8,128)(2,1)} %bitcast.8, bf16[256,1536]{1,0:T(8,128)(2,1)} %bitcast.10, bf16[2048,1536]{1,0:T(8,128)(2,1)} %get-tuple-element.39.nrm_ref, ...), custom_call_target="tpu_custom_call" | custom-call | tf_op jit(solution)/shard_map/pallas_call | solution.py:1410
  223.3 11.2 %shard_map.205 = (bf16[256,1536]{1,0:T(8,128)(2,1)}, f32[256,1536]{1,0:T(8,128)}, f32[6448,384]{1,0:T(8,128)}, f32[768,1536]{1,0:T(8,128)}, f32[4,832]{1,0:T(4,1...) custom-call(bf16[256,1536]{1,0:T(8,128)(2,1)} %get-tuple-element.51.l, ...), custom_call_target="tpu_custom_call" | custom-call | tf_op jit(solution)/shard_map/pallas_call | solution.py:1497

commit v7 on v6

--- a/solution.py
+++ b/solution.py
@@ -479,7 +479,7 @@
     gm = jnp.where(mask, dot_nt(cm, bm), 0.0)
     ex = spread()
     gh = gather_heads()
-    step_x = split_dot(step, ex)
+    step_x = dot(step.astype(BF), ex)
     xs = (x * step_x).astype(BF)
     dyb = dy.astype(BF)
     dyt = dy.T.astype(BF)
@@ -507,21 +507,21 @@
     old_b = old.astype(BF)
     dnew = dstate[...]
     dnew_b = dnew.astype(BF)
-    carry_x = split_dot(keep * jnp.exp(cum), ex)
+    carry_x = dot((keep * jnp.exp(cum)).astype(BF), ex)
     dyk_f = dy * carry_x
     dyk = dyk_f.astype(BF)
     carried = dot(cm, old_b)
     last = cum[BLK - 1 : BLK, :]
     fade = jnp.exp(last - cum) * tok[:, 8:9]
     weights = fade * step
-    weights_x = split_dot(weights, ex)
+    weights_x = dot(weights.astype(BF), ex)
     zt = dot(bm, dnew_b)
     xw = (x * weights_x).astype(BF)
     through = keep[BLK - 1 :, :] * jnp.exp(last)
     through_x = split_dot(jnp.broadcast_to(through, (8, 128)), ex)[0:1, :]
-    k_term = split_dot(dyk_f * carried, gh)
-    r_term = split_dot(x * zt, gh)
-    q_term = split_dot(x * e, gh)
+    k_term = dot((dyk_f * carried).astype(BF), gh)
+    r_term = dot((x * zt).astype(BF), gh)
+    q_term = dot((x * e).astype(BF), gh)
     pass_term = jnp.sum(old * dnew, axis=0, keepdims=True) * through_x
     pass_h = split_dot(jnp.broadcast_to(pass_term, (8, CH)), gh)[0:1, :]
     wr = weights * r_term

time: 235 us -> 234 us (level)
  no operation moved by 1% of the time
where the time goes in v7:
time: 234 us
  Pallas kernels  233 us (100%)
    pallas_call x1, Pallas kernels, backward_call(): pl.pallas_call(backward_kernel, grid=(2 * TEAM + 2,), in_specs=[any_space...  122 us
    pallas_call x1, Pallas kernels, forward_call(): pl.pallas_call(forward_kernel, grid=(2 * TEAM,), in_specs=[any_space] * 4...  99.3 us
    pallas_call x1, Pallas kernels, finish_call(): pl.pallas_call(finish_kernel, in_specs=[any_space] * 4 + [vmem], out_spec...  11.2 us

profile of v7, /device:TPU:0, one launch (start us, length us, event | category | flops | bytes accessed | tf_op | source)
XLA Modules:
  0.0 233.8 jit_solution(4967098636043454187)
XLA Ops:
  0.6 99.3 %shard_map.203 = (bf16[2048,1536]{1,0:T(8,128)(2,1)}, bf16[2048,704]{1,0:T(8,128)(2,1)}, bf16[2048,384]{1,0:T(8,128)(2,1)}, f32[8,128,384]{2,1,0:T(8,128)}, f32[...) custom-call(bf16[256,1536]{1,0:T(8,128)(2,1)} %bitcast.7, ...), custom_call_target="tpu_custom_call" | custom-call | tf_op jit(solution)/shard_map/pallas_call | solution.py:919
  100.0 122.5 %shard_map.204 = (bf16[256,1536]{1,0:T(8,128)(2,1)}, f32[256,1536]{1,0:T(8,128)}, bf16[6448,384]{1,0:T(8,128)(2,1)}, bf16[768,1536]{1,0:T(8,128)(2,1)}, f32[8,16,640]{2,1,0:T(8,128)}) custom-call(bf16[256,1536]{1,0:T(8,128)(2,1)} %bitcast.8, bf16[256,1536]{1,0:T(8,128)(2,1)} %bitcast.10, bf16[2048,1536]{1,0:T(8,128)(2,1)} %get-tuple-element.39.nrm_ref, ...), custom_call_target="tpu_custom_call" | custom-call | tf_op jit(solution)/shard_map/pallas_call | solution.py:1410
  222.4 11.2 %shard_map.205 = (bf16[256,1536]{1,0:T(8,128)(2,1)}, f32[256,1536]{1,0:T(8,128)}, f32[6448,384]{1,0:T(8,128)}, f32[768,1536]{1,0:T(8,128)}, f32[4,832]{1,0:T(4,1...) custom-call(bf16[256,1536]{1,0:T(8,128)(2,1)} %get-tuple-element.51.l, ...), custom_call_target="tpu_custom_call" | custom-call | tf_op jit(solution)/shard_map/pallas_call | solution.py:1497
